TPU v7x, 128 devices: a whole 4x4x4 slice. The times are simulated.
128 devices in a mesh: tile: 64 (over z, y, x), slide: 2 (over core).
Axes of the slice: x: 4, y: 4, z: 4, core: 2. Of those that a mesh axis runs over, the one named last changes fastest.
Arguments:
- features: bfloat16 [256, 32, 32, 256], P(('slide', 'tile')), parts along dimension 0, may hold values from -8 to 8
- neighbours: int32 [256, 8], P(('slide', 'tile')), parts along dimension 0, may hold values from 0 to 128, as said below
- conv_weight: bfloat16 [3, 3, 256, 256], replicated, may hold values from -0.125 to 0.125
- patch_weight: bfloat16 [4096, 768], replicated, may hold values from -1 to 1
- query_weight: bfloat16 [768, 768], replicated, may hold values from -2 to 2
- key_weight: bfloat16 [768, 768], replicated, may hold values from -2 to 2
- value_weight: bfloat16 [768, 768], replicated, may hold values from -0.21875 to 0.21875
- output_weight: bfloat16 [768, 768], replicated, may hold values from -0.21875 to 0.21875
- cotangent: bfloat16 [16384, 768], P(('slide', 'tile')), parts along dimension 0, may hold values from -6 to 6
Outputs:
- mixed: bfloat16 [16384, 768], P(('slide', 'tile')), parts along dimension 0
- output_grad: float32 [1536, 768], P('slide'), parts along dimension 0
There are 2 independent parts, one for each index of `slide`. A program takes and returns all parts, laid end to end along the dimension named above; an argument that names none is the same for every part. Nothing has to cross between parts.
Inputs may be any that keep to these rules, and one draw needn't show every extreme that they name: Tiles are tissue cells of a grid 16 cells wide; the tile numbers are given to the tissue cells in a drawn order, so neighbours may have any numbers; each entry is the index of the tissue tile at that grid offset, or 128.
All inputs are finite; a program needn't handle non-finite values.
Results may differ from a plain program's by a relative error of at most 0.02.
Values may be sent and summed in bfloat16 or wider, within the bound.
No kernel may reach another device: no remote copies, remote signals or barrier semaphores. Data moves between devices by JAX's collectives and lax.ppermute only.
A program may use at most 192 MiB of HBM per device.

v0:
```python
import jax
import jax.numpy as jnp
from jax import lax
from jax.sharding import PartitionSpec as P

PATCH = 4
HEADS = 12
HD = 64


def tile_faces(maps):
    return jnp.stack([maps[:, 0], maps[:, -1], maps[:, :, 0], maps[:, :, -1]], axis=1)


def pad_tiles(maps, all_faces, links):
    upper = all_faces[links[:, 1], 1]
    lower = all_faces[links[:, 6], 0]
    left_col = all_faces[links[:, 3], 3]
    right_col = all_faces[links[:, 4], 2]
    corner_ul = all_faces[links[:, 0], 1, -1]
    corner_ur = all_faces[links[:, 2], 1, 0]
    corner_dl = all_faces[links[:, 5], 0, -1]
    corner_dr = all_faces[links[:, 7], 0, 0]
    top_row = jnp.concatenate([corner_ul[:, None], upper, corner_ur[:, None]], axis=1)
    bottom_row = jnp.concatenate([corner_dl[:, None], lower, corner_dr[:, None]], axis=1)
    middle = jnp.concatenate([left_col[:, :, None], maps, right_col[:, :, None]], axis=2)
    return jnp.concatenate([top_row[:, None], middle, bottom_row[:, None]], axis=1)


def conv_tiles(padded, kernel):
    count = padded.shape[0]
    side = padded.shape[1] - 2
    chans = padded.shape[3]
    total = jnp.zeros((count * side * side, kernel.shape[3]), jnp.float32)
    for row_off in range(3):
        for col_off in range(3):
            window = padded[:, row_off : row_off + side, col_off : col_off + side, :].reshape(
                -1, chans
            )
            total = total + jnp.dot(
                window, kernel[row_off, col_off], preferred_element_type=jnp.float32
            )
    return jax.nn.gelu(total).astype(jnp.bfloat16).reshape(count, side, side, -1)


def patchify(hidden, patch):
    count, side, _, chans = hidden.shape
    blocks = side // patch
    grid = hidden.reshape(count, blocks, patch, blocks, patch, chans).transpose(0, 1, 3, 2, 4, 5)
    return grid.reshape(count * blocks * blocks, patch * patch * chans)


def local(
    features,
    neighbours,
    conv_weight,
    patch_weight,
    query_weight,
    key_weight,
    value_weight,
    output_weight,
    cotangent,
):
    local_faces = tile_faces(features)
    gathered = lax.all_gather(local_faces, "tile", axis=0, tiled=True)
    all_faces = jnp.concatenate(
        [gathered, jnp.zeros((1,) + gathered.shape[1:], jnp.bfloat16)], axis=0
    )
    padded = pad_tiles(features, all_faces, neighbours)
    hidden = conv_tiles(padded, conv_weight)
    tokens = jnp.dot(
        patchify(hidden, PATCH), patch_weight, preferred_element_type=jnp.float32
    ).astype(jnp.bfloat16)
    rows = tokens.shape[0]
    query = (
        jnp.dot(tokens, query_weight, preferred_element_type=jnp.float32)
        .astype(jnp.bfloat16)
        .reshape(rows, HEADS, HD)
    )
    scale = HD ** (-0.5)
    keys = jnp.dot(tokens, key_weight, preferred_element_type=jnp.float32).astype(jnp.bfloat16)
    values = jnp.dot(tokens, value_weight, preferred_element_type=jnp.float32).astype(jnp.bfloat16)
    top = jnp.full((HEADS, rows), -1e30, jnp.float32)
    key_heads = lax.all_gather(keys, "tile", axis=0, tiled=True).reshape(-1, HEADS, HD)
    value_heads = lax.all_gather(values, "tile", axis=0, tiled=True).reshape(-1, HEADS, HD)
    scores = (
        jnp.einsum("qhd,khd->hqk", query, key_heads, preferred_element_type=jnp.float32) * scale
    )
    new_top = jnp.maximum(top, jnp.max(scores, axis=-1))
    weights = jnp.exp(scores - new_top[..., None])
    total = jnp.sum(weights, axis=-1)
    accum = jnp.einsum(
        "hqk,khd->hqd",
        weights.astype(jnp.bfloat16),
        value_heads,
        preferred_element_type=jnp.float32,
    )
    top, total, accum = (new_top, total, accum)
    attended = (
        (accum / total[..., None]).transpose(1, 0, 2).reshape(rows, HEADS * HD).astype(jnp.bfloat16)
    )
    mixed = (
        tokens.astype(jnp.float32)
        + jnp.dot(attended, output_weight, preferred_element_type=jnp.float32)
    ).astype(jnp.bfloat16)
    grad_term = jnp.dot(attended.T, cotangent, preferred_element_type=jnp.float32)
    output_grad = lax.psum(grad_term, "tile")
    return (mixed, output_grad)


def solution(mesh):
    in_specs = (
        P(("slide", "tile"), None, None, None),
        P(("slide", "tile"), None),
        P(),
        P(),
        P(),
        P(),
        P(),
        P(),
        P(("slide", "tile"), None),
    )
    out_specs = (P(("slide", "tile"), None), P("slide", None))
    return jax.shard_map(local, mesh=mesh, in_specs=in_specs, out_specs=out_specs, check_vma=False)
```

profile of v0, /device:TPU:0, one launch (start us, length us, event | category | flops | bytes accessed | tf_op | source)
XLA Modules:
  0.0 506.7 jit_solution(2070060483644725372)
XLA Ops:
  7.2 1.2 fusion.78
  8.5 0.8 fusion.77
  10.0 1.3 fusion.68
  11.3 81.0 %all-gather.4.cloned.1.call-done = bf16[128,4,32,256]{3,2,1,0:T(8,128)(2,1)} async-done(((bf16[2,4,32,256]{3,2,1,0:T(8,128)(2,1)}), bf16[128,4,32,256]{3,2,1,0:T(8,128)(2,1)}) %all-gather.4.cloned.1.call-update) | async-done | bytes 8388624 | tf_op jit(solution)/shard_map/all_gather | solution.py:65
  92.3 8.5 %concatenate.53 = bf16[129,4,32,256]{3,2,1,0:T(8,128)(2,1)} pad(bf16[128,4,32,256]{3,2,1,0:T(8,128)(2,1)} %all-gather.4.cloned.1.call-done, bf16[]{:T(256)} %constant.15.clone.1), padding=0_1x0_0x0_0x0_0 | pad | bytes 16842754 | tf_op jit(solution)/shard_map/concatenate | solution.py:66
  100.8 3.9 gather_fusion.1
  104.8 1.5 gather_fusion
  106.3 1.5 gather_fusion.2
  107.8 3.9 gather_fusion.6
  111.7 1.5 gather_fusion.5
  113.2 1.5 gather_fusion.7
  114.7 3.9 gather_fusion.3
  118.7 4.0 gather_fusion.4
  122.7 1.2 pad_maximum_fusion.1
  124.0 1.7 pad_maximum_fusion
  125.7 0.8 fusion.76
  131.3 0.9 fusion.13
  132.9 0.8 reshape.58
  133.7 3.8 convolution_convert_fusion.3
  137.5 1.0 convolution_convert_fusion.1
  138.6 2.3 convolution_convert_fusion
  141.7 87.6 %all-gather.6.cloned.1.call-done = bf16[8192,768]{1,0:T(8,128)(2,1)} async-done(((bf16[128,768]{1,0:T(8,128)(2,1)}), bf16[8192,768]{1,0:T(8,128)(2,1)}) %all-gather.6.cloned.1.call-update) | async-done | bytes 12582928 | tf_op jit(solution)/shard_map/all_gather | solution.py:84
  229.2 15.8 %copy.53 = bf16[8192,768]{0,1:T(8,128)(2,1)} copy(bf16[8192,768]{1,0:T(8,128)(2,1)} %all-gather.6.cloned.1.call-done) | data formatting | bytes 25165824 | tf_op jit(solution)/shard_map/all_gather | solution.py:84
  245.0 22.0 %multiply_reduce_fusion = (f32[12,128]{1,0:T(8,128)S(1)}, f32[12,128,8192]{2,1,0:T(8,128)}) fusion(bf16[128,12,64]{0,2,1:T(8,128)(2,1)S(1)} %bitcast.106, bf16[8192,12,64]{0,2,1:T(8,128)(2,1)} %bitcast.92), kind=kOutput, calls=%fused_computation.9 | convolution fusion | flops 1635777024 | bytes 63117312 | tf_op jit(solution)/shard_map/qhd,khd->hqk/dot_general | solution.py:87
  267.0 21.7 %fusion = f32[12,128]{1,0:T(8,128)S(1)} fusion(f32[12,128,8192]{2,1,0:T(8,128)} %get-tuple-element.25, f32[12,128]{1,0:T(8,128)S(1)} %broadcast_maximum_fusion), kind=kLoop, calls=%fused_computation.10 | loop fusion | flops 37747200 | bytes 50343936 | tf_op jit(solution)/shard_map/reduce_sum | solution.py:91
  288.8 34.3 %all-gather.8.cloned.1.call-done = bf16[8192,768]{1,0:T(8,128)(2,1)} async-done(((bf16[128,768]{1,0:T(8,128)(2,1)}), bf16[8192,768]{1,0:T(8,128)(2,1)}) %all-gather.8.cloned.1.call-update) | async-done | bytes 12582928 | tf_op jit(solution)/shard_map/all_gather | solution.py:85
  323.1 15.8 %copy.54 = bf16[8192,768]{0,1:T(8,128)(2,1)} copy(bf16[8192,768]{1,0:T(8,128)(2,1)} %all-gather.8.cloned.1.call-done) | data formatting | bytes 25165824 | tf_op jit(solution)/shard_map/all_gather | solution.py:85
  338.9 22.2 %fusion.21 = bf16[128,12,64]{0,2,1:T(8,128)(2,1)S(1)} fusion(bf16[8192,12,64]{0,2,1:T(8,128)(2,1)} %bitcast.93, f32[12,128,8192]{2,1,0:T(8,128)} %get-tuple-element.25, f32[12,128]{1,0:T(8,128)S(1)} %broadcast_maximum_fusion, f32[128,12]{0,1:T(8,128)S(1)} %bitcast.109), kind=kOutput, calls=%fused_computation.42 | convolution fusion | flops 1648558080 | bytes 63123456 | tf_op jit(solution)/shard_map/hqk,khd->hqd/dot_general | solution.py:92
  361.1 1.9 fusion.79
  363.0 1.0 fusion.17
  364.1 132.8 %all-reduce.8.cloned.1.call-done = f32[768,768]{1,0:T(8,128)} async-done(((f32[768,768]{1,0:T(8,128)}), f32[768,768]{1,0:T(8,128)}) %all-reduce.8.cloned.1.call-update) | async-done | bytes 2359312 | tf_op jit(solution)/shard_map/psum | solution.py:107
  496.9 3.2 copy.62
  (46 shorter events, 7.3 us)
Async XLA Ops:
  7.2 130.3 %copy-start = (bf16[768,768]{1,0:T(8,128)(2,1)S(1)}, bf16[768,768]{1,0:T(8,128)(2,1)}, u32[]{:S(2)}) copy-start(bf16[768,768]{1,0:T(8,128)(2,1)} %param.14) | copy-start | bytes 3538948
  7.2 85.1 %all-gather.4.cloned.1.call-start = ((), (), s32[]{:S(2)}) async-start(), calls=%async_computation | async-start | bytes 8519680 | tf_op jit(solution)/shard_map/all_gather | solution.py:65
  10.0 219.3 %all-gather.6.cloned.1.call-start = ((), (), s32[]{:S(2)}) async-start(), calls=%async_computation.1 | async-start | bytes 12779520 | tf_op jit(solution)/shard_map/all_gather | solution.py:84
  11.3 111.4 %copy-start.2 = (bf16[2,32,32,256]{3,2,1,0:T(8,128)(2,1)S(1)}, bf16[2,32,32,256]{3,2,1,0:T(8,128)(2,1)}, u32[]{:S(2)}) copy-start(bf16[2,32,32,256]{3,2,1,0:T(8,128)(2,1)} %param.9) | copy-start | bytes 3145732
  126.5 1.3 copy-start.5
  137.5 3.6 copy-start.3
  138.6 184.5 %all-gather.8.cloned.1.call-start = ((), (), s32[]{:S(2)}) async-start(), calls=%async_computation.2 | async-start | bytes 12779520 | tf_op jit(solution)/shard_map/all_gather | solution.py:85
  140.9 356.0 %all-reduce.8.cloned.1.call-start = ((), (), s32[]{:S(2)}) async-start(), calls=%async_computation.3 | async-start | bytes 4718592 | tf_op jit(solution)/shard_map/psum | solution.py:107
  338.9 22.2 %copy-start.6 = (bf16[128,768]{1,0:T(8,128)(2,1)S(1)}, bf16[128,768]{1,0:T(8,128)(2,1)}, u32[]{:S(2)}) copy-start(bf16[128,768]{1,0:T(8,128)(2,1)} %param.17) | copy-start | bytes 589828
  361.1 1.9 copy-start.4
  363.0 137.1 %copy-start.1 = (bf16[768,768]{1,0:T(8,128)(2,1)S(1)}, bf16[768,768]{1,0:T(8,128)(2,1)}, u32[]{:S(2)}) copy-start(bf16[768,768]{1,0:T(8,128)(2,1)} %param.14) | copy-start | bytes 3538948
Sparse Core Ops, SparseCore 0:
  11.4 80.8 all-gather.3
  138.7 90.4 all-gather.5
  232.5 90.5 all-gather.7
  363.1 133.7 all-reduce.7
where the time goes:
time: 508 us; the launch traced here: 507 us
  waiting for transfers between devices  336 us (66%)
  local copies, waits for them, and re-layouts  70.9 us (14%)
  matrix products  58.9 us (12%)
  other arithmetic  26.6 us (5%)
  between operations  14 us (3%)
    psum x1, waiting for transfers between devices, local(): output_grad = lax.psum(grad_term, 'tile')  133 us
    all_gather x1, waiting for transfers between devices, local(): lax.all_gather(keys, 'tile', axis=0, tiled=True).reshape(-1, HEADS, HD)  87.6 us
    all_gather x1, waiting for transfers between devices, local(): gathered = lax.all_gather(local_faces, 'tile', axis=0, tiled=True)  81 us
    all_gather x1, waiting for transfers between devices, local(): lax.all_gather(values, 'tile', axis=0, tiled=True).reshape(-1, HEADS, HD)  34.3 us
    dot_general x1, matrix products, local(): jnp.einsum('hqk,khd->hqd', weights.astype(jnp.bfloat16), value_heads, pre...  22.2 us
    dot_general x1, matrix products, local(): jnp.einsum('qhd,khd->hqk', query, key_heads, preferred_element_type=jnp.f...  22 us
    reduce_sum x1, other arithmetic, local(): total = jnp.sum(weights, axis=-1)  21.7 us
    all_gather x1, local copies, waits for them, and re-layouts, local(): lax.all_gather(keys, 'tile', axis=0, tiled=True).reshape(-1, HEADS, HD)  15.8 us
  transfers between devices with their start and end apart: 4, of which 4 were waited for; matrix products, arithmetic and copies ran while one was open for 13% of the time, Pallas kernels for 0%

commit v1 on v0

v1 whole, which is shorter than its diff:
```python
import jax
import jax.numpy as jnp
from jax import lax
from jax.experimental import pallas as pl
from jax.experimental.pallas import tpu as pltpu
from jax.sharding import PartitionSpec as P

PATCH = 4
HEADS = 12
HD = 64
DM = 768
SPLIT = 4
HG = HEADS // SPLIT
GW = HG * HD
BLK = 32
QKVW = 640
OW = 256
HALO = 144
BF = jnp.bfloat16
F32 = jnp.float32


def hi_bit(coord):
    return coord >> 1


def lo_bit(coord):
    return (coord ^ (coord >> 1)) & 1


def split_device(dev):
    z, y, x = dev >> 4, (dev >> 2) & 3, dev & 3
    outer = hi_bit(z) * 4 + hi_bit(y) * 2 + hi_bit(x)
    inner = lo_bit(z) * 4 + lo_bit(y) * 2 + lo_bit(x)
    return outer, inner


def device_groups():
    place = {}
    for dev in range(64):
        place[split_device(dev)] = dev
    inner_groups = [[place[(a, b)] for b in range(8)] for a in range(8)]
    outer_groups = [[place[(a, b)] for a in range(8)] for b in range(8)]
    return inner_groups, outer_groups


INNER, OUTER = device_groups()


def swap(x, groups=None):
    return lax.all_to_all(
        x, "tile", split_axis=0, concat_axis=0, tiled=True, axis_index_groups=groups
    )


EDGES = ((1, 0, 32), (6, 32, 0), (3, 64, 96), (4, 96, 64))
CORNERS = ((0, 0, 3), (2, 31, 2), (5, 32, 1), (7, 63, 0))


def route_kernel(links_ref, mine_ref, faces_ref, out_ref):
    out_ref[...] = jnp.zeros(out_ref.shape, BF)
    mine = mine_ref[0]
    row_ids = lax.broadcasted_iota(jnp.int32, (16, 256), 0)

    def per_tile(src, carry):
        def target(direction):
            tile = links_ref[src * 8 + direction]
            outer, inner = split_device(tile >> 1)
            return (tile < 128) & (inner == mine), outer & 7, tile & 1

        for direction, first, dest in EDGES:
            hit, outer, slot = target(direction)

            @pl.when(hit)
            def _():
                out_ref[outer * 2 + slot, dest : dest + 32, :] = faces_ref[src, first : first + 32, :]

        for direction, row, dest in CORNERS:
            hit, outer, slot = target(direction)

            @pl.when(hit)
            def _():
                base = row // 16 * 16
                cell = faces_ref[src, base : base + 16, :].astype(F32)[row - base : row - base + 1, :]
                old = out_ref[outer * 2 + slot, 128:144, :].astype(F32)
                new = jnp.where(row_ids == dest, jnp.broadcast_to(cell, (16, 256)), old)
                out_ref[outer * 2 + slot, 128:144, :] = new.astype(BF)

        return carry

    lax.fori_loop(0, 16, per_tile, 0)


def route(links, mine, faces):
    return pl.pallas_call(
        route_kernel,
        grid=(1,),
        in_specs=[
            pl.BlockSpec(memory_space=pltpu.SMEM),
            pl.BlockSpec(memory_space=pltpu.SMEM),
            pl.BlockSpec((16, HALO, 256), lambda i: (0, 0, 0)),
        ],
        out_specs=pl.BlockSpec((16, HALO, 256), lambda i: (0, 0, 0)),
        out_shape=jax.ShapeDtypeStruct((16, HALO, 256), BF),
        name="route",
    )(links, mine, faces)


def attend_kernel(q_ref, kv_ref, out_ref, key_ref, val_ref):
    @pl.when(pl.program_id(0) == 0)
    def _():
        lanes = lax.broadcasted_iota(jnp.int32, (2048, 64), 1)
        ones = jnp.where(lanes == 0, 1.0, 0.0).astype(BF)
        for g in range(HG):
            key_ref[g] = kv_ref[:, GW + g * HD : GW + (g + 1) * HD]
            val_ref[g, :, :HD] = kv_ref[:, 2 * GW + g * HD : 2 * GW + (g + 1) * HD]
            val_ref[g, :, HD:] = ones

    rows = q_ref.shape[0]
    lanes = lax.broadcasted_iota(jnp.int32, (rows, OW - GW), 1)
    tail = jnp.zeros((rows, OW - GW), F32)
    for g in range(HG):
        query = q_ref[:, g * HD : (g + 1) * HD] * BF(HD ** -0.5)
        scores = lax.dot_general(
            query, key_ref[g], (((1,), (1,)), ((), ())), preferred_element_type=F32
        )
        top = jnp.max(scores, axis=1, keepdims=True)
        weights = jnp.exp(scores - top).astype(BF)
        res = jnp.dot(weights, val_ref[g], preferred_element_type=F32)
        total = res[:, HD : HD + 1]
        out_ref[:, g * HD : (g + 1) * HD] = (res[:, :HD] / total).astype(BF)
        lse = top + jnp.log(total)
        first = lse.astype(BF).astype(F32)
        second = (lse - first).astype(BF).astype(F32)
        third = lse - first - second
        for n, part in enumerate((first, second, third)):
            tail = jnp.where(lanes == 3 * g + n, part, tail)
    out_ref[:, GW:] = tail.astype(BF)


def attend(packed):
    rows = 256
    return pl.pallas_call(
        attend_kernel,
        grid=(2048 // rows,),
        in_specs=[
            pl.BlockSpec((rows, QKVW), lambda i: (i, 0)),
            pl.BlockSpec((2048, QKVW), lambda i: (0, 0)),
        ],
        out_specs=pl.BlockSpec((rows, OW), lambda i: (i, 0)),
        out_shape=jax.ShapeDtypeStruct((2048, OW), BF),
        scratch_shapes=[pltpu.VMEM((HG, 2048, HD), BF), pltpu.VMEM((HG, 2048, 2 * HD), BF)],
        compiler_params=pltpu.CompilerParams(vmem_limit_bytes=48 << 20),
        name="attend",
    )(packed, packed)


def finish_kernel(parts_ref, tokens_ref, weight_ref, cot_ref, mixed_ref, grad_ref, att_ref):
    for h in range(SPLIT):
        for a in range(SPLIT):
            pieces = [parts_ref[(h * SPLIT + a) * SPLIT + b].astype(F32) for b in range(SPLIT)]
            for g in range(HG):
                col = GW + 3 * g
                lses = [
                    p[:, col : col + 1] + p[:, col + 1 : col + 2] + p[:, col + 2 : col + 3] for p in pieces
                ]
                top = jnp.maximum(jnp.maximum(lses[0], lses[1]), jnp.maximum(lses[2], lses[3]))
                ws = [jnp.exp(v - top) for v in lses]
                total = ws[0] + ws[1] + ws[2] + ws[3]
                acc = sum(w * p[:, g * HD : (g + 1) * HD] for w, p in zip(ws, pieces)) / total
                att_ref[a * BLK : (a + 1) * BLK, h * GW + g * HD : h * GW + (g + 1) * HD] = acc.astype(BF)
    att = att_ref[...]
    grad_ref[...] = lax.dot_general(
        att, cot_ref[...], (((0,), (0,)), ((), ())), preferred_element_type=F32
    ).astype(BF)
    mixed_ref[...] = (
        tokens_ref[...].astype(F32) + jnp.dot(att, weight_ref[...], preferred_element_type=F32)
    ).astype(BF)


def finish(parts, tokens, weight, cot):
    return pl.pallas_call(
        finish_kernel,
        out_shape=(
            jax.ShapeDtypeStruct((128, DM), BF),
            jax.ShapeDtypeStruct((DM, DM), BF),
        ),
        scratch_shapes=[pltpu.VMEM((128, DM), BF)],
        name="finish",
    )(parts, tokens, weight, cot)


def pad_tiles(maps, halo):
    top_row = jnp.concatenate([halo[:, 128:129], halo[:, 0:32], halo[:, 129:130]], axis=1)
    bottom_row = jnp.concatenate([halo[:, 130:131], halo[:, 32:64], halo[:, 131:132]], axis=1)
    middle = jnp.concatenate([halo[:, 64:96, None], maps, halo[:, 96:128, None]], axis=2)
    return jnp.concatenate([top_row[:, None], middle, bottom_row[:, None]], axis=1)


def conv_tiles(padded, kernel):
    count = padded.shape[0]
    side = padded.shape[1] - 2
    chans = padded.shape[3]
    total = jnp.zeros((count * side * side, kernel.shape[3]), F32)
    for row_off in range(3):
        for col_off in range(3):
            window = padded[:, row_off : row_off + side, col_off : col_off + side, :].reshape(-1, chans)
            total = total + jnp.dot(window, kernel[row_off, col_off], preferred_element_type=F32)
    return jax.nn.gelu(total).astype(BF).reshape(count, side, side, -1)


def patchify(hidden, patch):
    count, side, _, chans = hidden.shape
    blocks = side // patch
    grid = hidden.reshape(count, blocks, patch, blocks, patch, chans).transpose(0, 1, 3, 2, 4, 5)
    return grid.reshape(count * blocks * blocks, patch * patch * chans)


def local(
    features,
    neighbours,
    conv_weight,
    patch_weight,
    query_weight,
    key_weight,
    value_weight,
    output_weight,
    cotangent,
):
    outer, inner = split_device(lax.axis_index("tile"))
    link_rows = jnp.pad(neighbours.astype(BF)[:, None, :], ((0, 0), (0, 15), (0, 248)))
    faces = jnp.concatenate(
        [features[:, 0], features[:, -1], features[:, :, 0], features[:, :, -1], link_rows], axis=1
    )
    faces = swap(jnp.broadcast_to(faces[None], (8,) + faces.shape), INNER).reshape(16, HALO, 256)
    links = faces[:, 128, :8].astype(jnp.int32).reshape(128)
    halo = swap(route(links, inner.reshape(1), faces), OUTER).reshape(8, 2, HALO, 256)
    halo = jnp.sum(halo.astype(F32), axis=0).astype(BF)
    hidden = conv_tiles(pad_tiles(features, halo), conv_weight)
    tokens = jnp.dot(patchify(hidden, PATCH), patch_weight, preferred_element_type=F32).astype(BF)
    query = jnp.dot(tokens, query_weight, preferred_element_type=F32).astype(BF)
    keys = jnp.dot(tokens, key_weight, preferred_element_type=F32).astype(BF)
    values = jnp.dot(tokens, value_weight, preferred_element_type=F32).astype(BF)

    def by_block(x):
        return x.reshape(SPLIT, BLK, SPLIT, GW).transpose(2, 0, 1, 3)

    full = (SPLIT, SPLIT, SPLIT, BLK, GW)
    packed = jnp.concatenate(
        [
            jnp.broadcast_to(by_block(query)[:, :, None], full),
            jnp.broadcast_to(by_block(keys)[:, None], full),
            jnp.broadcast_to(by_block(values)[:, None], full),
            jnp.zeros((SPLIT, SPLIT, SPLIT, BLK, QKVW - 3 * GW), BF),
        ],
        axis=-1,
    ).reshape(64, BLK, QKVW)
    packed = swap(packed).reshape(64 * BLK, QKVW)
    parts = swap(attend(packed).reshape(64, BLK, OW))
    mixed, grad = finish(parts, tokens, output_weight, cotangent)

    def total(x):
        return jnp.sum(x.reshape(8, DM // 8, DM).astype(F32), axis=0).astype(BF)

    grad = total(swap(grad.reshape(8, DM // 8, DM), INNER))
    grad = total(swap(jnp.broadcast_to(grad[None], (8,) + grad.shape), OUTER))
    grad = swap(jnp.broadcast_to(grad[None], (8,) + grad.shape), INNER)
    return mixed, grad.reshape(DM, DM).astype(F32)


def solution(mesh):
    in_specs = (
        P(("slide", "tile"), None, None, None),
        P(("slide", "tile"), None),
        P(),
        P(),
        P(),
        P(),
        P(),
        P(),
        P(("slide", "tile"), None),
    )
    out_specs = (P(("slide", "tile"), None), P("slide", None))
    return jax.shard_map(local, mesh=mesh, in_specs=in_specs, out_specs=out_specs, check_vma=False)
```

time: 508 us -> 227 us (0.45)
  waiting for transfers between devices: 336 us -> 35.7 us
  blocking collectives: 0 us -> 114 us
  local copies, waits for them, and re-layouts: 70.9 us -> 11.7 us
  matrix products: 58.9 us -> 10.4 us
  Pallas kernels: 0 us -> 32.8 us
  other arithmetic: 26.6 us -> 6.97 us
  starting transfers between devices: 0.35 us -> 14 us
  between operations: 14 us -> 0.99 us
    all_gather x3 -> x0, waiting for transfers between devices: 203 us -> none  [the longest x1 87.6 us: local(): lax.all_gather(keys, 'tile', axis=0, tiled=True).reshape(-1, HEADS, HD)]
    psum x1 -> x0, waiting for transfers between devices: 133 us -> none  [local(): output_grad = lax.psum(grad_term, 'tile')]
    all_to_all x0 -> x5, blocking collectives: none -> 114 us  [swap(): lax.all_to_all(x, 'tile', split_axis=0, concat_axis=0, tiled=True, axis_i...]
    dot_general x17 -> x13, matrix products: 58.9 us -> 10.4 us  [the longest x9 4.38 us: conv_tiles(): jnp.dot(window, kernel[row_off, col_off], preferred_element_type=F32)]
    all_to_all x0 -> x2, waiting for transfers between devices: none -> 35.7 us  [swap(): lax.all_to_all(x, 'tile', split_axis=0, concat_axis=0, tiled=True, axis_i...]
    pallas_call x0 -> x3, Pallas kernels: none -> 32.8 us  [the longest x1 21.5 us: attend(): pl.pallas_call(attend_kernel, grid=(2048 // rows,), in_specs=[pl.BlockSpe...]
    all_gather x2 -> x0, local copies, waits for them, and re-layouts: 31.6 us -> none  [the longest x1 15.8 us: local(): lax.all_gather(keys, 'tile', axis=0, tiled=True).reshape(-1, HEADS, HD)]
    gather x8 -> x0, local copies, waits for them, and re-layouts: 21.7 us -> none  [the longest x1 3.95 us: pad_tiles(): right_col = all_faces[links[:, 4], 2]]
  transfers between devices with their start and end apart: 4 -> 2, of which waited for: 4 -> 2; matrix products, arithmetic and copies ran while one was open for 13% -> 0% of each run, Pallas kernels for 0% -> 0%
where the time goes in v1:
time: 227 us
  blocking collectives  114 us (50%)
  waiting for transfers between devices  35.7 us (16%)
  Pallas kernels  32.8 us (14%)
  starting transfers between devices  14 us (6%)
  local copies, waits for them, and re-layouts  11.7 us (5%)
  matrix products  10.4 us (5%)
  other arithmetic  6.97 us (3%)
    all_to_all x5, blocking collectives, swap(): lax.all_to_all(x, 'tile', split_axis=0, concat_axis=0, tiled=True, axis_i...  114 us
    all_to_all x2, waiting for transfers between devices, swap(): lax.all_to_all(x, 'tile', split_axis=0, concat_axis=0, tiled=True, axis_i...  35.7 us
    pallas_call x1, Pallas kernels, attend(): pl.pallas_call(attend_kernel, grid=(2048 // rows,), in_specs=[pl.BlockSpe...  21.5 us
    all_to_all x2, starting transfers between devices, swap(): lax.all_to_all(x, 'tile', split_axis=0, concat_axis=0, tiled=True, axis_i...  14 us
    pallas_call x1, Pallas kernels, finish(): pl.pallas_call(finish_kernel, out_shape=(jax.ShapeDtypeStruct((128, DM),...  6.74 us
  transfers between devices with their start and end apart: 2, of which 2 were waited for; matrix products, arithmetic and copies ran while one was open for 0% of the time, Pallas kernels for 0%

profile of v1, /device:TPU:0, one launch (start us, length us, event | category | flops | bytes accessed | tf_op | source)
XLA Modules:
  0.0 226.6 jit_solution(2616710696020780744)
XLA Ops:
  0.6 1.2 fusion.32
  1.9 0.8 bitcast_dynamic-update-slice_fusion.1
  2.7 0.8 bitcast_dynamic-update-slice_fusion
  3.4 0.7 convert_bitcast_fusion
  4.1 1.1 broadcast_in_dim.25
  5.2 5.2 %all-to-all-start = ((bf16[8,2,144,256]{3,2,1,0:T(8,128)(2,1)}), bf16[8,2,144,256]{3,2,1,0:T(8,128)(2,1)S(1)}, u32[]{:S(2)}, u32[]{:S(2)}) async-start(bf16[8,2,144,256]{3,2,1,0:T(8,128)(2,1)} %broadcast_in_dim.25), calls=%async_computation | async-start | bytes 2359296 | tf_op jit(solution)/shard_map/all_to_all | solution.py:51
  10.5 16.8 %all-to-all-done = bf16[8,2,144,256]{3,2,1,0:T(8,128)(2,1)S(1)} async-done(((bf16[8,2,144,256]{3,2,1,0:T(8,128)(2,1)}), bf16[8,2,144,256]{3,2,1,0:T(8,128)(2,1)S(1)}, u32[]{:S(2)}, u32[]{:S(2)}) %all-to-all-start) | async-done | bytes 1179680 | tf_op jit(solution)/shard_map/all_to_all | solution.py:51
  27.3 0.7 reshape.97.links_ref
  28.3 4.5 %route.1 = bf16[16,144,256]{2,1,0:T(8,128)(2,1)} custom-call(s32[128]{0:T(128)} %reshape.97.links_ref, s32[1]{0:T(128)} %bitcast.6.mine_ref, bf16[16,144,256]{2,1,0:T(8,128)(2,1)} %bitcast.105), custom_call_target="tpu_custom_call" | custom-call | tf_op jit(solution)/shard_map/route/pallas_call | solution.py:95
  32.8 8.7 %all-to-all-start.1 = ((bf16[16,144,256]{2,1,0:T(8,128)(2,1)}), bf16[16,144,256]{2,1,0:T(8,128)(2,1)S(1)}, u32[]{:S(2)}, u32[]{:S(2)}) async-start(bf16[16,144,256]{2,1,0:T(8,128)(2,1)} %route.1), calls=%async_computation.1 | async-start | bytes 2359296 | tf_op jit(solution)/shard_map/all_to_all | solution.py:51
  41.5 0.7 pad.8.clone
  42.2 18.9 %all-to-all-done.1 = bf16[16,144,256]{2,1,0:T(8,128)(2,1)S(1)} async-done(((bf16[16,144,256]{2,1,0:T(8,128)(2,1)}), bf16[16,144,256]{2,1,0:T(8,128)(2,1)S(1)}, u32[]{:S(2)}, u32[]{:S(2)}) %all-to-all-start.1) | async-done | bytes 1179680 | tf_op jit(solution)/shard_map/all_to_all | solution.py:51
  61.4 1.2 pad_maximum_fusion.1
  62.7 1.7 pad_maximum_fusion
  64.4 0.8 fusion.31
  65.2 0.8 fusion.30
  65.9 0.5 copy-done.5
  69.5 0.4 convolution_add_fusion.1
  70.0 0.9 fusion.7
  71.6 1.0 reshape.89
  72.6 3.8 %convolution_convert_fusion.3.tokens_ref = bf16[128,768]{1,0:T(8,128)(2,1)S(1)} fusion(bf16[128,4096]{1,0:T(8,128)(2,1)S(1)} %reshape.89, bf16[4096,768]{1,0:T(8,128)(2,1)} %param.12), kind=kOutput, calls=%fused_computation.24 | convolution fusion | flops 805404672 | bytes 7536640 | tf_op jit(solution)/shard_map/dot_general | solution.py:240
  77.0 0.7 copy-done.4
  78.4 1.6 convolution_convert_fusion
  81.0 1.2 maximum_maximum_fusion
  82.1 38.7 %all_to_all.35 = bf16[64,32,640]{2,1,0:T(8,128)(2,1)S(1)} all-to-all(bf16[64,32,640]{2,1,0:T(8,128)(2,1)S(1)} %bitcast.103), channel_id=1, replica_groups=mesh['tile'=64,'slide'=2] {'tile'}, dimensions={0} | all-to-all | bytes 5242880 | tf_op jit(solution)/shard_map/all_to_all | solution.py:51
  120.8 21.5 %attend.1 = bf16[2048,256]{1,0:T(8,128)(2,1)S(1)} custom-call(bf16[2048,640]{1,0:T(8,128)(2,1)S(1)} %bitcast.99, bf16[2048,640]{1,0:T(8,128)(2,1)S(1)} %bitcast.100), custom_call_target="tpu_custom_call" | custom-call | tf_op jit(solution)/shard_map/attend/pallas_call | solution.py:143
  142.4 22.4 %all_to_all.36.parts_ref = bf16[64,32,256]{2,1,0:T(8,128)(2,1)} all-to-all(bf16[64,32,256]{2,1,0:T(8,128)(2,1)S(1)} %bitcast.101), channel_id=1, replica_groups=mesh['tile'=64,'slide'=2] {'tile'}, dimensions={0} | all-to-all | bytes 2097152 | tf_op jit(solution)/shard_map/all_to_all | solution.py:51
  164.8 6.7 %finish.1 = (bf16[128,768]{1,0:T(8,128)(2,1)}, bf16[768,768]{1,0:T(8,128)(2,1)}) custom-call(bf16[64,32,256]{2,1,0:T(8,128)(2,1)} %all_to_all.36.parts_ref, bf16[128,768]{1,0:T(8,128)(2,1)} %copy-done.2, bf16[768,768]{1,0:T(8,128)(2,1)} %weight_ref.1, bf16[128,768]{1,0:T(8,128)(2,1)} %cot_ref.1), custom_call_target="tpu_custom_call" | custom-call | tf_op jit(solution)/shard_map/finish/pallas_call | solution.py:182
  171.6 17.9 %all_to_all.37 = bf16[8,96,768]{2,1,0:T(8,128)(2,1)S(1)} all-to-all(bf16[8,96,768]{2,1,0:T(8,128)(2,1)} %bitcast.115), channel_id=1, replica_groups={{0,2,8,10,32,34,40,42},{6,4,14,12,38,36,46,44},{24,26,16,18,56,58,48,50..., dimensions={0} | all-to-all | bytes 2359296 | tf_op jit(solution)/shard_map/all_to_all | solution.py:51
  189.7 20.0 %all_to_all.38 = bf16[8,96,768]{2,1,0:T(8,128)(2,1)S(1)} all-to-all(bf16[8,96,768]{2,1,0:T(8,128)(2,1)S(1)} %broadcast_in_dim.64), channel_id=1, replica_groups={{0,6,24,30,96,102,120,126},{2,4,26,28,98,100,122,124},{8,14,16,22,104,1..., dimensions={0} | all-to-all | bytes 2359296 | tf_op jit(solution)/shard_map/all_to_all | solution.py:51
  210.0 15.0 %all_to_all.39 = bf16[8,96,768]{2,1,0:T(8,128)(2,1)S(1)} all-to-all(bf16[8,96,768]{2,1,0:T(8,128)(2,1)S(1)} %broadcast_in_dim.65), channel_id=1, replica_groups={{0,2,8,10,32,34,40,42},{6,4,14,12,38,36,46,44},{24,26,16,18,56,58,48,50..., dimensions={0} | all-to-all | bytes 2359296 | tf_op jit(solution)/shard_map/all_to_all | solution.py:51
  224.9 1.7 bitcast_convert_fusion
  (48 shorter events, 7.1 us)
Async XLA Ops:
  0.6 75.7 %copy-start = (bf16[768,768]{1,0:T(8,128)(2,1)S(1)}, bf16[768,768]{1,0:T(8,128)(2,1)}, u32[]{:S(2)}) copy-start(bf16[768,768]{1,0:T(8,128)(2,1)} %param.13) | copy-start | bytes 3538948
  5.2 22.0 %all-to-all-start = ((bf16[8,2,144,256]{3,2,1,0:T(8,128)(2,1)}), bf16[8,2,144,256]{3,2,1,0:T(8,128)(2,1)S(1)}, u32[]{:S(2)}, u32[]{:S(2)}) async-start(bf16[8,2,144,256]{3,2,1,0:T(8,128)(2,1)} %broadcast_in_dim.25), calls=%async_computation | async-start | bytes 2359296 | tf_op jit(solution)/shard_map/all_to_all | solution.py:51
  27.3 1.0 copy-start.3
  32.8 28.6 %copy-start.1 = (bf16[2,32,32,256]{3,2,1,0:T(8,128)(2,1)S(1)}, bf16[2,32,32,256]{3,2,1,0:T(8,128)(2,1)}, u32[]{:S(2)}) copy-start(bf16[2,32,32,256]{3,2,1,0:T(8,128)(2,1)} %param.9) | copy-start | bytes 3145732
  32.8 28.3 %all-to-all-start.1 = ((bf16[16,144,256]{2,1,0:T(8,128)(2,1)}), bf16[16,144,256]{2,1,0:T(8,128)(2,1)S(1)}, u32[]{:S(2)}, u32[]{:S(2)}) async-start(bf16[16,144,256]{2,1,0:T(8,128)(2,1)} %route.1), calls=%async_computation.1 | async-start | bytes 2359296 | tf_op jit(solution)/shard_map/all_to_all | solution.py:51
  65.2 1.3 copy-start.5
  76.4 2.0 copy-start.2
  76.4 1.3 copy-start.4
  80.3 0.7 copy-start.6

commit v2 on v1

--- a/solution.py
+++ b/solution.py
@@ -15,7 +15,7 @@
 BLK = 32
 QKVW = 640
 OW = 256
-HALO = 144
+HALO = 136
 BF = jnp.bfloat16
 F32 = jnp.float32
 
@@ -60,7 +60,7 @@
 def route_kernel(links_ref, mine_ref, faces_ref, out_ref):
     out_ref[...] = jnp.zeros(out_ref.shape, BF)
     mine = mine_ref[0]
-    row_ids = lax.broadcasted_iota(jnp.int32, (16, 256), 0)
+    row_ids = lax.broadcasted_iota(jnp.int32, (8, 256), 0)
 
     def per_tile(src, carry):
         def target(direction):
@@ -80,11 +80,11 @@
 
             @pl.when(hit)
             def _():
-                base = row // 16 * 16
-                cell = faces_ref[src, base : base + 16, :].astype(F32)[row - base : row - base + 1, :]
-                old = out_ref[outer * 2 + slot, 128:144, :].astype(F32)
-                new = jnp.where(row_ids == dest, jnp.broadcast_to(cell, (16, 256)), old)
-                out_ref[outer * 2 + slot, 128:144, :] = new.astype(BF)
+                base = row // 8 * 8
+                cell = faces_ref[src, base : base + 8, :].astype(F32)[row - base : row - base + 1, :]
+                old = out_ref[outer * 2 + slot, 128:HALO, :].astype(F32)
+                new = jnp.where(row_ids == dest, jnp.broadcast_to(cell, (8, 256)), old)
+                out_ref[outer * 2 + slot, 128:HALO, :] = new.astype(BF)
 
         return carry
 
@@ -170,9 +170,9 @@
                 acc = sum(w * p[:, g * HD : (g + 1) * HD] for w, p in zip(ws, pieces)) / total
                 att_ref[a * BLK : (a + 1) * BLK, h * GW + g * HD : h * GW + (g + 1) * HD] = acc.astype(BF)
     att = att_ref[...]
-    grad_ref[...] = lax.dot_general(
-        att, cot_ref[...], (((0,), (0,)), ((), ())), preferred_element_type=F32
-    ).astype(BF)
+    grad = lax.dot_general(att, cot_ref[...], (((0,), (0,)), ((), ())), preferred_element_type=F32)
+    for c in range(DM // 128):
+        grad_ref[c] = grad[:, c * 128 : (c + 1) * 128].astype(BF)
     mixed_ref[...] = (
         tokens_ref[...].astype(F32) + jnp.dot(att, weight_ref[...], preferred_element_type=F32)
     ).astype(BF)
@@ -183,7 +183,7 @@
         finish_kernel,
         out_shape=(
             jax.ShapeDtypeStruct((128, DM), BF),
-            jax.ShapeDtypeStruct((DM, DM), BF),
+            jax.ShapeDtypeStruct((DM // 128, DM, 128), BF),
         ),
         scratch_shapes=[pltpu.VMEM((128, DM), BF)],
         name="finish",
@@ -228,7 +228,7 @@
     cotangent,
 ):
     outer, inner = split_device(lax.axis_index("tile"))
-    link_rows = jnp.pad(neighbours.astype(BF)[:, None, :], ((0, 0), (0, 15), (0, 248)))
+    link_rows = jnp.pad(neighbours.astype(BF)[:, None, :], ((0, 0), (0, 7), (0, 248)))
     faces = jnp.concatenate(
         [features[:, 0], features[:, -1], features[:, :, 0], features[:, :, -1], link_rows], axis=1
     )
@@ -259,13 +259,11 @@
     parts = swap(attend(packed).reshape(64, BLK, OW))
     mixed, grad = finish(parts, tokens, output_weight, cotangent)
 
-    def total(x):
-        return jnp.sum(x.reshape(8, DM // 8, DM).astype(F32), axis=0).astype(BF)
-
-    grad = total(swap(grad.reshape(8, DM // 8, DM), INNER))
-    grad = total(swap(jnp.broadcast_to(grad[None], (8,) + grad.shape), OUTER))
-    grad = swap(jnp.broadcast_to(grad[None], (8,) + grad.shape), INNER)
-    return mixed, grad.reshape(DM, DM).astype(F32)
+    grad = swap(grad.reshape(64, 72, 128))
+    grad = jnp.sum(grad.astype(F32), axis=0).astype(BF)
+    grad = swap(jnp.broadcast_to(grad[None], (64, 72, 128)))
+    grad = grad.reshape(DM // 128, DM, 128).transpose(1, 0, 2).reshape(DM, DM)
+    return mixed, grad.astype(F32)
 
 
 def solution(mesh):

time: 227 us -> 221 us (0.974)
  blocking collectives: 114 us -> 106 us
  local copies, waits for them, and re-layouts: 11.7 us -> 15.8 us
    all_to_all x5 -> x4, blocking collectives: 114 us -> 106 us  [swap(): lax.all_to_all(x, 'tile', split_axis=0, concat_axis=0, tiled=True, axis_i...]
    unnamed x18 -> x17, local copies, waits for them, and re-layouts: 3.31 us -> 6.05 us
where the time goes in v2:
time: 221 us; the launch traced here: 220 us
  blocking collectives  106 us (48%)
  waiting for transfers between devices  34.9 us (16%)
  Pallas kernels  32.7 us (15%)
  local copies, waits for them, and re-layouts  15.8 us (7%)
  starting transfers between devices  14 us (6%)
  matrix products  10.4 us (5%)
  other arithmetic  5.32 us (2%)
    all_to_all x4, blocking collectives, swap(): lax.all_to_all(x, 'tile', split_axis=0, concat_axis=0, tiled=True, axis_i...  106 us
    all_to_all x2, waiting for transfers between devices, swap(): lax.all_to_all(x, 'tile', split_axis=0, concat_axis=0, tiled=True, axis_i...  34.9 us
    pallas_call x1, Pallas kernels, attend(): pl.pallas_call(attend_kernel, grid=(2048 // rows,), in_specs=[pl.BlockSpe...  21.5 us
    all_to_all x2, starting transfers between devices, swap(): lax.all_to_all(x, 'tile', split_axis=0, concat_axis=0, tiled=True, axis_i...  14 us
    pallas_call x1, Pallas kernels, finish(): pl.pallas_call(finish_kernel, out_shape=(jax.ShapeDtypeStruct((128, DM),...  6.74 us
    unnamed x17, local copies, waits for them, and re-layouts  6.05 us
    pallas_call x1, Pallas kernels, route(): pl.pallas_call(route_kernel, grid=(1,), in_specs=[pl.BlockSpec(memory_spa...  4.44 us
  transfers between devices with their start and end apart: 2, of which 2 were waited for; matrix products, arithmetic and copies ran while one was open for 0% of the time, Pallas kernels for 0%

profile of v2, /device:TPU:0, one launch (start us, length us, event | category | flops | bytes accessed | tf_op | source)
XLA Modules:
  0.0 220.0 jit_solution(10859633500170890204)
XLA Ops:
  0.6 1.2 fusion.32
  1.9 0.8 bitcast_dynamic-update-slice_fusion.1
  2.7 0.8 bitcast_dynamic-update-slice_fusion
  3.4 0.7 convert_bitcast_fusion.1
  4.1 1.1 broadcast_in_dim.23
  5.2 5.2 %all-to-all-start = ((bf16[8,2,136,256]{3,2,1,0:T(8,128)(2,1)}), bf16[8,2,136,256]{3,2,1,0:T(8,128)(2,1)S(1)}, u32[]{:S(2)}, u32[]{:S(2)}) async-start(bf16[8,2,136,256]{3,2,1,0:T(8,128)(2,1)} %broadcast_in_dim.23), calls=%async_computation | async-start | bytes 2228224 | tf_op jit(solution)/shard_map/all_to_all | solution.py:51
  10.4 16.1 %all-to-all-done = bf16[8,2,136,256]{3,2,1,0:T(8,128)(2,1)S(1)} async-done(((bf16[8,2,136,256]{3,2,1,0:T(8,128)(2,1)}), bf16[8,2,136,256]{3,2,1,0:T(8,128)(2,1)S(1)}, u32[]{:S(2)}, u32[]{:S(2)}) %all-to-all-start) | async-done | bytes 1114144 | tf_op jit(solution)/shard_map/all_to_all | solution.py:51
  26.6 0.7 reshape.99.links_ref
  27.5 4.4 %route.1 = bf16[16,136,256]{2,1,0:T(8,128)(2,1)} custom-call(s32[128]{0:T(128)} %reshape.99.links_ref, s32[1]{0:T(128)} %bitcast.6.mine_ref, bf16[16,136,256]{2,1,0:T(8,128)(2,1)} %bitcast.109), custom_call_target="tpu_custom_call" | custom-call | tf_op jit(solution)/shard_map/route/pallas_call | solution.py:95
  32.0 8.7 %all-to-all-start.1 = ((bf16[16,136,256]{2,1,0:T(8,128)(2,1)}), bf16[16,136,256]{2,1,0:T(8,128)(2,1)S(1)}, u32[]{:S(2)}, u32[]{:S(2)}) async-start(bf16[16,136,256]{2,1,0:T(8,128)(2,1)} %route.1), calls=%async_computation.1 | async-start | bytes 2228224 | tf_op jit(solution)/shard_map/all_to_all | solution.py:51
  40.8 18.8 %all-to-all-done.1 = bf16[16,136,256]{2,1,0:T(8,128)(2,1)S(1)} async-done(((bf16[16,136,256]{2,1,0:T(8,128)(2,1)}), bf16[16,136,256]{2,1,0:T(8,128)(2,1)S(1)}, u32[]{:S(2)}, u32[]{:S(2)}) %all-to-all-start.1) | async-done | bytes 1114144 | tf_op jit(solution)/shard_map/all_to_all | solution.py:51
  59.9 1.2 pad_maximum_fusion.1
  61.2 1.7 pad_maximum_fusion
  62.9 0.8 fusion.31
  63.6 0.8 fusion.30
  64.4 0.5 copy-done.5
  65.3 0.4 convolution_add_fusion.7
  67.1 0.4 convolution_add_fusion.3
  68.4 0.9 fusion.7
  70.1 1.0 reshape.91
  71.1 3.8 %convolution_convert_fusion.3.tokens_ref = bf16[128,768]{1,0:T(8,128)(2,1)S(1)} fusion(bf16[128,4096]{1,0:T(8,128)(2,1)S(1)} %reshape.91, bf16[4096,768]{1,0:T(8,128)(2,1)} %param.12), kind=kOutput, calls=%fused_computation.24 | convolution fusion | flops 805404672 | bytes 7536640 | tf_op jit(solution)/shard_map/dot_general | solution.py:240
  75.5 0.7 copy-done.4
  76.8 1.6 convolution_convert_fusion
  79.1 1.2 maximum_maximum_fusion
  80.3 38.7 %all_to_all.30 = bf16[64,32,640]{2,1,0:T(8,128)(2,1)S(1)} all-to-all(bf16[64,32,640]{2,1,0:T(8,128)(2,1)S(1)} %bitcast.105), channel_id=1, replica_groups=mesh['tile'=64,'slide'=2] {'tile'}, dimensions={0} | all-to-all | bytes 5242880 | tf_op jit(solution)/shard_map/all_to_all | solution.py:51
  119.0 21.5 %attend.1 = bf16[2048,256]{1,0:T(8,128)(2,1)S(1)} custom-call(bf16[2048,640]{1,0:T(8,128)(2,1)S(1)} %bitcast.101, bf16[2048,640]{1,0:T(8,128)(2,1)S(1)} %bitcast.102), custom_call_target="tpu_custom_call" | custom-call | tf_op jit(solution)/shard_map/attend/pallas_call | solution.py:143
  140.5 22.4 %all_to_all.31.parts_ref = bf16[64,32,256]{2,1,0:T(8,128)(2,1)} all-to-all(bf16[64,32,256]{2,1,0:T(8,128)(2,1)S(1)} %bitcast.103), channel_id=1, replica_groups=mesh['tile'=64,'slide'=2] {'tile'}, dimensions={0} | all-to-all | bytes 2097152 | tf_op jit(solution)/shard_map/all_to_all | solution.py:51
  162.9 6.7 %finish.1 = (bf16[128,768]{1,0:T(8,128)(2,1)}, bf16[6,768,128]{2,1,0:T(8,128)(2,1)}) custom-call(bf16[64,32,256]{2,1,0:T(8,128)(2,1)} %all_to_all.31.parts_ref, bf16[128,768]{1,0:T(8,128)(2,1)} %copy-done.2, bf16[768,768]{1,0:T(8,128)(2,1)} %weight_ref.1, bf16[128,768]{1,0:T(8,128)(2,1)} %cot_ref.1), custom_call_target="tpu_custom_call" | custom-call | tf_op jit(solution)/shard_map/finish/pallas_call | solution.py:182
  169.7 22.7 %all_to_all.32 = bf16[64,72,128]{2,1,0:T(8,128)(2,1)S(1)} all-to-all(bf16[64,72,128]{2,1,0:T(8,128)(2,1)} %bitcast.119), channel_id=1, replica_groups=mesh['tile'=64,'slide'=2] {'tile'}, dimensions={0} | all-to-all | bytes 2359296 | tf_op jit(solution)/shard_map/all_to_all | solution.py:51
  192.7 22.1 %all_to_all.33 = bf16[64,72,128]{2,1,0:T(8,128)(2,1)S(1)} all-to-all(bf16[64,72,128]{2,1,0:T(8,128)(2,1)S(1)} %broadcast_in_dim.58), channel_id=1, replica_groups=mesh['tile'=64,'slide'=2] {'tile'}, dimensions={0} | all-to-all | bytes 2359296 | tf_op jit(solution)/shard_map/all_to_all | solution.py:51
  215.0 2.0 copy.37
  216.9 3.0 %copy.38 = f32[768,768]{1,0:T(8,128)} copy(f32[768,768]{0,1:T(8,128)} %bitcast.106) | data formatting | bytes 4718592
  (45 shorter events, 6.4 us)
Async XLA Ops:
  0.6 74.2 %copy-start = (bf16[768,768]{1,0:T(8,128)(2,1)S(1)}, bf16[768,768]{1,0:T(8,128)(2,1)}, u32[]{:S(2)}) copy-start(bf16[768,768]{1,0:T(8,128)(2,1)} %param.13) | copy-start | bytes 3538948
  5.2 21.3 %all-to-all-start = ((bf16[8,2,136,256]{3,2,1,0:T(8,128)(2,1)}), bf16[8,2,136,256]{3,2,1,0:T(8,128)(2,1)S(1)}, u32[]{:S(2)}, u32[]{:S(2)}) async-start(bf16[8,2,136,256]{3,2,1,0:T(8,128)(2,1)} %broadcast_in_dim.23), calls=%async_computation | async-start | bytes 2228224 | tf_op jit(solution)/shard_map/all_to_all | solution.py:51
  26.5 1.0 copy-start.3
  32.0 27.9 %copy-start.1 = (bf16[2,32,32,256]{3,2,1,0:T(8,128)(2,1)S(1)}, bf16[2,32,32,256]{3,2,1,0:T(8,128)(2,1)}, u32[]{:S(2)}) copy-start(bf16[2,32,32,256]{3,2,1,0:T(8,128)(2,1)} %param.9) | copy-start | bytes 3145732
  32.0 27.6 %all-to-all-start.1 = ((bf16[16,136,256]{2,1,0:T(8,128)(2,1)}), bf16[16,136,256]{2,1,0:T(8,128)(2,1)S(1)}, u32[]{:S(2)}, u32[]{:S(2)}) async-start(bf16[16,136,256]{2,1,0:T(8,128)(2,1)} %route.1), calls=%async_computation.1 | async-start | bytes 2228224 | tf_op jit(solution)/shard_map/all_to_all | solution.py:51
  63.6 1.3 copy-start.5
  74.9 2.0 copy-start.2
  74.9 1.3 copy-start.4

commit v3 on v2

--- a/solution.py
+++ b/solution.py
@@ -13,7 +13,7 @@
 HG = HEADS // SPLIT
 GW = HG * HD
 BLK = 32
-QKVW = 640
+CHUNK = 144
 OW = 256
 HALO = 136
 BF = jnp.bfloat16
@@ -106,21 +106,29 @@
     )(links, mine, faces)
 
 
-def attend_kernel(q_ref, kv_ref, out_ref, key_ref, val_ref):
+def attend_kernel(in_ref, all_ref, out_ref, key_ref, val_ref):
     @pl.when(pl.program_id(0) == 0)
     def _():
-        lanes = lax.broadcasted_iota(jnp.int32, (2048, 64), 1)
+        lanes = lax.broadcasted_iota(jnp.int32, (2048, HD), 1)
         ones = jnp.where(lanes == 0, 1.0, 0.0).astype(BF)
         for g in range(HG):
-            key_ref[g] = kv_ref[:, GW + g * HD : GW + (g + 1) * HD]
-            val_ref[g, :, :HD] = kv_ref[:, 2 * GW + g * HD : 2 * GW + (g + 1) * HD]
             val_ref[g, :, HD:] = ones
-
-    rows = q_ref.shape[0]
-    lanes = lax.broadcasted_iota(jnp.int32, (rows, OW - GW), 1)
-    tail = jnp.zeros((rows, OW - GW), F32)
+        for g in range(2):
+            key_ref[g] = all_ref[:, 32:64, g * HD : (g + 1) * HD].reshape(2048, HD)
+            val_ref[g, :, :HD] = all_ref[:, 64:96, g * HD : (g + 1) * HD].reshape(2048, HD)
+            key_ref[2, g * 1024 : (g + 1) * 1024, :] = all_ref[
+                :, 96 + g * 16 : 112 + g * 16, HD:
+            ].reshape(1024, HD)
+            val_ref[2, g * 1024 : (g + 1) * 1024, :HD] = all_ref[
+                :, 128:144, g * HD : (g + 1) * HD
+            ].reshape(1024, HD)
+
+    rows = in_ref.shape[0] * BLK
+    lanes = lax.broadcasted_iota(jnp.int32, (rows, HD), 1)
+    tail = jnp.zeros((rows, HD), F32)
     for g in range(HG):
-        query = q_ref[:, g * HD : (g + 1) * HD] * BF(HD ** -0.5)
+        first, lane = ((0, 0), (0, HD), (96, 0))[g]
+        query = in_ref[:, first : first + BLK, lane : lane + HD].reshape(rows, HD) * BF(HD ** -0.5)
         scores = lax.dot_general(
             query, key_ref[g], (((1,), (1,)), ((), ())), preferred_element_type=F32
         )
@@ -130,24 +138,24 @@
         total = res[:, HD : HD + 1]
         out_ref[:, g * HD : (g + 1) * HD] = (res[:, :HD] / total).astype(BF)
         lse = top + jnp.log(total)
-        first = lse.astype(BF).astype(F32)
-        second = (lse - first).astype(BF).astype(F32)
-        third = lse - first - second
-        for n, part in enumerate((first, second, third)):
+        one = lse.astype(BF).astype(F32)
+        two = (lse - one).astype(BF).astype(F32)
+        three = lse - one - two
+        for n, part in enumerate((one, two, three)):
             tail = jnp.where(lanes == 3 * g + n, part, tail)
     out_ref[:, GW:] = tail.astype(BF)
 
 
 def attend(packed):
-    rows = 256
+    srcs = 8
     return pl.pallas_call(
         attend_kernel,
-        grid=(2048 // rows,),
+        grid=(64 // srcs,),
         in_specs=[
-            pl.BlockSpec((rows, QKVW), lambda i: (i, 0)),
-            pl.BlockSpec((2048, QKVW), lambda i: (0, 0)),
+            pl.BlockSpec((srcs, CHUNK, 128), lambda i: (i, 0, 0)),
+            pl.BlockSpec((64, CHUNK, 128), lambda i: (0, 0, 0)),
         ],
-        out_specs=pl.BlockSpec((rows, OW), lambda i: (i, 0)),
+        out_specs=pl.BlockSpec((srcs * BLK, OW), lambda i: (i, 0)),
         out_shape=jax.ShapeDtypeStruct((2048, OW), BF),
         scratch_shapes=[pltpu.VMEM((HG, 2048, HD), BF), pltpu.VMEM((HG, 2048, 2 * HD), BF)],
         compiler_params=pltpu.CompilerParams(vmem_limit_bytes=48 << 20),
@@ -168,7 +176,8 @@
                 ws = [jnp.exp(v - top) for v in lses]
                 total = ws[0] + ws[1] + ws[2] + ws[3]
                 acc = sum(w * p[:, g * HD : (g + 1) * HD] for w, p in zip(ws, pieces)) / total
-                att_ref[a * BLK : (a + 1) * BLK, h * GW + g * HD : h * GW + (g + 1) * HD] = acc.astype(BF)
+                head = 2 * h + g if g < 2 else 8 + h
+                att_ref[a * BLK : (a + 1) * BLK, head * HD : (head + 1) * HD] = acc.astype(BF)
     att = att_ref[...]
     grad = lax.dot_general(att, cot_ref[...], (((0,), (0,)), ((), ())), preferred_element_type=F32)
     for c in range(DM // 128):
@@ -190,30 +199,173 @@
     )(parts, tokens, weight, cot)
 
 
-def pad_tiles(maps, halo):
-    top_row = jnp.concatenate([halo[:, 128:129], halo[:, 0:32], halo[:, 129:130]], axis=1)
-    bottom_row = jnp.concatenate([halo[:, 130:131], halo[:, 32:64], halo[:, 131:132]], axis=1)
-    middle = jnp.concatenate([halo[:, 64:96, None], maps, halo[:, 96:128, None]], axis=2)
-    return jnp.concatenate([top_row[:, None], middle, bottom_row[:, None]], axis=1)
-
-
-def conv_tiles(padded, kernel):
-    count = padded.shape[0]
-    side = padded.shape[1] - 2
-    chans = padded.shape[3]
-    total = jnp.zeros((count * side * side, kernel.shape[3]), F32)
-    for row_off in range(3):
-        for col_off in range(3):
-            window = padded[:, row_off : row_off + side, col_off : col_off + side, :].reshape(-1, chans)
-            total = total + jnp.dot(window, kernel[row_off, col_off], preferred_element_type=F32)
-    return jax.nn.gelu(total).astype(BF).reshape(count, side, side, -1)
-
-
-def patchify(hidden, patch):
-    count, side, _, chans = hidden.shape
-    blocks = side // patch
-    grid = hidden.reshape(count, blocks, patch, blocks, patch, chans).transpose(0, 1, 3, 2, 4, 5)
-    return grid.reshape(count * blocks * blocks, patch * patch * chans)
+def spread_kernel(in_ref, out_ref):
+    out_ref[...] = in_ref[0].astype(F32)
+
+
+def spread(grad):
+    return pl.pallas_call(
+        spread_kernel,
+        grid=(DM // 128,),
+        in_specs=[pl.BlockSpec((1, DM, 128), lambda i: (i, 0, 0))],
+        out_specs=pl.BlockSpec((DM, 128), lambda i: (0, i)),
+        out_shape=jax.ShapeDtypeStruct((DM, DM), F32),
+        name="spread",
+    )(grad)
+
+
+ZW = 48
+Z0 = 8
+
+
+def stem_kernel(
+    halo_ref,
+    conv_ref,
+    features_hbm,
+    patch_hbm,
+    query_hbm,
+    key_hbm,
+    value_hbm,
+    tokens_ref,
+    packed_ref,
+    maps_ref,
+    side_ref,
+    left_ref,
+    mid_ref,
+    right_ref,
+    hid_ref,
+    patch_ref,
+    wq_ref,
+    wk_ref,
+    wv_ref,
+    sems,
+):
+    loads = [pltpu.make_async_copy(features_hbm.at[t], maps_ref.at[t, 1:33], sems.at[t]) for t in range(2)]
+    pairs = ((patch_hbm, patch_ref), (query_hbm, wq_ref), (key_hbm, wk_ref), (value_hbm, wv_ref))
+    loads += [pltpu.make_async_copy(src, dst, sems.at[2 + n]) for n, (src, dst) in enumerate(pairs)]
+    for load in loads:
+        load.start()
+    zrefs = (left_ref, mid_ref, right_ref)
+
+    def halo_rows(t, first, count):
+        total = halo_ref[0, t, first : first + count, :].astype(F32)
+        for n in range(1, 8):
+            total = total + halo_ref[n, t, first : first + count, :].astype(F32)
+        return total
+
+    for t in range(2):
+        maps_ref[t, 0] = halo_rows(t, 0, 32).astype(BF)
+        maps_ref[t, 33] = halo_rows(t, 32, 32).astype(BF)
+        corner = halo_rows(t, 128, 8)
+        for side in range(2):
+            side_ref[side, t, Z0 : Z0 + 32, :] = halo_rows(t, 64 + 32 * side, 32)
+            side_ref[side, t, Z0 - 1 : Z0, :] = corner[side : side + 1]
+            side_ref[side, t, Z0 + 32 : Z0 + 33, :] = corner[2 + side : 3 + side]
+    for t in range(2):
+        for side in range(2):
+            edge = jnp.zeros((32, 256), F32)
+            for dy in range(3):
+                part = side_ref[side, t, Z0 - 1 + dy : Z0 + 31 + dy, :].astype(BF)
+                edge = edge + jnp.dot(part, conv_ref[dy * 3 + side * 2], preferred_element_type=F32)
+            dest, first = ((left_ref, Z0 - 1), (right_ref, Z0 + 32))[side]
+            for lt in range(2):
+                dest[lt, pl.ds(t * 32 * ZW + first, 32, stride=ZW), :] = edge[:, lt * 128 : lt * 128 + 128]
+    for t in range(2):
+        loads[t].wait()
+        for y in range(0, 32, 8):
+            for dx in range(3):
+                acc = jnp.zeros((256, 256), F32)
+                for dy in range(3):
+                    rows = maps_ref[t, y + dy : y + dy + 8].reshape(256, 256)
+                    acc = acc + jnp.dot(rows, conv_ref[dy * 3 + dx], preferred_element_type=F32)
+                for n in range(8):
+                    first = (t * 32 + y + n) * ZW + Z0
+                    for lt in range(2):
+                        zrefs[dx][lt, first : first + 32, :] = acc[n * 32 : n * 32 + 32, lt * 128 : lt * 128 + 128]
+
+    for r in range(4):
+        for c in range(4):
+            for t in range(2):
+                for pr in range(8):
+                    first = (t * 32 + pr * 4 + r) * ZW + Z0 + c
+                    row = (t * 8 + pr) * 8
+                    for lt in range(2):
+                        total = (
+                            mid_ref[lt, pl.ds(first, 8, stride=4), :]
+                            + left_ref[lt, pl.ds(first - 1, 8, stride=4), :]
+                            + right_ref[lt, pl.ds(first + 1, 8, stride=4), :]
+                        )
+                        col = (r * 4 + c) * 256 + lt * 128
+                        hid_ref[row : row + 8, col : col + 128] = jax.nn.gelu(total).astype(BF)
+    loads[2].wait()
+    tokens = jnp.dot(hid_ref[...], patch_ref[...], preferred_element_type=F32).astype(BF)
+    tokens_ref[...] = tokens
+    for load in loads[3:]:
+        load.wait()
+    query = jnp.dot(tokens, wq_ref[...], preferred_element_type=F32)
+    keys = jnp.dot(tokens, wk_ref[...], preferred_element_type=F32)
+    values = jnp.dot(tokens, wv_ref[...], preferred_element_type=F32)
+    low = lax.broadcasted_iota(jnp.int32, (128, 128), 1) < HD
+
+    def pair_of(x, h):
+        return x[:, h * 128 : (h + 1) * 128]
+
+    for h in range(SPLIT):
+        one = 4 + h // 2
+        q1, k1, v1 = pair_of(query, one), pair_of(keys, one), pair_of(values, one)
+        if h % 2 == 0:
+            k1 = pltpu.roll(k1, HD, 1)
+            v2 = pltpu.roll(v1, HD, 1)
+        else:
+            q1 = pltpu.roll(q1, HD, 1)
+            v2 = v1
+            v1 = pltpu.roll(v1, HD, 1)
+        qk = jnp.where(low, q1, k1).astype(BF)
+        pieces = (pair_of(query, h).astype(BF), pair_of(keys, h).astype(BF), pair_of(values, h).astype(BF))
+        for a in range(SPLIT):
+            for b in range(SPLIT):
+                at = (h * SPLIT + a) * SPLIT + b
+                qa, kb = slice(a * BLK, (a + 1) * BLK), slice(b * BLK, (b + 1) * BLK)
+                packed_ref[at, 0:32, :] = pieces[0][qa]
+                packed_ref[at, 32:64, :] = pieces[1][kb]
+                packed_ref[at, 64:96, :] = pieces[2][kb]
+                if a == b:
+                    packed_ref[at, 96:128, :] = qk[qa]
+                else:
+                    packed_ref[at, 96:128, :] = jnp.where(low[:BLK], q1[qa], k1[kb]).astype(BF)
+                half = b * BLK + BLK // 2
+                packed_ref[at, 128:144, :] = jnp.where(
+                    low[: BLK // 2], v1[b * BLK : half], v2[half : (b + 1) * BLK]
+                ).astype(BF)
+
+
+def stem(halo, conv_weight, features, patch_weight, query_weight, key_weight, value_weight):
+    hbm = pl.BlockSpec(memory_space=pl.ANY)
+    vmem = pl.BlockSpec(memory_space=pltpu.VMEM)
+    return pl.pallas_call(
+        stem_kernel,
+        in_specs=[vmem, vmem] + [hbm] * 5,
+        out_specs=(vmem, vmem),
+        out_shape=(
+            jax.ShapeDtypeStruct((128, DM), BF),
+            jax.ShapeDtypeStruct((64, CHUNK, 128), BF),
+        ),
+        scratch_shapes=[
+            pltpu.VMEM((2, 34, 32, 256), BF),
+            pltpu.VMEM((2, 2, ZW, 256), F32),
+            pltpu.VMEM((2, 64 * ZW, 128), F32),
+            pltpu.VMEM((2, 64 * ZW, 128), F32),
+            pltpu.VMEM((2, 64 * ZW, 128), F32),
+            pltpu.VMEM((128, 4096), BF),
+            pltpu.VMEM((4096, DM), BF),
+            pltpu.VMEM((DM, DM), BF),
+            pltpu.VMEM((DM, DM), BF),
+            pltpu.VMEM((DM, DM), BF),
+            pltpu.SemaphoreType.DMA((6,)),
+        ],
+        compiler_params=pltpu.CompilerParams(vmem_limit_bytes=48 << 20),
+        name="stem",
+    )(halo, conv_weight, features, patch_weight, query_weight, key_weight, value_weight)
 
 
 def local(
@@ -235,35 +387,17 @@
     faces = swap(jnp.broadcast_to(faces[None], (8,) + faces.shape), INNER).reshape(16, HALO, 256)
     links = faces[:, 128, :8].astype(jnp.int32).reshape(128)
     halo = swap(route(links, inner.reshape(1), faces), OUTER).reshape(8, 2, HALO, 256)
-    halo = jnp.sum(halo.astype(F32), axis=0).astype(BF)
-    hidden = conv_tiles(pad_tiles(features, halo), conv_weight)
-    tokens = jnp.dot(patchify(hidden, PATCH), patch_weight, preferred_element_type=F32).astype(BF)
-    query = jnp.dot(tokens, query_weight, preferred_element_type=F32).astype(BF)
-    keys = jnp.dot(tokens, key_weight, preferred_element_type=F32).astype(BF)
-    values = jnp.dot(tokens, value_weight, preferred_element_type=F32).astype(BF)
-
-    def by_block(x):
-        return x.reshape(SPLIT, BLK, SPLIT, GW).transpose(2, 0, 1, 3)
-
-    full = (SPLIT, SPLIT, SPLIT, BLK, GW)
-    packed = jnp.concatenate(
-        [
-            jnp.broadcast_to(by_block(query)[:, :, None], full),
-            jnp.broadcast_to(by_block(keys)[:, None], full),
-            jnp.broadcast_to(by_block(values)[:, None], full),
-            jnp.zeros((SPLIT, SPLIT, SPLIT, BLK, QKVW - 3 * GW), BF),
-        ],
-        axis=-1,
-    ).reshape(64, BLK, QKVW)
-    packed = swap(packed).reshape(64 * BLK, QKVW)
+    halo, conv_weight = lax.optimization_barrier((halo, conv_weight))
+    taps = conv_weight.reshape(9, 256, 256)
+    tokens, packed = stem(halo, taps, features, patch_weight, query_weight, key_weight, value_weight)
+    packed = swap(packed)
     parts = swap(attend(packed).reshape(64, BLK, OW))
     mixed, grad = finish(parts, tokens, output_weight, cotangent)
 
     grad = swap(grad.reshape(64, 72, 128))
     grad = jnp.sum(grad.astype(F32), axis=0).astype(BF)
     grad = swap(jnp.broadcast_to(grad[None], (64, 72, 128)))
-    grad = grad.reshape(DM // 128, DM, 128).transpose(1, 0, 2).reshape(DM, DM)
-    return mixed, grad.astype(F32)
+    return mixed, spread(grad.reshape(DM // 128, DM, 128))
 
 
 def solution(mesh):

time: 221 us -> 204 us (0.923)
  blocking collectives: 106 us -> 130 us
  waiting for transfers between devices: 34.9 us -> 16.1 us
  Pallas kernels: 32.7 us -> 45 us
  matrix products: 10.4 us -> 0 us
  local copies, waits for them, and re-layouts: 15.8 us -> 5.56 us
  starting transfers between devices: 14 us -> 5.38 us
  other arithmetic: 5.32 us -> 0.9 us
    all_to_all x4 -> x5, blocking collectives: 106 us -> 130 us  [swap(): lax.all_to_all(x, 'tile', split_axis=0, concat_axis=0, tiled=True, axis_i...]
    all_to_all x2 -> x1, waiting for transfers between devices: 34.9 us -> 16.1 us  [swap(): lax.all_to_all(x, 'tile', split_axis=0, concat_axis=0, tiled=True, axis_i...]
    pallas_call x1 -> x3, Pallas kernels: 21.5 us -> 34.2 us  [the longest x1 21.8 us: attend(): pl.pallas_call(attend_kernel, grid=(64 // srcs,), in_specs=[pl.BlockSpec(...]
    dot_general x13 -> x0, matrix products: 10.4 us -> none  [the longest x9 4.38 us: conv_tiles(): jnp.dot(window, kernel[row_off, col_off], preferred_element_type=F32)]
    all_to_all x2 -> x1, starting transfers between devices: 14 us -> 5.38 us  [swap(): lax.all_to_all(x, 'tile', split_axis=0, concat_axis=0, tiled=True, axis_i...]
    concatenate x3 -> x0, other arithmetic: 4.07 us -> none  [the longest x1 1.69 us: pad_tiles(): jnp.concatenate([top_row[:, None], middle, bottom_row[:, None]], axis=1)]
    unnamed x17 -> x16, local copies, waits for them, and re-layouts: 6.05 us -> 2.47 us
  transfers between devices with their start and end apart: 2 -> 1, of which waited for: 2 -> 1; matrix products, arithmetic and copies ran while one was open for 0% -> 0% of each run, Pallas kernels for 0% -> 0%
where the time goes in v3:
time: 204 us; the launch traced here: 203 us
  blocking collectives  130 us (64%)
  Pallas kernels  45 us (22%)
  waiting for transfers between devices  16.1 us (8%)
  local copies, waits for them, and re-layouts  5.56 us (3%)
  starting transfers between devices  5.38 us (3%)
    all_to_all x5, blocking collectives, swap(): lax.all_to_all(x, 'tile', split_axis=0, concat_axis=0, tiled=True, axis_i...  130 us
    pallas_call x1, Pallas kernels, attend(): pl.pallas_call(attend_kernel, grid=(64 // srcs,), in_specs=[pl.BlockSpec(...  21.8 us
    all_to_all x1, waiting for transfers between devices, swap(): lax.all_to_all(x, 'tile', split_axis=0, concat_axis=0, tiled=True, axis_i...  16.1 us
    pallas_call x1, Pallas kernels, stem(): pl.pallas_call(stem_kernel, in_specs=[vmem, vmem] + [hbm] * 5, out_specs=...  7.77 us
    pallas_call x1, Pallas kernels, finish(): pl.pallas_call(finish_kernel, out_shape=(jax.ShapeDtypeStruct((128, DM),...  6.28 us
    all_to_all x1, starting transfers between devices, swap(): lax.all_to_all(x, 'tile', split_axis=0, concat_axis=0, tiled=True, axis_i...  5.38 us
    pallas_call x1, Pallas kernels, spread(): pl.pallas_call(spread_kernel, grid=(DM // 128,), in_specs=[pl.BlockSpec((...  4.61 us
    pallas_call x1, Pallas kernels, route(): pl.pallas_call(route_kernel, grid=(1,), in_specs=[pl.BlockSpec(memory_spa...  4.52 us
  transfers between devices with their start and end apart: 1, of which 1 were waited for; matrix products, arithmetic and copies ran while one was open for 0% of the time, Pallas kernels for 0%

profile of v3, /device:TPU:0, one launch (start us, length us, event | category | flops | bytes accessed | tf_op | source)
XLA Modules:
  0.0 203.3 jit_solution(9040834843796643216)
XLA Ops:
  0.6 1.1 fusion.3
  1.8 0.8 bitcast_dynamic-update-slice_fusion.1
  2.5 0.7 convert_bitcast_fusion
  3.2 0.8 bitcast_dynamic-update-slice_fusion
  4.0 1.1 broadcast_in_dim.7
  5.1 0.0 copy-start.3
  5.1 5.4 %all-to-all-start = ((bf16[8,2,136,256]{3,2,1,0:T(8,128)(2,1)}), bf16[8,2,136,256]{3,2,1,0:T(8,128)(2,1)S(1)}, u32[]{:S(2)}, u32[]{:S(2)}) async-start(bf16[8,2,136,256]{3,2,1,0:T(8,128)(2,1)} %broadcast_in_dim.7), calls=%async_computation | async-start | bytes 2228224 | tf_op jit(solution)/shard_map/all_to_all | solution.py:51
  10.5 16.1 %all-to-all-done = bf16[8,2,136,256]{3,2,1,0:T(8,128)(2,1)S(1)} async-done(((bf16[8,2,136,256]{3,2,1,0:T(8,128)(2,1)}), bf16[8,2,136,256]{3,2,1,0:T(8,128)(2,1)S(1)}, u32[]{:S(2)}, u32[]{:S(2)}) %all-to-all-start) | async-done | bytes 1114144 | tf_op jit(solution)/shard_map/all_to_all | solution.py:51
  26.6 0.0 copy-start.5
  26.6 0.7 reshape.38.links_ref
  27.3 0.2 copy-done.5
  27.6 0.0 copy-start.2
  27.6 4.5 %route.1 = bf16[16,136,256]{2,1,0:T(8,128)(2,1)} custom-call(s32[128]{0:T(128)} %reshape.38.links_ref, s32[1]{0:T(128)} %bitcast.6.mine_ref, bf16[16,136,256]{2,1,0:T(8,128)(2,1)} %bitcast.30), custom_call_target="tpu_custom_call" | custom-call | tf_op jit(solution)/shard_map/route/pallas_call | solution.py:95
  32.1 0.0 copy-start
  32.1 0.0 copy-start.1
  32.1 27.6 %all_to_all.30 = bf16[16,136,256]{2,1,0:T(8,128)(2,1)S(1)} all-to-all(bf16[16,136,256]{2,1,0:T(8,128)(2,1)} %route.1), channel_id=1, replica_groups={{0,6,24,30,96,102,120,126},{2,4,26,28,98,100,122,124},{8,14,16,22,104,1..., dimensions={0} | all-to-all | bytes 2228224 | tf_op jit(solution)/shard_map/all_to_all | solution.py:51
  59.7 0.0 copy-done.3
  59.7 0.0 copy-done.2
  59.7 0.0 copy-done
  59.7 0.0 copy-done.1
  59.7 7.8 %stem.1 = (bf16[128,768]{1,0:T(8,128)(2,1)S(1)}, bf16[64,144,128]{2,1,0:T(8,128)(2,1)}) custom-call(bf16[8,2,136,256]{3,2,1,0:T(8,128)(2,1)S(1)} %bitcast.25, bf16[9,256,256]{2,1,0:T(8,128)(2,1)S(1)} %bitcast.27, bf16[2,32,32,256]{3,2,1,0:T(8,128)(2,1)S(1)} %copy-done, bf16[4096,768]{1,0:T(8,128)(2,1)} %patch_hbm.1, bf16[768,768]{1,0:T(8,128)(2,1)S(1)} %copy-done.2, ...), custom_call_target="tpu_custom_call" | custom-call | tf_op jit(solution)/shard_map/stem/pallas_call | solution.py:345
  67.5 0.0 copy-start.4
  67.5 0.7 copy-done.4
  68.2 35.9 %all_to_all.31.in_ref.all_ref = bf16[64,144,128]{2,1,0:T(8,128)(2,1)S(1)} all-to-all(bf16[64,144,128]{2,1,0:T(8,128)(2,1)} %get-tuple-element.10), channel_id=1, replica_groups=mesh['tile'=64,'slide'=2] {'tile'}, dimensions={0} | all-to-all | bytes 4718592 | tf_op jit(solution)/shard_map/all_to_all | solution.py:51
  104.0 21.8 %attend.1 = bf16[2048,256]{1,0:T(8,128)(2,1)S(1)} custom-call(bf16[64,144,128]{2,1,0:T(8,128)(2,1)S(1)} %all_to_all.31.in_ref.all_ref, bf16[64,144,128]{2,1,0:T(8,128)(2,1)S(1)} %all_to_all.31.in_ref.all_ref), custom_call_target="tpu_custom_call" | custom-call | tf_op jit(solution)/shard_map/attend/pallas_call | solution.py:151
  125.9 22.2 %all_to_all.32.parts_ref = bf16[64,32,256]{2,1,0:T(8,128)(2,1)} all-to-all(bf16[64,32,256]{2,1,0:T(8,128)(2,1)S(1)} %bitcast.26), channel_id=1, replica_groups=mesh['tile'=64,'slide'=2] {'tile'}, dimensions={0} | all-to-all | bytes 2097152 | tf_op jit(solution)/shard_map/all_to_all | solution.py:51
  148.1 6.3 %finish.1 = (bf16[128,768]{1,0:T(8,128)(2,1)}, bf16[6,768,128]{2,1,0:T(8,128)(2,1)}) custom-call(bf16[64,32,256]{2,1,0:T(8,128)(2,1)} %all_to_all.32.parts_ref, bf16[128,768]{1,0:T(8,128)(2,1)} %copy-done.4, bf16[768,768]{1,0:T(8,128)(2,1)} %weight_ref.1, bf16[128,768]{1,0:T(8,128)(2,1)} %cot_ref.1), custom_call_target="tpu_custom_call" | custom-call | tf_op jit(solution)/shard_map/finish/pallas_call | solution.py:191
  154.4 22.3 %all_to_all.33 = bf16[64,72,128]{2,1,0:T(8,128)(2,1)S(1)} all-to-all(bf16[64,72,128]{2,1,0:T(8,128)(2,1)} %bitcast.31), channel_id=1, replica_groups=mesh['tile'=64,'slide'=2] {'tile'}, dimensions={0} | all-to-all | bytes 2359296 | tf_op jit(solution)/shard_map/all_to_all | solution.py:51
  176.7 0.2 reduce_sum.12
  176.9 0.2 broadcast_in_dim.8
  177.0 21.7 %all_to_all.34 = bf16[64,72,128]{2,1,0:T(8,128)(2,1)} all-to-all(bf16[64,72,128]{2,1,0:T(8,128)(2,1)S(1)} %broadcast_in_dim.8), channel_id=1, replica_groups=mesh['tile'=64,'slide'=2] {'tile'}, dimensions={0} | all-to-all | bytes 2359296 | tf_op jit(solution)/shard_map/all_to_all | solution.py:51
  198.7 4.6 %spread.1 = f32[768,768]{1,0:T(8,128)} custom-call(bf16[6,768,128]{2,1,0:T(8,128)(2,1)} %bitcast.28), custom_call_target="tpu_custom_call" | custom-call | tf_op jit(solution)/shard_map/spread/pallas_call | solution.py:207
  (5 shorter events, 0.1 us)
Async XLA Ops:
  5.1 54.6 %copy-start.3 = (bf16[768,768]{1,0:T(8,128)(2,1)S(1)}, bf16[768,768]{1,0:T(8,128)(2,1)}, u32[]{:S(2)}) copy-start(bf16[768,768]{1,0:T(8,128)(2,1)} %key_hbm.1) | copy-start | bytes 3538948
  5.1 21.5 %all-to-all-start = ((bf16[8,2,136,256]{3,2,1,0:T(8,128)(2,1)}), bf16[8,2,136,256]{3,2,1,0:T(8,128)(2,1)S(1)}, u32[]{:S(2)}, u32[]{:S(2)}) async-start(bf16[8,2,136,256]{3,2,1,0:T(8,128)(2,1)} %broadcast_in_dim.7), calls=%async_computation | async-start | bytes 2228224 | tf_op jit(solution)/shard_map/all_to_all | solution.py:51
  26.6 1.0 copy-start.5
  27.6 32.1 %copy-start.2 = (bf16[768,768]{1,0:T(8,128)(2,1)S(1)}, bf16[768,768]{1,0:T(8,128)(2,1)}, u32[]{:S(2)}) copy-start(bf16[768,768]{1,0:T(8,128)(2,1)} %query_hbm.1) | copy-start | bytes 3538948
  32.1 27.6 %copy-start = (bf16[2,32,32,256]{3,2,1,0:T(8,128)(2,1)S(1)}, bf16[2,32,32,256]{3,2,1,0:T(8,128)(2,1)}, u32[]{:S(2)}) copy-start(bf16[2,32,32,256]{3,2,1,0:T(8,128)(2,1)} %features_hbm.1) | copy-start | bytes 3145732
  32.1 27.6 %copy-start.1 = (bf16[3,3,256,256]{3,2,1,0:T(8,128)(2,1)S(1)}, bf16[3,3,256,256]{3,2,1,0:T(8,128)(2,1)}, u32[]{:S(2)}) copy-start(bf16[3,3,256,256]{3,2,1,0:T(8,128)(2,1)} %param.11) | copy-start | bytes 3538948
  67.5 0.7 copy-start.4

commit v4 on v3

--- a/solution.py
+++ b/solution.py
@@ -47,6 +47,17 @@
 INNER, OUTER = device_groups()
 
 
+def place(h, a, b):
+    def coord(hi, lo):
+        return hi * 2 + (hi ^ lo)
+
+    return coord(a >> 1, b >> 1) * 16 + coord(a & 1, b & 1) * 4 + h
+
+
+KEY_GROUPS = [[place(h, a, b) for b in range(SPLIT)] for h in range(SPLIT) for a in range(SPLIT)]
+HEAD_GROUPS = [[place(h, a, b) for a in range(SPLIT) for b in range(SPLIT)] for h in range(SPLIT)]
+
+
 def swap(x, groups=None):
     return lax.all_to_all(
         x, "tile", split_axis=0, concat_axis=0, tiled=True, axis_index_groups=groups
@@ -106,7 +117,7 @@
     )(links, mine, faces)
 
 
-def attend_kernel(in_ref, all_ref, out_ref, key_ref, val_ref):
+def attend_kernel(in_ref, all_ref, out_ref, key_ref, val_ref, row_ref):
     @pl.when(pl.program_id(0) == 0)
     def _():
         lanes = lax.broadcasted_iota(jnp.int32, (2048, HD), 1)
@@ -126,24 +137,30 @@
     rows = in_ref.shape[0] * BLK
     lanes = lax.broadcasted_iota(jnp.int32, (rows, HD), 1)
     tail = jnp.zeros((rows, HD), F32)
+    scores = []
     for g in range(HG):
         first, lane = ((0, 0), (0, HD), (96, 0))[g]
         query = in_ref[:, first : first + BLK, lane : lane + HD].reshape(rows, HD) * BF(HD ** -0.5)
-        scores = lax.dot_general(
-            query, key_ref[g], (((1,), (1,)), ((), ())), preferred_element_type=F32
+        scores.append(
+            lax.dot_general(query, key_ref[g], (((1,), (1,)), ((), ())), preferred_element_type=F32)
         )
-        top = jnp.max(scores, axis=1, keepdims=True)
-        weights = jnp.exp(scores - top).astype(BF)
+    for g in range(HG):
+        top = jnp.max(scores[g], axis=1, keepdims=True)
+        weights = jnp.exp(scores[g] - top).astype(BF)
         res = jnp.dot(weights, val_ref[g], preferred_element_type=F32)
         total = res[:, HD : HD + 1]
-        out_ref[:, g * HD : (g + 1) * HD] = (res[:, :HD] / total).astype(BF)
+        row_ref[:, g * HD : (g + 1) * HD] = res[:, :HD] / total
         lse = top + jnp.log(total)
         one = lse.astype(BF).astype(F32)
         two = (lse - one).astype(BF).astype(F32)
         three = lse - one - two
         for n, part in enumerate((one, two, three)):
             tail = jnp.where(lanes == 3 * g + n, part, tail)
-    out_ref[:, GW:] = tail.astype(BF)
+    row_ref[:, GW:] = tail
+    for n in range(rows // BLK):
+        for b in range(SPLIT):
+            first = n * BLK + b * 8
+            out_ref[b, n * 8 : n * 8 + 8, :] = row_ref[first : first + 8, :].astype(BF)
 
 
 def attend(packed):
@@ -155,63 +172,119 @@
             pl.BlockSpec((srcs, CHUNK, 128), lambda i: (i, 0, 0)),
             pl.BlockSpec((64, CHUNK, 128), lambda i: (0, 0, 0)),
         ],
-        out_specs=pl.BlockSpec((srcs * BLK, OW), lambda i: (i, 0)),
-        out_shape=jax.ShapeDtypeStruct((2048, OW), BF),
-        scratch_shapes=[pltpu.VMEM((HG, 2048, HD), BF), pltpu.VMEM((HG, 2048, 2 * HD), BF)],
+        out_specs=pl.BlockSpec((SPLIT, srcs * 8, OW), lambda i: (0, i, 0)),
+        out_shape=jax.ShapeDtypeStruct((SPLIT, 512, OW), BF),
+        scratch_shapes=[
+            pltpu.VMEM((HG, 2048, HD), BF),
+            pltpu.VMEM((HG, 2048, 2 * HD), BF),
+            pltpu.VMEM((srcs * BLK, OW), F32),
+        ],
         compiler_params=pltpu.CompilerParams(vmem_limit_bytes=48 << 20),
         name="attend",
     )(packed, packed)
 
 
-def finish_kernel(parts_ref, tokens_ref, weight_ref, cot_ref, mixed_ref, grad_ref, att_ref):
+SHARE = 72
+ROWS = SHARE + 16
+
+
+def merge_kernel(parts_ref, cot_ref, att_ref, grad_ref, pair_ref, single_ref):
+    tails = []
+    for b in range(SPLIT):
+        tail = parts_ref[b, :, 128:].astype(F32)
+        tails.append(tail + pltpu.roll(tail, 127, 1) + pltpu.roll(tail, 126, 1))
+    top = jnp.maximum(jnp.maximum(tails[0], tails[1]), jnp.maximum(tails[2], tails[3]))
+    ws = [jnp.exp(tail - top) for tail in tails]
+    total = ws[0] + ws[1] + ws[2] + ws[3]
+    low = lax.broadcasted_iota(jnp.int32, (512, 128), 1) < HD
+    pair = jnp.zeros((512, 128), F32)
+    single = jnp.zeros((512, 128), F32)
+    for b in range(SPLIT):
+        share = ws[b] / total
+        w0, w1, w2 = (share[:, HD + 3 * g : HD + 3 * g + 1] for g in range(HG))
+        pair = pair + jnp.where(low, w0, w1) * parts_ref[b, :, :128].astype(F32)
+        single = single + w2 * parts_ref[b, :, 128:].astype(F32)
+    single = jnp.where(low, single, 0.0)
+    pair_ref[...] = pair.astype(BF)
+    single_ref[...] = single.astype(BF)
+    for n in range(64):
+        att_ref[n, :8, :] = pair[n * 8 : n * 8 + 8].astype(BF)
+        att_ref[n, 8:, :] = single[n * 8 : n * 8 + 8].astype(BF)
+    for first, ref, count in ((0, pair_ref, 128), (128, single_ref, 64)):
+        grad = lax.dot_general(
+            ref[...], cot_ref[...], (((0,), (0,)), ((), ())), preferred_element_type=F32
+        )
+        for c in range(DM // 128):
+            grad_ref[c, first : first + count, :] = grad[:count, c * 128 : (c + 1) * 128].astype(BF)
+
+
+def merge(parts, cot):
+    return pl.pallas_call(
+        merge_kernel,
+        out_shape=(
+            jax.ShapeDtypeStruct((64, 16, 128), BF),
+            jax.ShapeDtypeStruct((DM // 128, GW, 128), BF),
+        ),
+        scratch_shapes=[pltpu.VMEM((512, 128), BF), pltpu.VMEM((512, 128), BF)],
+        name="merge",
+    )(parts, cot)
+
+
+def share_kernel(terms_ref, att_ref, out_ref):
+    total = terms_ref[0].astype(F32)
+    for n in range(1, 16):
+        total = total + terms_ref[n].astype(F32)
+    total = total.astype(BF)
+    for n in range(64):
+        out_ref[n, :SHARE, :] = total
+        out_ref[n, SHARE:, :] = att_ref[n]
+
+
+def share_out(terms, att):
+    return pl.pallas_call(
+        share_kernel, out_shape=jax.ShapeDtypeStruct((64, ROWS, 128), BF), name="share"
+    )(terms, att)
+
+
+def finish_kernel(all_ref, tokens_ref, weight_ref, mixed_ref, grad_ref, att_ref):
+    lanes = lax.broadcasted_iota(jnp.int32, (8, 128), 1) < HD
+    for a in range(SPLIT):
+        for b in range(SPLIT):
+            row = a * BLK + b * 8
+            for h in range(SPLIT):
+                att_ref[row : row + 8, h * 128 : (h + 1) * 128] = all_ref[place(h, a, b), SHARE : SHARE + 8, :]
+            for h in range(0, SPLIT, 2):
+                even = all_ref[place(h, a, b), SHARE + 8 :, :].astype(F32)
+                odd = pltpu.roll(all_ref[place(h + 1, a, b), SHARE + 8 :, :].astype(F32), HD, 1)
+                first = 512 + h * HD
+                att_ref[row : row + 8, first : first + 128] = jnp.where(lanes, even, odd).astype(BF)
     for h in range(SPLIT):
-        for a in range(SPLIT):
-            pieces = [parts_ref[(h * SPLIT + a) * SPLIT + b].astype(F32) for b in range(SPLIT)]
-            for g in range(HG):
-                col = GW + 3 * g
-                lses = [
-                    p[:, col : col + 1] + p[:, col + 1 : col + 2] + p[:, col + 2 : col + 3] for p in pieces
-                ]
-                top = jnp.maximum(jnp.maximum(lses[0], lses[1]), jnp.maximum(lses[2], lses[3]))
-                ws = [jnp.exp(v - top) for v in lses]
-                total = ws[0] + ws[1] + ws[2] + ws[3]
-                acc = sum(w * p[:, g * HD : (g + 1) * HD] for w, p in zip(ws, pieces)) / total
-                head = 2 * h + g if g < 2 else 8 + h
-                att_ref[a * BLK : (a + 1) * BLK, head * HD : (head + 1) * HD] = acc.astype(BF)
-    att = att_ref[...]
-    grad = lax.dot_general(att, cot_ref[...], (((0,), (0,)), ((), ())), preferred_element_type=F32)
-    for c in range(DM // 128):
-        grad_ref[c] = grad[:, c * 128 : (c + 1) * 128].astype(BF)
+        for m in range(16):
+            at = place(h, m // SPLIT, m % SPLIT)
+            done = 0
+            while done < SHARE:
+                block, row = divmod(m * SHARE + done, GW)
+                count = min(SHARE - done, (128 if row < 128 else GW) - row)
+                dest = h * 128 + row if row < 128 else 512 + h * HD + row - 128
+                grad_ref[dest : dest + count, block * 128 : (block + 1) * 128] = all_ref[
+                    at, done : done + count, :
+                ].astype(F32)
+                done += count
     mixed_ref[...] = (
-        tokens_ref[...].astype(F32) + jnp.dot(att, weight_ref[...], preferred_element_type=F32)
+        tokens_ref[...].astype(F32) + jnp.dot(att_ref[...], weight_ref[...], preferred_element_type=F32)
     ).astype(BF)
 
 
-def finish(parts, tokens, weight, cot):
+def finish(received, tokens, weight):
     return pl.pallas_call(
         finish_kernel,
         out_shape=(
             jax.ShapeDtypeStruct((128, DM), BF),
-            jax.ShapeDtypeStruct((DM // 128, DM, 128), BF),
+            jax.ShapeDtypeStruct((DM, DM), F32),
         ),
         scratch_shapes=[pltpu.VMEM((128, DM), BF)],
         name="finish",
-    )(parts, tokens, weight, cot)
-
-
-def spread_kernel(in_ref, out_ref):
-    out_ref[...] = in_ref[0].astype(F32)
-
-
-def spread(grad):
-    return pl.pallas_call(
-        spread_kernel,
-        grid=(DM // 128,),
-        in_specs=[pl.BlockSpec((1, DM, 128), lambda i: (i, 0, 0))],
-        out_specs=pl.BlockSpec((DM, 128), lambda i: (0, i)),
-        out_shape=jax.ShapeDtypeStruct((DM, DM), F32),
-        name="spread",
-    )(grad)
+    )(received, tokens, weight)
 
 
 ZW = 48
@@ -221,6 +294,7 @@
 def stem_kernel(
     halo_ref,
     conv_ref,
+    cot_ref,
     features_hbm,
     patch_hbm,
     query_hbm,
@@ -228,6 +302,7 @@
     value_hbm,
     tokens_ref,
     packed_ref,
+    cots_ref,
     maps_ref,
     side_ref,
     left_ref,
@@ -324,7 +399,8 @@
         pieces = (pair_of(query, h).astype(BF), pair_of(keys, h).astype(BF), pair_of(values, h).astype(BF))
         for a in range(SPLIT):
             for b in range(SPLIT):
-                at = (h * SPLIT + a) * SPLIT + b
+                at = place(h, a, b)
+                cots_ref[at] = cot_ref[a * BLK + b * 8 : a * BLK + b * 8 + 8, :]
                 qa, kb = slice(a * BLK, (a + 1) * BLK), slice(b * BLK, (b + 1) * BLK)
                 packed_ref[at, 0:32, :] = pieces[0][qa]
                 packed_ref[at, 32:64, :] = pieces[1][kb]
@@ -339,16 +415,17 @@
                 ).astype(BF)
 
 
-def stem(halo, conv_weight, features, patch_weight, query_weight, key_weight, value_weight):
+def stem(halo, conv_weight, cotangent, features, patch_weight, query_weight, key_weight, value_weight):
     hbm = pl.BlockSpec(memory_space=pl.ANY)
     vmem = pl.BlockSpec(memory_space=pltpu.VMEM)
     return pl.pallas_call(
         stem_kernel,
-        in_specs=[vmem, vmem] + [hbm] * 5,
-        out_specs=(vmem, vmem),
+        in_specs=[vmem, vmem, vmem] + [hbm] * 5,
+        out_specs=(vmem, vmem, vmem),
         out_shape=(
             jax.ShapeDtypeStruct((128, DM), BF),
             jax.ShapeDtypeStruct((64, CHUNK, 128), BF),
+            jax.ShapeDtypeStruct((64, 8, DM), BF),
         ),
         scratch_shapes=[
             pltpu.VMEM((2, 34, 32, 256), BF),
@@ -365,7 +442,7 @@
         ],
         compiler_params=pltpu.CompilerParams(vmem_limit_bytes=48 << 20),
         name="stem",
-    )(halo, conv_weight, features, patch_weight, query_weight, key_weight, value_weight)
+    )(halo, conv_weight, cotangent, features, patch_weight, query_weight, key_weight, value_weight)
 
 
 def local(
@@ -389,15 +466,17 @@
     halo = swap(route(links, inner.reshape(1), faces), OUTER).reshape(8, 2, HALO, 256)
     halo, conv_weight = lax.optimization_barrier((halo, conv_weight))
     taps = conv_weight.reshape(9, 256, 256)
-    tokens, packed = stem(halo, taps, features, patch_weight, query_weight, key_weight, value_weight)
+    tokens, packed, cots = stem(
+        halo, taps, cotangent, features, patch_weight, query_weight, key_weight, value_weight
+    )
     packed = swap(packed)
-    parts = swap(attend(packed).reshape(64, BLK, OW))
-    mixed, grad = finish(parts, tokens, output_weight, cotangent)
-
-    grad = swap(grad.reshape(64, 72, 128))
-    grad = jnp.sum(grad.astype(F32), axis=0).astype(BF)
-    grad = swap(jnp.broadcast_to(grad[None], (64, 72, 128)))
-    return mixed, spread(grad.reshape(DM // 128, DM, 128))
+    packed, cots = lax.optimization_barrier((packed, cots))
+    cots = swap(cots).reshape(512, DM)
+    parts = swap(attend(packed), KEY_GROUPS)
+    att, grad = merge(parts, cots)
+    terms = swap(grad.reshape(16, SHARE, 128), HEAD_GROUPS)
+    received = swap(share_out(terms, att))
+    return finish(received, tokens, output_weight)
 
 
 def solution(mesh):

time: 204 us -> 195 us (0.956)
  blocking collectives: 130 us -> 119 us
  starting transfers between devices: 5.38 us -> 10.7 us
  Pallas kernels: 45 us -> 41.6 us
    all_to_all x5, blocking collectives: 130 us -> 119 us  [swap(): lax.all_to_all(x, 'tile', split_axis=0, concat_axis=0, tiled=True, axis_i...]
    all_to_all x1 -> x2, starting transfers between devices: 5.38 us -> 10.7 us  [swap(): lax.all_to_all(x, 'tile', split_axis=0, concat_axis=0, tiled=True, axis_i...]
    pallas_call x1, Pallas kernels: 21.8 us -> 19.1 us  [attend(): pl.pallas_call(attend_kernel, grid=(64 // srcs,), in_specs=[pl.BlockSpec(...]
    pallas_call x1, Pallas kernels: 6.28 us -> 3.67 us  [finish(): pl.pallas_call(finish_kernel, out_shape=(jax.ShapeDtypeStruct((128, DM),...]
    pallas_call x2 -> x3, Pallas kernels: 12.4 us -> 14.3 us  [the longest x1 7.73 us: stem(): pl.pallas_call(stem_kernel, in_specs=[vmem, vmem, vmem] + [hbm] * 5, out_...]
    all_to_all x1 -> x2, waiting for transfers between devices: 16.1 us -> 16.1 us  [swap(): lax.all_to_all(x, 'tile', split_axis=0, concat_axis=0, tiled=True, axis_i...]
  transfers between devices with their start and end apart: 1 -> 2, of which waited for: 1 -> 1; matrix products, arithmetic and copies ran while one was open for 0% -> 0% of each run, Pallas kernels for 0% -> 10%
where the time goes in v4:
time: 195 us; the launch traced here: 194 us
  blocking collectives  119 us (61%)
  Pallas kernels  41.6 us (21%)
  waiting for transfers between devices  16.1 us (8%)
  starting transfers between devices  10.7 us (5%)
  local copies, waits for them, and re-layouts  4.74 us (2%)
    all_to_all x5, blocking collectives, swap(): lax.all_to_all(x, 'tile', split_axis=0, concat_axis=0, tiled=True, axis_i...  119 us
    pallas_call x1, Pallas kernels, attend(): pl.pallas_call(attend_kernel, grid=(64 // srcs,), in_specs=[pl.BlockSpec(...  19.1 us
    all_to_all x2, waiting for transfers between devices, swap(): lax.all_to_all(x, 'tile', split_axis=0, concat_axis=0, tiled=True, axis_i...  16.1 us
    all_to_all x2, starting transfers between devices, swap(): lax.all_to_all(x, 'tile', split_axis=0, concat_axis=0, tiled=True, axis_i...  10.7 us
    pallas_call x1, Pallas kernels, stem(): pl.pallas_call(stem_kernel, in_specs=[vmem, vmem, vmem] + [hbm] * 5, out_...  7.73 us
    pallas_call x1, Pallas kernels, route(): pl.pallas_call(route_kernel, grid=(1,), in_specs=[pl.BlockSpec(memory_spa...  4.55 us
    pallas_call x1, Pallas kernels, merge(): pl.pallas_call(merge_kernel, out_shape=(jax.ShapeDtypeStruct((64, 16, 128...  4.3 us
  transfers between devices with their start and end apart: 2, of which 1 were waited for; matrix products, arithmetic and copies ran while one was open for 0% of the time, Pallas kernels for 10%

profile of v4, /device:TPU:0, one launch (start us, length us, event | category | flops | bytes accessed | tf_op | source)
XLA Modules:
  0.0 193.8 jit_solution(15077356465481022146)
XLA Ops:
  0.6 1.1 fusion.3
  1.8 0.8 bitcast_dynamic-update-slice_fusion.1
  2.5 0.7 convert_bitcast_fusion
  3.2 0.8 bitcast_dynamic-update-slice_fusion
  4.0 1.1 broadcast_in_dim.10
  5.1 5.2 %all-to-all-start = ((bf16[8,2,136,256]{3,2,1,0:T(8,128)(2,1)}), bf16[8,2,136,256]{3,2,1,0:T(8,128)(2,1)S(1)}, u32[]{:S(2)}, u32[]{:S(2)}) async-start(bf16[8,2,136,256]{3,2,1,0:T(8,128)(2,1)} %broadcast_in_dim.10), calls=%async_computation | async-start | bytes 2228224 | tf_op jit(solution)/shard_map/all_to_all | solution.py:62
  10.3 16.1 %all-to-all-done = bf16[8,2,136,256]{3,2,1,0:T(8,128)(2,1)S(1)} async-done(((bf16[8,2,136,256]{3,2,1,0:T(8,128)(2,1)}), bf16[8,2,136,256]{3,2,1,0:T(8,128)(2,1)S(1)}, u32[]{:S(2)}, u32[]{:S(2)}) %all-to-all-start) | async-done | bytes 1114144 | tf_op jit(solution)/shard_map/all_to_all | solution.py:62
  26.4 0.0 copy-start.5
  26.5 0.7 reshape.33.links_ref
  27.2 0.2 copy-done.5
  27.4 0.0 copy-start.2
  27.4 0.0 copy-start.3
  27.4 4.6 %route.1 = bf16[16,136,256]{2,1,0:T(8,128)(2,1)} custom-call(s32[128]{0:T(128)} %reshape.33.links_ref, s32[1]{0:T(128)} %bitcast.6.mine_ref, bf16[16,136,256]{2,1,0:T(8,128)(2,1)} %bitcast.27), custom_call_target="tpu_custom_call" | custom-call | tf_op jit(solution)/shard_map/route/pallas_call | solution.py:106
  32.0 0.0 copy-start
  32.0 27.6 %all_to_all.35 = bf16[16,136,256]{2,1,0:T(8,128)(2,1)S(1)} all-to-all(bf16[16,136,256]{2,1,0:T(8,128)(2,1)} %route.1), channel_id=1, replica_groups={{0,6,24,30,96,102,120,126},{2,4,26,28,98,100,122,124},{8,14,16,22,104,1..., dimensions={0} | all-to-all | bytes 2228224 | tf_op jit(solution)/shard_map/all_to_all | solution.py:62
  59.6 0.0 copy-done.2
  59.6 0.0 copy-done.3
  59.6 0.0 copy-done
  59.6 0.0 copy-done.1
  59.6 7.7 %stem.1 = (bf16[128,768]{1,0:T(8,128)(2,1)S(1)}, bf16[64,144,128]{2,1,0:T(8,128)(2,1)}, bf16[64,8,768]{2,1,0:T(8,128)(2,1)}) custom-call(bf16[8,2,136,256]{3,2,1,0:T(8,128)(2,1)S(1)} %bitcast.24, bf16[9,256,256]{2,1,0:T(8,128)(2,1)S(1)} %bitcast.25, bf16[128,768]{1,0:T(8,128)(2,1)S(1)} %copy-done.3, bf16[2,32,32,256]{3,2,1,0:T(8,128)(2,1)S(1)} %copy-done, ...), custom_call_target="tpu_custom_call" | custom-call | tf_op jit(solution)/shard_map/stem/pallas_call | solution.py:421
  67.3 0.0 copy-start.4
  67.4 35.9 %all_to_all.36.in_ref.all_ref = bf16[64,144,128]{2,1,0:T(8,128)(2,1)S(1)} all-to-all(bf16[64,144,128]{2,1,0:T(8,128)(2,1)} %get-tuple-element.13), channel_id=1, replica_groups=mesh['tile'=64,'slide'=2] {'tile'}, dimensions={0} | all-to-all | bytes 4718592 | tf_op jit(solution)/shard_map/all_to_all | solution.py:62
  103.2 0.0 copy-done.4
  103.2 5.5 %all-to-all-start.4 = ((bf16[64,8,768]{2,1,0:T(8,128)(2,1)}), bf16[64,8,768]{2,1,0:T(8,128)(2,1)}, u32[]{:S(2)}, u32[]{:S(2)}) async-start(bf16[64,8,768]{2,1,0:T(8,128)(2,1)} %get-tuple-element.16), calls=%async_computation.4 | async-start | bytes 1572864 | tf_op jit(solution)/shard_map/all_to_all | solution.py:62
  108.7 19.1 %attend.1 = bf16[4,512,256]{2,1,0:T(8,128)(2,1)S(1)} custom-call(bf16[64,144,128]{2,1,0:T(8,128)(2,1)S(1)} %all_to_all.36.in_ref.all_ref, bf16[64,144,128]{2,1,0:T(8,128)(2,1)S(1)} %all_to_all.36.in_ref.all_ref), custom_call_target="tpu_custom_call" | custom-call | tf_op jit(solution)/shard_map/attend/pallas_call | solution.py:168
  127.9 0.0 all-to-all-done.4
  127.9 15.5 %all_to_all.37.parts_ref = bf16[4,512,256]{2,1,0:T(8,128)(2,1)} all-to-all(bf16[4,512,256]{2,1,0:T(8,128)(2,1)S(1)} %attend.1), channel_id=1, replica_groups={{0,8,32,40},{24,16,56,48},{96,104,64,72},{120,112,88,80},{2,10,34,42},{..., dimensions={0} | all-to-all | bytes 2097152 | tf_op jit(solution)/shard_map/all_to_all | solution.py:62
  143.3 4.3 %merge.1 = (bf16[64,16,128]{2,1,0:T(8,128)(2,1)}, bf16[6,192,128]{2,1,0:T(8,128)(2,1)}) custom-call(bf16[4,512,256]{2,1,0:T(8,128)(2,1)} %all_to_all.37.parts_ref, bf16[512,768]{1,0:T(8,128)(2,1)} %bitcast.9.cot_ref), custom_call_target="tpu_custom_call" | custom-call | tf_op jit(solution)/shard_map/merge/pallas_call | solution.py:222
  147.6 15.5 %all_to_all.38.terms_ref = bf16[16,72,128]{2,1,0:T(8,128)(2,1)} all-to-all(bf16[16,72,128]{2,1,0:T(8,128)(2,1)} %bitcast.28), channel_id=1, replica_groups={{0,8,32,40,24,16,56,48,96,104,64,72,120,112,88,80},{2,10,34,42,26,18,58..., dimensions={0} | all-to-all | bytes 589824 | tf_op jit(solution)/shard_map/all_to_all | solution.py:62
  163.2 2.2 %share.1 = bf16[64,88,128]{2,1,0:T(8,128)(2,1)} custom-call(bf16[16,72,128]{2,1,0:T(8,128)(2,1)} %all_to_all.38.terms_ref, bf16[64,16,128]{2,1,0:T(8,128)(2,1)} %get-tuple-element.18.att_ref), custom_call_target="tpu_custom_call" | custom-call | tf_op jit(solution)/shard_map/share/pallas_call | solution.py:244
  165.4 24.6 %all_to_all.39.all_ref = bf16[64,88,128]{2,1,0:T(8,128)(2,1)} all-to-all(bf16[64,88,128]{2,1,0:T(8,128)(2,1)} %share.1), channel_id=1, replica_groups=mesh['tile'=64,'slide'=2] {'tile'}, dimensions={0} | all-to-all | bytes 2883584 | tf_op jit(solution)/shard_map/all_to_all | solution.py:62
  190.1 3.7 %finish.1 = (bf16[128,768]{1,0:T(8,128)(2,1)}, f32[768,768]{1,0:T(8,128)}) custom-call(bf16[64,88,128]{2,1,0:T(8,128)(2,1)} %all_to_all.39.all_ref, bf16[128,768]{1,0:T(8,128)(2,1)} %copy-done.4, bf16[768,768]{1,0:T(8,128)(2,1)} %weight_ref.1), custom_call_target="tpu_custom_call" | custom-call | tf_op jit(solution)/shard_map/finish/pallas_call | solution.py:279
  (6 shorter events, 0.1 us)
Async XLA Ops:
  5.1 21.3 %all-to-all-start = ((bf16[8,2,136,256]{3,2,1,0:T(8,128)(2,1)}), bf16[8,2,136,256]{3,2,1,0:T(8,128)(2,1)S(1)}, u32[]{:S(2)}, u32[]{:S(2)}) async-start(bf16[8,2,136,256]{3,2,1,0:T(8,128)(2,1)} %broadcast_in_dim.10), calls=%async_computation | async-start | bytes 2228224 | tf_op jit(solution)/shard_map/all_to_all | solution.py:62
  26.4 1.0 copy-start.5
  27.4 32.2 %copy-start.2 = (bf16[768,768]{1,0:T(8,128)(2,1)S(1)}, bf16[768,768]{1,0:T(8,128)(2,1)}, u32[]{:S(2)}) copy-start(bf16[768,768]{1,0:T(8,128)(2,1)} %query_hbm.1) | copy-start | bytes 3538948
  27.4 32.2 %copy-start.3 = (bf16[128,768]{1,0:T(8,128)(2,1)S(1)}, bf16[128,768]{1,0:T(8,128)(2,1)}, u32[]{:S(2)}) copy-start(bf16[128,768]{1,0:T(8,128)(2,1)} %cot_ref.1) | copy-start | bytes 589828
  32.0 27.6 %copy-start = (bf16[2,32,32,256]{3,2,1,0:T(8,128)(2,1)S(1)}, bf16[2,32,32,256]{3,2,1,0:T(8,128)(2,1)}, u32[]{:S(2)}) copy-start(bf16[2,32,32,256]{3,2,1,0:T(8,128)(2,1)} %features_hbm.1) | copy-start | bytes 3145732
  32.0 27.6 %copy-start.1 = (bf16[3,3,256,256]{3,2,1,0:T(8,128)(2,1)S(1)}, bf16[3,3,256,256]{3,2,1,0:T(8,128)(2,1)}, u32[]{:S(2)}) copy-start(bf16[3,3,256,256]{3,2,1,0:T(8,128)(2,1)} %param.11) | copy-start | bytes 3538948
  67.3 35.9 %copy-start.4 = (bf16[128,768]{1,0:T(8,128)(2,1)}, bf16[128,768]{1,0:T(8,128)(2,1)S(1)}, u32[]{:S(2)}) copy-start(bf16[128,768]{1,0:T(8,128)(2,1)S(1)} %get-tuple-element.19.tokens_ref) | copy-start | bytes 589828
  103.2 24.6 %all-to-all-start.4 = ((bf16[64,8,768]{2,1,0:T(8,128)(2,1)}), bf16[64,8,768]{2,1,0:T(8,128)(2,1)}, u32[]{:S(2)}, u32[]{:S(2)}) async-start(bf16[64,8,768]{2,1,0:T(8,128)(2,1)} %get-tuple-element.16), calls=%async_computation.4 | async-start | bytes 1572864 | tf_op jit(solution)/shard_map/all_to_all | solution.py:62

commit v5 on v4

--- a/solution.py
+++ b/solution.py
@@ -13,7 +13,7 @@
 HG = HEADS // SPLIT
 GW = HG * HD
 BLK = 32
-CHUNK = 144
+CHUNK = 96
 OW = 256
 HALO = 136
 BF = jnp.bfloat16
@@ -64,109 +64,187 @@
     )
 
 
-EDGES = ((1, 0, 32), (6, 32, 0), (3, 64, 96), (4, 96, 64))
-CORNERS = ((0, 0, 3), (2, 31, 2), (5, 32, 1), (7, 63, 0))
-
-
-def route_kernel(links_ref, mine_ref, faces_ref, out_ref):
+def faces_kernel(links_ref, features_hbm, out_hbm, sides_ref, cols_ref, faces_ref, sems):
+    loads = []
+    for t in range(2):
+        for n, y in enumerate((0, 31)):
+            loads.append((features_hbm.at[t, y], faces_ref.at[t, n * 32 : n * 32 + 32]))
+        for n, x in enumerate((0, 24)):
+            loads.append((features_hbm.at[t, :, x : x + 8], sides_ref.at[t, n]))
+    loads = [pltpu.make_async_copy(src, dst, sems.at[n]) for n, (src, dst) in enumerate(loads)]
+    for load in loads:
+        load.start()
+    lanes = lax.broadcasted_iota(jnp.int32, (8, 128), 1)
+    for t in range(2):
+        row = jnp.zeros((8, 128), F32)
+        for d in range(8):
+            row = jnp.where(lanes == d, links_ref[t, d].astype(F32), row)
+        faces_ref[t, 128:HALO, :128] = row.astype(BF)
+        faces_ref[t, 128:HALO, 128:] = jnp.zeros((8, 128), BF)
+    for load in loads:
+        load.wait()
+    for t in range(2):
+        for n, x in enumerate((0, 7)):
+            for lt in range(2):
+                cols_ref[...] = sides_ref[t, n, :, :, lt * 128 : lt * 128 + 128].astype(F32).reshape(256, 128)
+                faces_ref[t, 64 + n * 32 : 96 + n * 32, lt * 128 : lt * 128 + 128] = cols_ref[
+                    pl.ds(x, 32, stride=8), :
+                ].astype(BF)
+    stores = [pltpu.make_async_copy(faces_ref, out_hbm.at[n], sems.at[n]) for n in range(8)]
+    for store in stores:
+        store.start()
+    for store in stores:
+        store.wait()
+
+
+def gather_faces(links, features):
+    hbm = pl.BlockSpec(memory_space=pl.ANY)
+    return pl.pallas_call(
+        faces_kernel,
+        in_specs=[pl.BlockSpec(memory_space=pltpu.SMEM), hbm],
+        out_specs=hbm,
+        out_shape=jax.ShapeDtypeStruct((8, 2, HALO, 256), BF),
+        scratch_shapes=[
+            pltpu.VMEM((2, 2, 32, 8, 256), BF),
+            pltpu.VMEM((256, 128), F32),
+            pltpu.VMEM((2, HALO, 256), BF),
+            pltpu.SemaphoreType.DMA((8,)),
+        ],
+        name="faces",
+    )(links, features)
+
+
+EDGES = {1: (0, 32), 6: (32, 0), 3: (64, 96), 4: (96, 64)}
+CORNERS = {0: (0, 3), 2: (31, 2), 5: (32, 1), 7: (63, 0)}
+
+
+def route_kernel(targets_ref, faces_ref, out_ref):
     out_ref[...] = jnp.zeros(out_ref.shape, BF)
-    mine = mine_ref[0]
     row_ids = lax.broadcasted_iota(jnp.int32, (8, 256), 0)
 
     def per_tile(src, carry):
-        def target(direction):
-            tile = links_ref[src * 8 + direction]
-            outer, inner = split_device(tile >> 1)
-            return (tile < 128) & (inner == mine), outer & 7, tile & 1
-
-        for direction, first, dest in EDGES:
-            hit, outer, slot = target(direction)
-
-            @pl.when(hit)
+        for direction in range(8):
+            target = targets_ref[src, direction]
+
+            @pl.when(target >= 0)
             def _():
-                out_ref[outer * 2 + slot, dest : dest + 32, :] = faces_ref[src, first : first + 32, :]
-
-        for direction, row, dest in CORNERS:
-            hit, outer, slot = target(direction)
-
-            @pl.when(hit)
-            def _():
-                base = row // 8 * 8
-                cell = faces_ref[src, base : base + 8, :].astype(F32)[row - base : row - base + 1, :]
-                old = out_ref[outer * 2 + slot, 128:HALO, :].astype(F32)
-                new = jnp.where(row_ids == dest, jnp.broadcast_to(cell, (8, 256)), old)
-                out_ref[outer * 2 + slot, 128:HALO, :] = new.astype(BF)
+                if direction in EDGES:
+                    first, dest = EDGES[direction]
+                    out_ref[target, dest : dest + 32, :] = faces_ref[src, first : first + 32, :]
+                else:
+                    row, dest = CORNERS[direction]
+                    base = row // 8 * 8
+                    cell = faces_ref[src, base : base + 8, :].astype(F32)[row - base : row - base + 1, :]
+                    old = out_ref[target, 128:HALO, :].astype(F32)
+                    new = jnp.where(row_ids == dest, jnp.broadcast_to(cell, (8, 256)), old)
+                    out_ref[target, 128:HALO, :] = new.astype(BF)
 
         return carry
 
     lax.fori_loop(0, 16, per_tile, 0)
 
 
-def route(links, mine, faces):
+def route(targets, faces):
+    vmem = pl.BlockSpec(memory_space=pltpu.VMEM)
     return pl.pallas_call(
         route_kernel,
-        grid=(1,),
-        in_specs=[
-            pl.BlockSpec(memory_space=pltpu.SMEM),
-            pl.BlockSpec(memory_space=pltpu.SMEM),
-            pl.BlockSpec((16, HALO, 256), lambda i: (0, 0, 0)),
-        ],
-        out_specs=pl.BlockSpec((16, HALO, 256), lambda i: (0, 0, 0)),
+        in_specs=[pl.BlockSpec(memory_space=pltpu.SMEM), vmem],
+        out_specs=vmem,
         out_shape=jax.ShapeDtypeStruct((16, HALO, 256), BF),
         name="route",
-    )(links, mine, faces)
-
-
-def attend_kernel(in_ref, all_ref, out_ref, key_ref, val_ref, row_ref):
+    )(targets, faces)
+
+
+def attend_heads(units):
+    scores = [
+        lax.dot_general(q * BF(HD ** -0.5), k, (((1,), (1,)), ((), ())), preferred_element_type=F32)
+        for q, k, _ in units
+    ]
+    results = []
+    for score, (_, _, value) in zip(scores, units):
+        top = jnp.max(score, axis=1, keepdims=True)
+        weights = jnp.exp(score - top).astype(BF)
+        res = jnp.dot(weights, value, preferred_element_type=F32)
+        total = res[:, HD : HD + 1]
+        lse = top + jnp.log(total)
+        one = lse.astype(BF).astype(F32)
+        two = (lse - one).astype(BF).astype(F32)
+        results.append((res[:, :HD] / total, (one, two, lse - one - two)))
+    return results
+
+
+def put_rows(row_ref, out_ref, lanes):
+    for n in range(row_ref.shape[0] // BLK):
+        for b in range(SPLIT):
+            first = n * BLK + b * 8
+            out_ref[b, n * 8 : n * 8 + 8, :] = row_ref[first : first + 8, lanes].astype(BF)
+
+
+def pair_kernel(in_ref, all_ref, out_ref, key_ref, val_ref, row_ref):
     @pl.when(pl.program_id(0) == 0)
     def _():
-        lanes = lax.broadcasted_iota(jnp.int32, (2048, HD), 1)
-        ones = jnp.where(lanes == 0, 1.0, 0.0).astype(BF)
-        for g in range(HG):
-            val_ref[g, :, HD:] = ones
+        ones = jnp.where(lax.broadcasted_iota(jnp.int32, (2048, HD), 1) == 0, 1.0, 0.0).astype(BF)
         for g in range(2):
             key_ref[g] = all_ref[:, 32:64, g * HD : (g + 1) * HD].reshape(2048, HD)
             val_ref[g, :, :HD] = all_ref[:, 64:96, g * HD : (g + 1) * HD].reshape(2048, HD)
-            key_ref[2, g * 1024 : (g + 1) * 1024, :] = all_ref[
-                :, 96 + g * 16 : 112 + g * 16, HD:
-            ].reshape(1024, HD)
-            val_ref[2, g * 1024 : (g + 1) * 1024, :HD] = all_ref[
-                :, 128:144, g * HD : (g + 1) * HD
-            ].reshape(1024, HD)
-
-    rows = in_ref.shape[0] * BLK
-    lanes = lax.broadcasted_iota(jnp.int32, (rows, HD), 1)
-    tail = jnp.zeros((rows, HD), F32)
-    scores = []
-    for g in range(HG):
-        first, lane = ((0, 0), (0, HD), (96, 0))[g]
-        query = in_ref[:, first : first + BLK, lane : lane + HD].reshape(rows, HD) * BF(HD ** -0.5)
-        scores.append(
-            lax.dot_general(query, key_ref[g], (((1,), (1,)), ((), ())), preferred_element_type=F32)
-        )
-    for g in range(HG):
-        top = jnp.max(scores[g], axis=1, keepdims=True)
-        weights = jnp.exp(scores[g] - top).astype(BF)
-        res = jnp.dot(weights, val_ref[g], preferred_element_type=F32)
-        total = res[:, HD : HD + 1]
-        row_ref[:, g * HD : (g + 1) * HD] = res[:, :HD] / total
-        lse = top + jnp.log(total)
-        one = lse.astype(BF).astype(F32)
-        two = (lse - one).astype(BF).astype(F32)
-        three = lse - one - two
-        for n, part in enumerate((one, two, three)):
-            tail = jnp.where(lanes == 3 * g + n, part, tail)
-    row_ref[:, GW:] = tail
-    for n in range(rows // BLK):
+            val_ref[g, :, HD:] = ones
+
+    half = 8
+    units = []
+    for first in range(0, in_ref.shape[0], half):
+        for g in range(2):
+            query = in_ref[first : first + half, :BLK, g * HD : (g + 1) * HD].reshape(half * BLK, HD)
+            units.append((query, key_ref[g], val_ref[g]))
+    results = attend_heads(units)
+    lanes = lax.broadcasted_iota(jnp.int32, (half * BLK, 128), 1)
+    for n in range(len(units) // 2):
+        rows = slice(n * half * BLK, (n + 1) * half * BLK)
+        tail = jnp.zeros((half * BLK, 128), F32)
+        for g in range(2):
+            out, parts = results[2 * n + g]
+            row_ref[rows, g * HD : (g + 1) * HD] = out
+            for i, part in enumerate(parts):
+                tail = jnp.where(lanes == HD + 3 * g + i, part, tail)
+        row_ref[rows, 128:] = tail
+    put_rows(row_ref, out_ref, slice(0, OW))
+
+
+def single_kernel(in_ref, all_ref, part_ref, out_ref, key_ref, val_ref, row_ref):
+    @pl.when(pl.program_id(0) == 0)
+    def _():
+        ones = jnp.where(lax.broadcasted_iota(jnp.int32, (2048, HD), 1) == 0, 1.0, 0.0).astype(BF)
+        val_ref[:, HD:] = ones
+        for g in range(2):
+            rows = slice(g * 1024, (g + 1) * 1024)
+            key_ref[rows, :] = all_ref[:, g * 16 : g * 16 + 16, HD:].reshape(1024, HD)
+            val_ref[rows, :HD] = all_ref[:, 32:48, g * HD : (g + 1) * HD].reshape(1024, HD)
+
+    half = 8
+    units = []
+    for first in range(0, in_ref.shape[0], half):
+        query = in_ref[first : first + half, :BLK, :HD].reshape(half * BLK, HD)
+        units.append((query, key_ref[...], val_ref[...]))
+    results = attend_heads(units)
+    lanes = lax.broadcasted_iota(jnp.int32, (half * BLK, 128), 1)
+    for n, (out, parts) in enumerate(results):
+        rows = slice(n * half * BLK, (n + 1) * half * BLK)
+        tail = jnp.zeros((half * BLK, 128), F32)
+        for i, part in enumerate(parts):
+            tail = jnp.where(lanes == HD + 6 + i, part, tail)
+        row_ref[rows, :] = tail
+        row_ref[rows, :HD] = out
+    for n in range(row_ref.shape[0] // BLK):
         for b in range(SPLIT):
             first = n * BLK + b * 8
-            out_ref[b, n * 8 : n * 8 + 8, :] = row_ref[first : first + 8, :].astype(BF)
-
-
-def attend(packed):
-    srcs = 8
-    return pl.pallas_call(
-        attend_kernel,
+            old = part_ref[b, n * 8 : n * 8 + 8, 128:].astype(F32)
+            out_ref[b, n * 8 : n * 8 + 8, :128] = part_ref[b, n * 8 : n * 8 + 8, :128]
+            out_ref[b, n * 8 : n * 8 + 8, 128:] = (old + row_ref[first : first + 8, :]).astype(BF)
+
+
+def attend_pair(packed):
+    srcs = 16
+    return pl.pallas_call(
+        pair_kernel,
         grid=(64 // srcs,),
         in_specs=[
             pl.BlockSpec((srcs, CHUNK, 128), lambda i: (i, 0, 0)),
@@ -175,20 +253,45 @@
         out_specs=pl.BlockSpec((SPLIT, srcs * 8, OW), lambda i: (0, i, 0)),
         out_shape=jax.ShapeDtypeStruct((SPLIT, 512, OW), BF),
         scratch_shapes=[
-            pltpu.VMEM((HG, 2048, HD), BF),
-            pltpu.VMEM((HG, 2048, 2 * HD), BF),
+            pltpu.VMEM((2, 2048, HD), BF),
+            pltpu.VMEM((2, 2048, 2 * HD), BF),
             pltpu.VMEM((srcs * BLK, OW), F32),
         ],
         compiler_params=pltpu.CompilerParams(vmem_limit_bytes=48 << 20),
-        name="attend",
+        name="attend_pair",
     )(packed, packed)
+
+
+def attend_single(rest, parts):
+    srcs = 16
+    block = pl.BlockSpec((SPLIT, srcs * 8, OW), lambda i: (0, i, 0))
+    return pl.pallas_call(
+        single_kernel,
+        grid=(64 // srcs,),
+        in_specs=[
+            pl.BlockSpec((srcs, CHUNK, 128), lambda i: (i, 0, 0)),
+            pl.BlockSpec((64, CHUNK, 128), lambda i: (0, 0, 0)),
+            block,
+        ],
+        out_specs=block,
+        out_shape=jax.ShapeDtypeStruct((SPLIT, 512, OW), BF),
+        scratch_shapes=[
+            pltpu.VMEM((2048, HD), BF),
+            pltpu.VMEM((2048, 2 * HD), BF),
+            pltpu.VMEM((srcs * BLK, 128), F32),
+        ],
+        compiler_params=pltpu.CompilerParams(vmem_limit_bytes=48 << 20),
+        name="attend_single",
+    )(rest, rest, parts)
 
 
 SHARE = 72
 ROWS = SHARE + 16
 
 
-def merge_kernel(parts_ref, cot_ref, att_ref, grad_ref, pair_ref, single_ref):
+def merge_kernel(parts_ref, rest_ref, att_ref, grad_ref, pair_ref, single_ref, cot_ref):
+    for c in range(DM // 128):
+        cot_ref[:, c * 128 : (c + 1) * 128] = rest_ref[:, 48 + 8 * c : 56 + 8 * c, :].reshape(512, 128)
     tails = []
     for b in range(SPLIT):
         tail = parts_ref[b, :, 128:].astype(F32)
@@ -218,16 +321,16 @@
             grad_ref[c, first : first + count, :] = grad[:count, c * 128 : (c + 1) * 128].astype(BF)
 
 
-def merge(parts, cot):
+def merge(parts, rest):
     return pl.pallas_call(
         merge_kernel,
         out_shape=(
             jax.ShapeDtypeStruct((64, 16, 128), BF),
             jax.ShapeDtypeStruct((DM // 128, GW, 128), BF),
         ),
-        scratch_shapes=[pltpu.VMEM((512, 128), BF), pltpu.VMEM((512, 128), BF)],
+        scratch_shapes=[pltpu.VMEM((512, 128), BF), pltpu.VMEM((512, 128), BF), pltpu.VMEM((512, DM), BF)],
         name="merge",
-    )(parts, cot)
+    )(parts, rest)
 
 
 def share_kernel(terms_ref, att_ref, out_ref):
@@ -302,7 +405,7 @@
     value_hbm,
     tokens_ref,
     packed_ref,
-    cots_ref,
+    rest_ref,
     maps_ref,
     side_ref,
     left_ref,
@@ -395,24 +498,22 @@
             q1 = pltpu.roll(q1, HD, 1)
             v2 = v1
             v1 = pltpu.roll(v1, HD, 1)
-        qk = jnp.where(low, q1, k1).astype(BF)
         pieces = (pair_of(query, h).astype(BF), pair_of(keys, h).astype(BF), pair_of(values, h).astype(BF))
         for a in range(SPLIT):
             for b in range(SPLIT):
                 at = place(h, a, b)
-                cots_ref[at] = cot_ref[a * BLK + b * 8 : a * BLK + b * 8 + 8, :]
                 qa, kb = slice(a * BLK, (a + 1) * BLK), slice(b * BLK, (b + 1) * BLK)
                 packed_ref[at, 0:32, :] = pieces[0][qa]
                 packed_ref[at, 32:64, :] = pieces[1][kb]
                 packed_ref[at, 64:96, :] = pieces[2][kb]
-                if a == b:
-                    packed_ref[at, 96:128, :] = qk[qa]
-                else:
-                    packed_ref[at, 96:128, :] = jnp.where(low[:BLK], q1[qa], k1[kb]).astype(BF)
+                rest_ref[at, 0:32, :] = jnp.where(low[:BLK], q1[qa], k1[kb]).astype(BF)
                 half = b * BLK + BLK // 2
-                packed_ref[at, 128:144, :] = jnp.where(
+                rest_ref[at, 32:48, :] = jnp.where(
                     low[: BLK // 2], v1[b * BLK : half], v2[half : (b + 1) * BLK]
                 ).astype(BF)
+                row = a * BLK + b * 8
+                for c in range(DM // 128):
+                    rest_ref[at, 48 + 8 * c : 56 + 8 * c, :] = cot_ref[row : row + 8, c * 128 : (c + 1) * 128]
 
 
 def stem(halo, conv_weight, cotangent, features, patch_weight, query_weight, key_weight, value_weight):
@@ -425,7 +526,7 @@
         out_shape=(
             jax.ShapeDtypeStruct((128, DM), BF),
             jax.ShapeDtypeStruct((64, CHUNK, 128), BF),
-            jax.ShapeDtypeStruct((64, 8, DM), BF),
+            jax.ShapeDtypeStruct((64, CHUNK, 128), BF),
         ),
         scratch_shapes=[
             pltpu.VMEM((2, 34, 32, 256), BF),
@@ -456,24 +557,22 @@
     output_weight,
     cotangent,
 ):
-    outer, inner = split_device(lax.axis_index("tile"))
-    link_rows = jnp.pad(neighbours.astype(BF)[:, None, :], ((0, 0), (0, 7), (0, 248)))
-    faces = jnp.concatenate(
-        [features[:, 0], features[:, -1], features[:, :, 0], features[:, :, -1], link_rows], axis=1
-    )
-    faces = swap(jnp.broadcast_to(faces[None], (8,) + faces.shape), INNER).reshape(16, HALO, 256)
-    links = faces[:, 128, :8].astype(jnp.int32).reshape(128)
-    halo = swap(route(links, inner.reshape(1), faces), OUTER).reshape(8, 2, HALO, 256)
+    _, inner = split_device(lax.axis_index("tile"))
+    faces = swap(gather_faces(neighbours, features), INNER).reshape(16, HALO, 256)
+    tiles = faces[:, 128, :8].astype(jnp.int32)
+    outer, goal = split_device(tiles >> 1)
+    targets = jnp.where((tiles < 128) & (goal == inner), (outer & 7) * 2 + (tiles & 1), -1)
+    halo = swap(route(targets, faces), OUTER).reshape(8, 2, HALO, 256)
     halo, conv_weight = lax.optimization_barrier((halo, conv_weight))
     taps = conv_weight.reshape(9, 256, 256)
-    tokens, packed, cots = stem(
+    tokens, packed, rest = stem(
         halo, taps, cotangent, features, patch_weight, query_weight, key_weight, value_weight
     )
     packed = swap(packed)
-    packed, cots = lax.optimization_barrier((packed, cots))
-    cots = swap(cots).reshape(512, DM)
-    parts = swap(attend(packed), KEY_GROUPS)
-    att, grad = merge(parts, cots)
+    packed, rest = lax.optimization_barrier((packed, rest))
+    rest = swap(rest)
+    parts = swap(attend_single(rest, attend_pair(packed)), KEY_GROUPS)
+    att, grad = merge(parts, rest)
     terms = swap(grad.reshape(16, SHARE, 128), HEAD_GROUPS)
     received = swap(share_out(terms, att))
     return finish(received, tokens, output_weight)

time: 195 us -> 190 us (0.974)
  blocking collectives: 119 us -> 105 us
  waiting for transfers between devices: 16.1 us -> 24.6 us
  Pallas kernels: 41.6 us -> 44.3 us
    all_to_all x5, blocking collectives: 119 us -> 105 us  [swap(): lax.all_to_all(x, 'tile', split_axis=0, concat_axis=0, tiled=True, axis_i...]
    all_to_all x2, waiting for transfers between devices: 16.1 us -> 24.6 us  [swap(): lax.all_to_all(x, 'tile', split_axis=0, concat_axis=0, tiled=True, axis_i...]
    pallas_call x2 -> x4, Pallas kernels: 23.7 us -> 25.8 us  [the longest x1 11.9 us: attend_pair(): pl.pallas_call(pair_kernel, grid=(64 // srcs,), in_specs=[pl.BlockSpec((s...]
  transfers between devices with their start and end apart: 2 -> 2, of which waited for: 1 -> 2; matrix products, arithmetic and copies ran while one was open for 0% -> 0% of each run, Pallas kernels for 10% -> 6%
where the time goes in v5:
time: 190 us; the launch traced here: 189 us
  blocking collectives  105 us (55%)
  Pallas kernels  44.3 us (23%)
  waiting for transfers between devices  24.6 us (13%)
  starting transfers between devices  10.4 us (5%)
  local copies, waits for them, and re-layouts  3.15 us (2%)
    all_to_all x5, blocking collectives, swap(): lax.all_to_all(x, 'tile', split_axis=0, concat_axis=0, tiled=True, axis_i...  105 us
    all_to_all x2, waiting for transfers between devices, swap(): lax.all_to_all(x, 'tile', split_axis=0, concat_axis=0, tiled=True, axis_i...  24.6 us
    pallas_call x1, Pallas kernels, attend_pair(): pl.pallas_call(pair_kernel, grid=(64 // srcs,), in_specs=[pl.BlockSpec((s...  11.9 us
    all_to_all x2, starting transfers between devices, swap(): lax.all_to_all(x, 'tile', split_axis=0, concat_axis=0, tiled=True, axis_i...  10.4 us
    pallas_call x1, Pallas kernels, stem(): pl.pallas_call(stem_kernel, in_specs=[vmem, vmem, vmem] + [hbm] * 5, out_...  7.94 us
    pallas_call x1, Pallas kernels, attend_single(): pl.pallas_call(single_kernel, grid=(64 // srcs,), in_specs=[pl.BlockSpec(...  7.18 us
    pallas_call x1, Pallas kernels, merge(): pl.pallas_call(merge_kernel, out_shape=(jax.ShapeDtypeStruct((64, 16, 128...  4.61 us
  transfers between devices with their start and end apart: 2, of which 2 were waited for; matrix products, arithmetic and copies ran while one was open for 0% of the time, Pallas kernels for 6%

profile of v5, /device:TPU:0, one launch (start us, length us, event | category | flops | bytes accessed | tf_op | source)
XLA Modules:
  0.0 189.3 jit_solution(6384484564866845320)
XLA Ops:
  0.6 3.0 %faces.1 = bf16[8,2,136,256]{3,2,1,0:T(8,128)(2,1)} custom-call(s32[2,8]{1,0:T(2,128)} %links_ref.1, bf16[2,32,32,256]{3,2,1,0:T(8,128)(2,1)} %features_hbm.3), custom_call_target="tpu_custom_call" | custom-call | tf_op jit(solution)/shard_map/faces/pallas_call | solution.py:102
  3.6 0.0 copy-start.6
  3.7 5.4 %all-to-all-start = ((bf16[8,2,136,256]{3,2,1,0:T(8,128)(2,1)}), bf16[8,2,136,256]{3,2,1,0:T(8,128)(2,1)S(1)}, u32[]{:S(2)}, u32[]{:S(2)}) async-start(bf16[8,2,136,256]{3,2,1,0:T(8,128)(2,1)} %faces.1), calls=%async_computation | async-start | bytes 2228224 | tf_op jit(solution)/shard_map/all_to_all | solution.py:62
  9.0 16.1 %all-to-all-done = bf16[8,2,136,256]{3,2,1,0:T(8,128)(2,1)S(1)} async-done(((bf16[8,2,136,256]{3,2,1,0:T(8,128)(2,1)}), bf16[8,2,136,256]{3,2,1,0:T(8,128)(2,1)S(1)}, u32[]{:S(2)}, u32[]{:S(2)}) %all-to-all-start) | async-done | bytes 1114144 | tf_op jit(solution)/shard_map/all_to_all | solution.py:62
  25.1 0.0 copy-start.9
  25.2 0.9 copy-done.9
  26.1 0.6 fusion.12.targets_ref
  26.7 3.7 %route.1 = bf16[16,136,256]{2,1,0:T(8,128)(2,1)} custom-call(s32[16,8]{1,0:T(8,128)} %fusion.12.targets_ref, bf16[16,136,256]{2,1,0:T(8,128)(2,1)} %bitcast.17), custom_call_target="tpu_custom_call" | custom-call | tf_op jit(solution)/shard_map/route/pallas_call | solution.py:149
  30.4 27.6 %all_to_all.35 = bf16[16,136,256]{2,1,0:T(8,128)(2,1)S(1)} all-to-all(bf16[16,136,256]{2,1,0:T(8,128)(2,1)} %route.1), channel_id=1, replica_groups={{0,6,24,30,96,102,120,126},{2,4,26,28,98,100,122,124},{8,14,16,22,104,1..., dimensions={0} | all-to-all | bytes 2228224 | tf_op jit(solution)/shard_map/all_to_all | solution.py:62
  58.0 0.0 copy-done.6
  58.0 0.0 copy-done.5
  58.0 0.0 copy-done.7
  58.0 0.0 copy-done.1
  58.1 0.0 copy-done.4
  58.1 7.9 %stem.1 = (bf16[128,768]{1,0:T(8,128)(2,1)S(1)}, bf16[64,96,128]{2,1,0:T(8,128)(2,1)}, bf16[64,96,128]{2,1,0:T(8,128)(2,1)}) custom-call(bf16[8,2,136,256]{3,2,1,0:T(8,128)(2,1)S(1)} %bitcast.13, bf16[9,256,256]{2,1,0:T(8,128)(2,1)S(1)} %bitcast.14, bf16[128,768]{1,0:T(8,128)(2,1)S(1)} %copy-done.7, bf16[2,32,32,256]{3,2,1,0:T(8,128)(2,1)S(1)} %copy-done.1, ...), custom_call_target="tpu_custom_call" | custom-call | tf_op jit(solution)/shard_map/stem/pallas_call | solution.py:522
  66.0 0.0 copy-start.8
  66.0 27.2 %all_to_all.36.in_ref.all_ref = bf16[64,96,128]{2,1,0:T(8,128)(2,1)S(1)} all-to-all(bf16[64,96,128]{2,1,0:T(8,128)(2,1)} %get-tuple-element.13), channel_id=1, replica_groups=mesh['tile'=64,'slide'=2] {'tile'}, dimensions={0} | all-to-all | bytes 3145728 | tf_op jit(solution)/shard_map/all_to_all | solution.py:62
  93.2 0.0 copy-done.8
  93.2 5.0 %all-to-all-start.3 = ((bf16[64,96,128]{2,1,0:T(8,128)(2,1)}), bf16[64,96,128]{2,1,0:T(8,128)(2,1)S(1)}, u32[]{:S(2)}, u32[]{:S(2)}) async-start(bf16[64,96,128]{2,1,0:T(8,128)(2,1)} %get-tuple-element.15), calls=%async_computation.3 | async-start | bytes 3145728 | tf_op jit(solution)/shard_map/all_to_all | solution.py:62
  98.3 11.9 %attend_pair.1.part_ref = bf16[4,512,256]{2,1,0:T(8,128)(2,1)S(1)} custom-call(bf16[64,96,128]{2,1,0:T(8,128)(2,1)S(1)} %all_to_all.36.in_ref.all_ref, bf16[64,96,128]{2,1,0:T(8,128)(2,1)S(1)} %all_to_all.36.in_ref.all_ref), custom_call_target="tpu_custom_call" | custom-call | tf_op jit(solution)/shard_map/attend_pair/pallas_call | solution.py:246
  110.2 0.0 copy-start.2
  110.2 1.0 copy-done.2
  111.2 8.6 %all-to-all-done.3.in_ref.all_ref.rest_ref = bf16[64,96,128]{2,1,0:T(8,128)(2,1)S(1)} async-done(((bf16[64,96,128]{2,1,0:T(8,128)(2,1)}), bf16[64,96,128]{2,1,0:T(8,128)(2,1)S(1)}, u32[]{:S(2)}, u32[]{:S(2)}) %all-to-all-start.3) | async-done | bytes 1572896 | tf_op jit(solution)/shard_map/all_to_all | solution.py:62
  119.8 1.2 copy-done.3
  121.0 7.2 %attend_single.1 = bf16[4,512,256]{2,1,0:T(8,128)(2,1)S(1)} custom-call(bf16[64,96,128]{2,1,0:T(8,128)(2,1)S(1)} %all-to-all-done.3.in_ref.all_ref.rest_ref, bf16[64,96,128]{2,1,0:T(8,128)(2,1)S(1)} %all-to-all-done.3.in_ref.all_ref.rest_ref, bf16[4,512,256]{2,1,0:T(8,128)(2,1)S(1)} %copy-done.3), custom_call_target="tpu_custom_call" | custom-call | tf_op jit(solution)/shard_map/attend_single/pallas_call | solution.py:268
  128.2 0.0 copy-done
  128.2 13.5 %all_to_all.37.parts_ref = bf16[4,512,256]{2,1,0:T(8,128)(2,1)} all-to-all(bf16[4,512,256]{2,1,0:T(8,128)(2,1)S(1)} %attend_single.1), channel_id=1, replica_groups={{0,8,32,40},{24,16,56,48},{96,104,64,72},{120,112,88,80},{2,10,34,42},{..., dimensions={0} | all-to-all | bytes 2097152 | tf_op jit(solution)/shard_map/all_to_all | solution.py:62
  141.7 4.6 %merge.1 = (bf16[64,16,128]{2,1,0:T(8,128)(2,1)}, bf16[6,192,128]{2,1,0:T(8,128)(2,1)}) custom-call(bf16[4,512,256]{2,1,0:T(8,128)(2,1)} %all_to_all.37.parts_ref, bf16[64,96,128]{2,1,0:T(8,128)(2,1)} %copy-done), custom_call_target="tpu_custom_call" | custom-call | tf_op jit(solution)/shard_map/merge/pallas_call | solution.py:325
  146.3 13.1 %all_to_all.38.terms_ref = bf16[16,72,128]{2,1,0:T(8,128)(2,1)} all-to-all(bf16[16,72,128]{2,1,0:T(8,128)(2,1)} %bitcast.18), channel_id=1, replica_groups={{0,8,32,40,24,16,56,48,96,104,64,72,120,112,88,80},{2,10,34,42,26,18,58..., dimensions={0} | all-to-all | bytes 589824 | tf_op jit(solution)/shard_map/all_to_all | solution.py:62
  159.4 2.2 %share.1 = bf16[64,88,128]{2,1,0:T(8,128)(2,1)} custom-call(bf16[16,72,128]{2,1,0:T(8,128)(2,1)} %all_to_all.38.terms_ref, bf16[64,16,128]{2,1,0:T(8,128)(2,1)} %get-tuple-element.18.att_ref), custom_call_target="tpu_custom_call" | custom-call | tf_op jit(solution)/shard_map/share/pallas_call | solution.py:347
  161.6 24.0 %all_to_all.39.all_ref = bf16[64,88,128]{2,1,0:T(8,128)(2,1)} all-to-all(bf16[64,88,128]{2,1,0:T(8,128)(2,1)} %share.1), channel_id=1, replica_groups=mesh['tile'=64,'slide'=2] {'tile'}, dimensions={0} | all-to-all | bytes 2883584 | tf_op jit(solution)/shard_map/all_to_all | solution.py:62
  185.7 3.7 %finish.1 = (bf16[128,768]{1,0:T(8,128)(2,1)}, f32[768,768]{1,0:T(8,128)}) custom-call(bf16[64,88,128]{2,1,0:T(8,128)(2,1)} %all_to_all.39.all_ref, bf16[128,768]{1,0:T(8,128)(2,1)} %copy-done.8, bf16[768,768]{1,0:T(8,128)(2,1)} %weight_ref.1), custom_call_target="tpu_custom_call" | custom-call | tf_op jit(solution)/shard_map/finish/pallas_call | solution.py:382
  (8 shorter events, 0.1 us)
Async XLA Ops:
  3.6 54.4 %copy-start.6 = (bf16[768,768]{1,0:T(8,128)(2,1)S(1)}, bf16[768,768]{1,0:T(8,128)(2,1)}, u32[]{:S(2)}) copy-start(bf16[768,768]{1,0:T(8,128)(2,1)} %key_hbm.1) | copy-start | bytes 3538948
  3.7 21.5 %all-to-all-start = ((bf16[8,2,136,256]{3,2,1,0:T(8,128)(2,1)}), bf16[8,2,136,256]{3,2,1,0:T(8,128)(2,1)S(1)}, u32[]{:S(2)}, u32[]{:S(2)}) async-start(bf16[8,2,136,256]{3,2,1,0:T(8,128)(2,1)} %faces.1), calls=%async_computation | async-start | bytes 2228224 | tf_op jit(solution)/shard_map/all_to_all | solution.py:62
  25.1 1.0 copy-start.9
  26.7 31.3 %copy-start.5 = (bf16[768,768]{1,0:T(8,128)(2,1)S(1)}, bf16[768,768]{1,0:T(8,128)(2,1)}, u32[]{:S(2)}) copy-start(bf16[768,768]{1,0:T(8,128)(2,1)} %query_hbm.1) | copy-start | bytes 3538948
  26.7 31.3 %copy-start.7 = (bf16[128,768]{1,0:T(8,128)(2,1)S(1)}, bf16[128,768]{1,0:T(8,128)(2,1)}, u32[]{:S(2)}) copy-start(bf16[128,768]{1,0:T(8,128)(2,1)} %cot_ref.1) | copy-start | bytes 589828
  30.4 27.6 %copy-start.1 = (bf16[2,32,32,256]{3,2,1,0:T(8,128)(2,1)S(1)}, bf16[2,32,32,256]{3,2,1,0:T(8,128)(2,1)}, u32[]{:S(2)}) copy-start(bf16[2,32,32,256]{3,2,1,0:T(8,128)(2,1)} %features_hbm.3) | copy-start | bytes 3145732
  30.4 27.6 %copy-start.4 = (bf16[3,3,256,256]{3,2,1,0:T(8,128)(2,1)S(1)}, bf16[3,3,256,256]{3,2,1,0:T(8,128)(2,1)}, u32[]{:S(2)}) copy-start(bf16[3,3,256,256]{3,2,1,0:T(8,128)(2,1)} %param.11) | copy-start | bytes 3538948
  66.0 27.2 %copy-start.8 = (bf16[128,768]{1,0:T(8,128)(2,1)}, bf16[128,768]{1,0:T(8,128)(2,1)S(1)}, u32[]{:S(2)}) copy-start(bf16[128,768]{1,0:T(8,128)(2,1)S(1)} %get-tuple-element.19.tokens_ref) | copy-start | bytes 589828
  93.2 26.5 %all-to-all-start.3 = ((bf16[64,96,128]{2,1,0:T(8,128)(2,1)}), bf16[64,96,128]{2,1,0:T(8,128)(2,1)S(1)}, u32[]{:S(2)}, u32[]{:S(2)}) async-start(bf16[64,96,128]{2,1,0:T(8,128)(2,1)} %get-tuple-element.15), calls=%async_computation.3 | async-start | bytes 3145728 | tf_op jit(solution)/shard_map/all_to_all | solution.py:62
  110.2 1.0 copy-start.2
  119.8 1.2 copy-start.3
  121.0 7.2 %copy-start = (bf16[64,96,128]{2,1,0:T(8,128)(2,1)}, bf16[64,96,128]{2,1,0:T(8,128)(2,1)S(1)}, u32[]{:S(2)}) copy-start(bf16[64,96,128]{2,1,0:T(8,128)(2,1)S(1)} %all-to-all-done.3.in_ref.all_ref.rest_ref) | copy-start | bytes 4718596

commit v6 on v5

--- a/solution.py
+++ b/solution.py
@@ -98,7 +98,7 @@
 
 
 def gather_faces(links, features):
-    hbm = pl.BlockSpec(memory_space=pl.ANY)
+    hbm = pl.BlockSpec(memory_space=pltpu.HBM)
     return pl.pallas_call(
         faces_kernel,
         in_specs=[pl.BlockSpec(memory_space=pltpu.SMEM), hbm],
@@ -110,6 +110,7 @@
             pltpu.VMEM((2, HALO, 256), BF),
             pltpu.SemaphoreType.DMA((8,)),
         ],
+        compiler_params=pltpu.CompilerParams(vmem_limit_bytes=6 << 20),
         name="faces",
     )(links, features)
 
@@ -151,6 +152,7 @@
         in_specs=[pl.BlockSpec(memory_space=pltpu.SMEM), vmem],
         out_specs=vmem,
         out_shape=jax.ShapeDtypeStruct((16, HALO, 256), BF),
+        compiler_params=pltpu.CompilerParams(vmem_limit_bytes=8 << 20),
         name="route",
     )(targets, faces)
 
@@ -251,13 +253,13 @@
             pl.BlockSpec((64, CHUNK, 128), lambda i: (0, 0, 0)),
         ],
         out_specs=pl.BlockSpec((SPLIT, srcs * 8, OW), lambda i: (0, i, 0)),
-        out_shape=jax.ShapeDtypeStruct((SPLIT, 512, OW), BF),
+        out_shape=pltpu.HBM((SPLIT, 512, OW), BF),
         scratch_shapes=[
             pltpu.VMEM((2, 2048, HD), BF),
             pltpu.VMEM((2, 2048, 2 * HD), BF),
             pltpu.VMEM((srcs * BLK, OW), F32),
         ],
-        compiler_params=pltpu.CompilerParams(vmem_limit_bytes=48 << 20),
+        compiler_params=pltpu.CompilerParams(vmem_limit_bytes=28 << 20),
         name="attend_pair",
     )(packed, packed)
 
@@ -280,7 +282,7 @@
             pltpu.VMEM((2048, 2 * HD), BF),
             pltpu.VMEM((srcs * BLK, 128), F32),
         ],
-        compiler_params=pltpu.CompilerParams(vmem_limit_bytes=48 << 20),
+        compiler_params=pltpu.CompilerParams(vmem_limit_bytes=20 << 20),
         name="attend_single",
     )(rest, rest, parts)
 
@@ -302,8 +304,9 @@
     low = lax.broadcasted_iota(jnp.int32, (512, 128), 1) < HD
     pair = jnp.zeros((512, 128), F32)
     single = jnp.zeros((512, 128), F32)
+    inverse = 1.0 / total
     for b in range(SPLIT):
-        share = ws[b] / total
+        share = ws[b] * inverse
         w0, w1, w2 = (share[:, HD + 3 * g : HD + 3 * g + 1] for g in range(HG))
         pair = pair + jnp.where(low, w0, w1) * parts_ref[b, :, :128].astype(F32)
         single = single + w2 * parts_ref[b, :, 128:].astype(F32)
@@ -329,38 +332,42 @@
             jax.ShapeDtypeStruct((DM // 128, GW, 128), BF),
         ),
         scratch_shapes=[pltpu.VMEM((512, 128), BF), pltpu.VMEM((512, 128), BF), pltpu.VMEM((512, DM), BF)],
+        compiler_params=pltpu.CompilerParams(vmem_limit_bytes=16 << 20),
         name="merge",
     )(parts, rest)
 
 
-def share_kernel(terms_ref, att_ref, out_ref):
-    total = terms_ref[0].astype(F32)
-    for n in range(1, 16):
-        total = total + terms_ref[n].astype(F32)
-    total = total.astype(BF)
-    for n in range(64):
-        out_ref[n, :SHARE, :] = total
+def share_kernel(terms_ref, att_ref, out_ref, total_ref):
+    @pl.when(pl.program_id(0) == 0)
+    def _():
+        total = terms_ref[0].astype(F32)
+        for n in range(1, 16):
+            total = total + terms_ref[n].astype(F32)
+        total_ref[...] = total.astype(BF)
+
+    for n in range(out_ref.shape[0]):
+        out_ref[n, :SHARE, :] = total_ref[...]
         out_ref[n, SHARE:, :] = att_ref[n]
 
 
 def share_out(terms, att):
-    return pl.pallas_call(
-        share_kernel, out_shape=jax.ShapeDtypeStruct((64, ROWS, 128), BF), name="share"
+    step = 16
+    return pl.pallas_call(
+        share_kernel,
+        grid=(64 // step,),
+        in_specs=[
+            pl.BlockSpec((16, SHARE, 128), lambda i: (0, 0, 0)),
+            pl.BlockSpec((step, 16, 128), lambda i: (i, 0, 0)),
+        ],
+        out_specs=pl.BlockSpec((step, ROWS, 128), lambda i: (i, 0, 0)),
+        out_shape=jax.ShapeDtypeStruct((64, ROWS, 128), BF),
+        scratch_shapes=[pltpu.VMEM((SHARE, 128), BF)],
+        compiler_params=pltpu.CompilerParams(vmem_limit_bytes=8 << 20),
+        name="share",
     )(terms, att)
 
 
-def finish_kernel(all_ref, tokens_ref, weight_ref, mixed_ref, grad_ref, att_ref):
-    lanes = lax.broadcasted_iota(jnp.int32, (8, 128), 1) < HD
-    for a in range(SPLIT):
-        for b in range(SPLIT):
-            row = a * BLK + b * 8
-            for h in range(SPLIT):
-                att_ref[row : row + 8, h * 128 : (h + 1) * 128] = all_ref[place(h, a, b), SHARE : SHARE + 8, :]
-            for h in range(0, SPLIT, 2):
-                even = all_ref[place(h, a, b), SHARE + 8 :, :].astype(F32)
-                odd = pltpu.roll(all_ref[place(h + 1, a, b), SHARE + 8 :, :].astype(F32), HD, 1)
-                first = 512 + h * HD
-                att_ref[row : row + 8, first : first + 128] = jnp.where(lanes, even, odd).astype(BF)
+def finish_kernel(all_ref, tokens_ref, weight_ref, mixed_ref, grad_hbm, att_ref, grad_ref, sems):
     for h in range(SPLIT):
         for m in range(16):
             at = place(h, m // SPLIT, m % SPLIT)
@@ -373,19 +380,46 @@
                     at, done : done + count, :
                 ].astype(F32)
                 done += count
+    copies = [
+        pltpu.make_async_copy(grad_ref.at[n * 384 : (n + 1) * 384], grad_hbm.at[n * 384 : (n + 1) * 384], sems.at[n])
+        for n in range(2)
+    ]
+    for copy in copies:
+        copy.start()
+    lanes = lax.broadcasted_iota(jnp.int32, (8, 128), 1) < HD
+    for a in range(SPLIT):
+        for b in range(SPLIT):
+            row = a * BLK + b * 8
+            for h in range(SPLIT):
+                att_ref[row : row + 8, h * 128 : (h + 1) * 128] = all_ref[place(h, a, b), SHARE : SHARE + 8, :]
+            for h in range(0, SPLIT, 2):
+                even = all_ref[place(h, a, b), SHARE + 8 :, :].astype(F32)
+                odd = pltpu.roll(all_ref[place(h + 1, a, b), SHARE + 8 :, :].astype(F32), HD, 1)
+                first = 512 + h * HD
+                att_ref[row : row + 8, first : first + 128] = jnp.where(lanes, even, odd).astype(BF)
     mixed_ref[...] = (
         tokens_ref[...].astype(F32) + jnp.dot(att_ref[...], weight_ref[...], preferred_element_type=F32)
     ).astype(BF)
+    for copy in copies:
+        copy.wait()
 
 
 def finish(received, tokens, weight):
+    vmem = pl.BlockSpec(memory_space=pltpu.VMEM)
     return pl.pallas_call(
         finish_kernel,
+        in_specs=[vmem] * 3,
+        out_specs=(vmem, pl.BlockSpec(memory_space=pl.ANY)),
         out_shape=(
             jax.ShapeDtypeStruct((128, DM), BF),
             jax.ShapeDtypeStruct((DM, DM), F32),
         ),
-        scratch_shapes=[pltpu.VMEM((128, DM), BF)],
+        scratch_shapes=[
+            pltpu.VMEM((128, DM), BF),
+            pltpu.VMEM((DM, DM), F32),
+            pltpu.SemaphoreType.DMA((2,)),
+        ],
+        compiler_params=pltpu.CompilerParams(vmem_limit_bytes=12 << 20),
         name="finish",
     )(received, tokens, weight)
 
@@ -521,7 +555,7 @@
     vmem = pl.BlockSpec(memory_space=pltpu.VMEM)
     return pl.pallas_call(
         stem_kernel,
-        in_specs=[vmem, vmem, vmem] + [hbm] * 5,
+        in_specs=[vmem, vmem, vmem, hbm, pl.BlockSpec(memory_space=pltpu.HBM)] + [hbm] * 3,
         out_specs=(vmem, vmem, vmem),
         out_shape=(
             jax.ShapeDtypeStruct((128, DM), BF),
@@ -541,9 +575,13 @@
             pltpu.VMEM((DM, DM), BF),
             pltpu.SemaphoreType.DMA((6,)),
         ],
-        compiler_params=pltpu.CompilerParams(vmem_limit_bytes=48 << 20),
+        compiler_params=pltpu.CompilerParams(vmem_limit_bytes=36 << 20),
         name="stem",
     )(halo, conv_weight, cotangent, features, patch_weight, query_weight, key_weight, value_weight)
+
+
+def in_hbm(x):
+    return pltpu.with_memory_space_constraint(x, pltpu.HBM)
 
 
 def local(
@@ -558,7 +596,7 @@
     cotangent,
 ):
     _, inner = split_device(lax.axis_index("tile"))
-    faces = swap(gather_faces(neighbours, features), INNER).reshape(16, HALO, 256)
+    faces = swap(gather_faces(neighbours, in_hbm(features)), INNER).reshape(16, HALO, 256)
     tiles = faces[:, 128, :8].astype(jnp.int32)
     outer, goal = split_device(tiles >> 1)
     targets = jnp.where((tiles < 128) & (goal == inner), (outer & 7) * 2 + (tiles & 1), -1)
@@ -566,12 +604,12 @@
     halo, conv_weight = lax.optimization_barrier((halo, conv_weight))
     taps = conv_weight.reshape(9, 256, 256)
     tokens, packed, rest = stem(
-        halo, taps, cotangent, features, patch_weight, query_weight, key_weight, value_weight
+        halo, taps, cotangent, features, in_hbm(patch_weight), query_weight, key_weight, value_weight
     )
     packed = swap(packed)
     packed, rest = lax.optimization_barrier((packed, rest))
     rest = swap(rest)
-    parts = swap(attend_single(rest, attend_pair(packed)), KEY_GROUPS)
+    parts = swap(attend_single(rest, in_hbm(attend_pair(packed))), KEY_GROUPS)
     att, grad = merge(parts, rest)
     terms = swap(grad.reshape(16, SHARE, 128), HEAD_GROUPS)
     received = swap(share_out(terms, att))

time: 190 us -> 178 us (0.937)
  Pallas kernels: 44.3 us -> 37.2 us
  local copies, waits for them, and re-layouts: 3.15 us -> 0.74 us
  blocking collectives: 105 us -> 103 us
    pallas_call x3, Pallas kernels: 13.9 us -> 9.48 us  [the longest x1 6.67 us: stem(): pl.pallas_call(stem_kernel, in_specs=[vmem, vmem, vmem, hbm, pl.BlockSpec...]
    pallas_call x1, Pallas kernels: 4.61 us -> 2.15 us  [merge(): pl.pallas_call(merge_kernel, out_shape=(jax.ShapeDtypeStruct((64, 16, 128...]
    unnamed x20 -> x22, local copies, waits for them, and re-layouts: 3.15 us -> 0.74 us
    all_to_all x5, blocking collectives: 105 us -> 103 us  [swap(): lax.all_to_all(x, 'tile', split_axis=0, concat_axis=0, tiled=True, axis_i...]
  transfers between devices with their start and end apart: 2 -> 2, of which waited for: 2 -> 2; matrix products, arithmetic and copies ran while one was open for 0% -> 0% of each run, Pallas kernels for 6% -> 7%
where the time goes in v6:
time: 178 us; the launch traced here: 177 us
  blocking collectives  103 us (58%)
  Pallas kernels  37.2 us (21%)
  waiting for transfers between devices  25.1 us (14%)
  starting transfers between devices  10.4 us (6%)
    all_to_all x5, blocking collectives, swap(): lax.all_to_all(x, 'tile', split_axis=0, concat_axis=0, tiled=True, axis_i...  103 us
    all_to_all x2, waiting for transfers between devices, swap(): lax.all_to_all(x, 'tile', split_axis=0, concat_axis=0, tiled=True, axis_i...  25.1 us
    pallas_call x1, Pallas kernels, attend_pair(): pl.pallas_call(pair_kernel, grid=(64 // srcs,), in_specs=[pl.BlockSpec((s...  12.6 us
    all_to_all x2, starting transfers between devices, swap(): lax.all_to_all(x, 'tile', split_axis=0, concat_axis=0, tiled=True, axis_i...  10.4 us
    pallas_call x1, Pallas kernels, attend_single(): pl.pallas_call(single_kernel, grid=(64 // srcs,), in_specs=[pl.BlockSpec(...  8.05 us
    pallas_call x1, Pallas kernels, stem(): pl.pallas_call(stem_kernel, in_specs=[vmem, vmem, vmem, hbm, pl.BlockSpec...  6.67 us
  transfers between devices with their start and end apart: 2, of which 2 were waited for; matrix products, arithmetic and copies ran while one was open for 0% of the time, Pallas kernels for 7%

profile of v6, /device:TPU:0, one launch (start us, length us, event | category | flops | bytes accessed | tf_op | source)
XLA Modules:
  0.0 177.5 jit_solution(13925781865148769338)
XLA Ops:
  0.6 0.0 copy-start.10
  0.6 0.7 copy-done.10
  1.3 2.9 %faces.1 = bf16[8,2,136,256]{3,2,1,0:T(8,128)(2,1)} custom-call(s32[2,8]{1,0:T(2,128)S(1)} %copy-done.10, bf16[2,32,32,256]{3,2,1,0:T(8,128)(2,1)} %features_hbm.3), custom_call_target="tpu_custom_call" | custom-call | tf_op jit(solution)/shard_map/faces/pallas_call | solution.py:102
  4.2 0.0 copy-start.4
  4.2 0.0 copy-start.5
  4.2 5.4 %all-to-all-start = ((bf16[8,2,136,256]{3,2,1,0:T(8,128)(2,1)}), bf16[8,2,136,256]{3,2,1,0:T(8,128)(2,1)S(1)}, u32[]{:S(2)}, u32[]{:S(2)}) async-start(bf16[8,2,136,256]{3,2,1,0:T(8,128)(2,1)} %faces.1), calls=%async_computation | async-start | bytes 2228224 | tf_op jit(solution)/shard_map/all_to_all | solution.py:62
  9.6 16.1 %all-to-all-done = bf16[8,2,136,256]{3,2,1,0:T(8,128)(2,1)S(1)} async-done(((bf16[8,2,136,256]{3,2,1,0:T(8,128)(2,1)}), bf16[8,2,136,256]{3,2,1,0:T(8,128)(2,1)S(1)}, u32[]{:S(2)}, u32[]{:S(2)}) %all-to-all-start) | async-done | bytes 1114144 | tf_op jit(solution)/shard_map/all_to_all | solution.py:62
  25.8 0.0 copy-start.3
  25.8 0.0 copy-start.7
  25.8 2.0 %route.1 = bf16[16,136,256]{2,1,0:T(8,128)(2,1)S(1)} custom-call(s32[16,8]{1,0:T(8,128)S(1)} %fusion.12.targets_ref, bf16[16,136,256]{2,1,0:T(8,128)(2,1)S(1)} %bitcast.15), custom_call_target="tpu_custom_call" | custom-call | tf_op jit(solution)/shard_map/route/pallas_call | solution.py:150
  27.8 0.0 copy-start
  27.8 0.0 copy-start.2
  27.8 27.4 %all_to_all.35 = bf16[16,136,256]{2,1,0:T(8,128)(2,1)S(1)} all-to-all(bf16[16,136,256]{2,1,0:T(8,128)(2,1)S(1)} %route.1), channel_id=1, replica_groups={{0,6,24,30,96,102,120,126},{2,4,26,28,98,100,122,124},{8,14,16,22,104,1..., dimensions={0} | all-to-all | bytes 2228224 | tf_op jit(solution)/shard_map/all_to_all | solution.py:62
  55.2 0.0 copy-done.4
  55.2 0.0 copy-done.5
  55.3 6.7 %stem.1 = (bf16[128,768]{1,0:T(8,128)(2,1)S(1)}, bf16[64,96,128]{2,1,0:T(8,128)(2,1)S(1)}, bf16[64,96,128]{2,1,0:T(8,128)(2,1)S(1)}) custom-call(bf16[8,2,136,256]{3,2,1,0:T(8,128)(2,1)S(1)} %bitcast.16, bf16[9,256,256]{2,1,0:T(8,128)(2,1)S(1)} %bitcast.17, bf16[128,768]{1,0:T(8,128)(2,1)S(1)} %copy-done.7, bf16[2,32,32,256]{3,2,1,0:T(8,128)(2,1)S(1)} %copy-done, ...), custom_call_target="tpu_custom_call" | custom-call | tf_op jit(solution)/shard_map/stem/pallas_call | solution.py:556
  61.9 0.0 copy-start.1
  61.9 0.0 copy-start.8
  62.0 26.5 %all_to_all.36.in_ref.all_ref = bf16[64,96,128]{2,1,0:T(8,128)(2,1)S(1)} all-to-all(bf16[64,96,128]{2,1,0:T(8,128)(2,1)S(1)} %get-tuple-element.13), channel_id=1, replica_groups=mesh['tile'=64,'slide'=2] {'tile'}, dimensions={0} | all-to-all | bytes 3145728 | tf_op jit(solution)/shard_map/all_to_all | solution.py:62
  88.5 0.0 copy-done.8
  88.5 5.0 %all-to-all-start.3 = ((bf16[64,96,128]{2,1,0:T(8,128)(2,1)}), bf16[64,96,128]{2,1,0:T(8,128)(2,1)S(1)}, u32[]{:S(2)}, u32[]{:S(2)}) async-start(bf16[64,96,128]{2,1,0:T(8,128)(2,1)} %copy-done.1), calls=%async_computation.3 | async-start | bytes 3145728 | tf_op jit(solution)/shard_map/all_to_all | solution.py:62
  93.5 12.6 %attend_pair.1.part_ref = bf16[4,512,256]{2,1,0:T(8,128)(2,1)} custom-call(bf16[64,96,128]{2,1,0:T(8,128)(2,1)S(1)} %all_to_all.36.in_ref.all_ref, bf16[64,96,128]{2,1,0:T(8,128)(2,1)S(1)} %all_to_all.36.in_ref.all_ref), custom_call_target="tpu_custom_call" | custom-call | tf_op jit(solution)/shard_map/attend_pair/pallas_call | solution.py:248
  106.1 9.0 %all-to-all-done.3.in_ref.all_ref.rest_ref = bf16[64,96,128]{2,1,0:T(8,128)(2,1)S(1)} async-done(((bf16[64,96,128]{2,1,0:T(8,128)(2,1)}), bf16[64,96,128]{2,1,0:T(8,128)(2,1)S(1)}, u32[]{:S(2)}, u32[]{:S(2)}) %all-to-all-start.3) | async-done | bytes 1572896 | tf_op jit(solution)/shard_map/all_to_all | solution.py:62
  115.1 8.1 %attend_single.1 = bf16[4,512,256]{2,1,0:T(8,128)(2,1)S(1)} custom-call(bf16[64,96,128]{2,1,0:T(8,128)(2,1)S(1)} %all-to-all-done.3.in_ref.all_ref.rest_ref, bf16[64,96,128]{2,1,0:T(8,128)(2,1)S(1)} %all-to-all-done.3.in_ref.all_ref.rest_ref, bf16[4,512,256]{2,1,0:T(8,128)(2,1)} %attend_pair.1.part_ref), custom_call_target="tpu_custom_call" | custom-call | tf_op jit(solution)/shard_map/attend_single/pallas_call | solution.py:270
  123.2 12.9 %all_to_all.37.parts_ref = bf16[4,512,256]{2,1,0:T(8,128)(2,1)S(1)} all-to-all(bf16[4,512,256]{2,1,0:T(8,128)(2,1)S(1)} %attend_single.1), channel_id=1, replica_groups={{0,8,32,40},{24,16,56,48},{96,104,64,72},{120,112,88,80},{2,10,34,42},{..., dimensions={0} | all-to-all | bytes 2097152 | tf_op jit(solution)/shard_map/all_to_all | solution.py:62
  136.1 2.2 %merge.1 = (bf16[64,16,128]{2,1,0:T(8,128)(2,1)S(1)}, bf16[6,192,128]{2,1,0:T(8,128)(2,1)S(1)}) custom-call(bf16[4,512,256]{2,1,0:T(8,128)(2,1)S(1)} %all_to_all.37.parts_ref, bf16[64,96,128]{2,1,0:T(8,128)(2,1)S(1)} %all-to-all-done.3.in_ref.all_ref.rest_ref), custom_call_target="tpu_custom_call" | custom-call | tf_op jit(solution)/shard_map/merge/pallas_call | solution.py:328
  138.3 11.5 %all_to_all.38.terms_ref = bf16[16,72,128]{2,1,0:T(8,128)(2,1)S(1)} all-to-all(bf16[16,72,128]{2,1,0:T(8,128)(2,1)S(1)} %bitcast.18), channel_id=1, replica_groups={{0,8,32,40,24,16,56,48,96,104,64,72,120,112,88,80},{2,10,34,42,26,18,58..., dimensions={0} | all-to-all | bytes 589824 | tf_op jit(solution)/shard_map/all_to_all | solution.py:62
  149.7 0.3 share.1
  150.0 0.0 copy-start.6
  150.0 0.0 copy-start.9
  150.1 24.7 %all_to_all.39.all_ref = bf16[64,88,128]{2,1,0:T(8,128)(2,1)S(1)} all-to-all(bf16[64,88,128]{2,1,0:T(8,128)(2,1)S(1)} %share.1), channel_id=1, replica_groups=mesh['tile'=64,'slide'=2] {'tile'}, dimensions={0} | all-to-all | bytes 2883584 | tf_op jit(solution)/shard_map/all_to_all | solution.py:62
  174.8 2.5 %finish.1 = (bf16[128,768]{1,0:T(8,128)(2,1)}, f32[768,768]{1,0:T(8,128)}) custom-call(bf16[64,88,128]{2,1,0:T(8,128)(2,1)S(1)} %all_to_all.39.all_ref, bf16[128,768]{1,0:T(8,128)(2,1)S(1)} %copy-done.9, bf16[768,768]{1,0:T(8,128)(2,1)S(1)} %copy-done.6), custom_call_target="tpu_custom_call" | custom-call | tf_op jit(solution)/shard_map/finish/pallas_call | solution.py:409
  (10 shorter events, 0.1 us)
Async XLA Ops:
  0.6 0.7 copy-start.10
  4.2 51.0 %copy-start.4 = (bf16[768,768]{1,0:T(8,128)(2,1)S(1)}, bf16[768,768]{1,0:T(8,128)(2,1)}, u32[]{:S(2)}) copy-start(bf16[768,768]{1,0:T(8,128)(2,1)} %key_hbm.1) | copy-start | bytes 3538948
  4.2 51.0 %copy-start.5 = (bf16[768,768]{1,0:T(8,128)(2,1)S(1)}, bf16[768,768]{1,0:T(8,128)(2,1)}, u32[]{:S(2)}) copy-start(bf16[768,768]{1,0:T(8,128)(2,1)} %value_hbm.1) | copy-start | bytes 3538948
  4.2 21.5 %all-to-all-start = ((bf16[8,2,136,256]{3,2,1,0:T(8,128)(2,1)}), bf16[8,2,136,256]{3,2,1,0:T(8,128)(2,1)S(1)}, u32[]{:S(2)}, u32[]{:S(2)}) async-start(bf16[8,2,136,256]{3,2,1,0:T(8,128)(2,1)} %faces.1), calls=%async_computation | async-start | bytes 2228224 | tf_op jit(solution)/shard_map/all_to_all | solution.py:62
  25.8 29.4 %copy-start.3 = (bf16[768,768]{1,0:T(8,128)(2,1)S(1)}, bf16[768,768]{1,0:T(8,128)(2,1)}, u32[]{:S(2)}) copy-start(bf16[768,768]{1,0:T(8,128)(2,1)} %query_hbm.1) | copy-start | bytes 3538948
  25.8 29.4 %copy-start.7 = (bf16[128,768]{1,0:T(8,128)(2,1)S(1)}, bf16[128,768]{1,0:T(8,128)(2,1)}, u32[]{:S(2)}) copy-start(bf16[128,768]{1,0:T(8,128)(2,1)} %cot_ref.1) | copy-start | bytes 589828
  27.8 27.5 %copy-start = (bf16[2,32,32,256]{3,2,1,0:T(8,128)(2,1)S(1)}, bf16[2,32,32,256]{3,2,1,0:T(8,128)(2,1)}, u32[]{:S(2)}) copy-start(bf16[2,32,32,256]{3,2,1,0:T(8,128)(2,1)} %features_hbm.3) | copy-start | bytes 3145732
  27.8 27.5 %copy-start.2 = (bf16[3,3,256,256]{3,2,1,0:T(8,128)(2,1)S(1)}, bf16[3,3,256,256]{3,2,1,0:T(8,128)(2,1)}, u32[]{:S(2)}) copy-start(bf16[3,3,256,256]{3,2,1,0:T(8,128)(2,1)} %param.11) | copy-start | bytes 3538948
  61.9 26.5 %copy-start.1 = (bf16[64,96,128]{2,1,0:T(8,128)(2,1)}, bf16[64,96,128]{2,1,0:T(8,128)(2,1)S(1)}, u32[]{:S(2)}) copy-start(bf16[64,96,128]{2,1,0:T(8,128)(2,1)S(1)} %get-tuple-element.15) | copy-start | bytes 4718596
  61.9 26.5 %copy-start.8 = (bf16[128,768]{1,0:T(8,128)(2,1)}, bf16[128,768]{1,0:T(8,128)(2,1)S(1)}, u32[]{:S(2)}) copy-start(bf16[128,768]{1,0:T(8,128)(2,1)S(1)} %get-tuple-element.19.tokens_ref) | copy-start | bytes 589828
  88.5 26.6 %all-to-all-start.3 = ((bf16[64,96,128]{2,1,0:T(8,128)(2,1)}), bf16[64,96,128]{2,1,0:T(8,128)(2,1)S(1)}, u32[]{:S(2)}, u32[]{:S(2)}) async-start(bf16[64,96,128]{2,1,0:T(8,128)(2,1)} %copy-done.1), calls=%async_computation.3 | async-start | bytes 3145728 | tf_op jit(solution)/shard_map/all_to_all | solution.py:62
  150.0 24.7 %copy-start.6 = (bf16[768,768]{1,0:T(8,128)(2,1)S(1)}, bf16[768,768]{1,0:T(8,128)(2,1)}, u32[]{:S(2)}) copy-start(bf16[768,768]{1,0:T(8,128)(2,1)} %weight_ref.1) | copy-start | bytes 3538948
  150.0 24.7 %copy-start.9 = (bf16[128,768]{1,0:T(8,128)(2,1)S(1)}, bf16[128,768]{1,0:T(8,128)(2,1)}, u32[]{:S(2)}) copy-start(bf16[128,768]{1,0:T(8,128)(2,1)} %copy-done.8) | copy-start | bytes 589828

commit v7 on v6

--- a/solution.py
+++ b/solution.py
@@ -64,7 +64,7 @@
     )
 
 
-def faces_kernel(links_ref, features_hbm, out_hbm, sides_ref, cols_ref, faces_ref, sems):
+def faces_kernel(links_ref, features_hbm, out_ref, sides_ref, cols_ref, faces_ref, sems):
     loads = []
     for t in range(2):
         for n, y in enumerate((0, 31)):
@@ -90,11 +90,8 @@
                 faces_ref[t, 64 + n * 32 : 96 + n * 32, lt * 128 : lt * 128 + 128] = cols_ref[
                     pl.ds(x, 32, stride=8), :
                 ].astype(BF)
-    stores = [pltpu.make_async_copy(faces_ref, out_hbm.at[n], sems.at[n]) for n in range(8)]
-    for store in stores:
-        store.start()
-    for store in stores:
-        store.wait()
+    for n in range(8):
+        out_ref[n] = faces_ref[...]
 
 
 def gather_faces(links, features):
@@ -102,7 +99,7 @@
     return pl.pallas_call(
         faces_kernel,
         in_specs=[pl.BlockSpec(memory_space=pltpu.SMEM), hbm],
-        out_specs=hbm,
+        out_specs=pl.BlockSpec(memory_space=pltpu.VMEM),
         out_shape=jax.ShapeDtypeStruct((8, 2, HALO, 256), BF),
         scratch_shapes=[
             pltpu.VMEM((2, 2, 32, 8, 256), BF),
@@ -244,7 +241,7 @@
 
 
 def attend_pair(packed):
-    srcs = 16
+    srcs = 32
     return pl.pallas_call(
         pair_kernel,
         grid=(64 // srcs,),
@@ -259,13 +256,13 @@
             pltpu.VMEM((2, 2048, 2 * HD), BF),
             pltpu.VMEM((srcs * BLK, OW), F32),
         ],
-        compiler_params=pltpu.CompilerParams(vmem_limit_bytes=28 << 20),
+        compiler_params=pltpu.CompilerParams(vmem_limit_bytes=38 << 20),
         name="attend_pair",
     )(packed, packed)
 
 
 def attend_single(rest, parts):
-    srcs = 16
+    srcs = 64
     block = pl.BlockSpec((SPLIT, srcs * 8, OW), lambda i: (0, i, 0))
     return pl.pallas_call(
         single_kernel,
@@ -282,7 +279,7 @@
             pltpu.VMEM((2048, 2 * HD), BF),
             pltpu.VMEM((srcs * BLK, 128), F32),
         ],
-        compiler_params=pltpu.CompilerParams(vmem_limit_bytes=20 << 20),
+        compiler_params=pltpu.CompilerParams(vmem_limit_bytes=38 << 20),
         name="attend_single",
     )(rest, rest, parts)
 
@@ -428,11 +425,60 @@
 Z0 = 8
 
 
+def conv_kernel(features_ref, conv_ref, out_ref, left_ref, right_ref):
+    for t in range(2):
+        for y in range(32):
+            for lt in range(2):
+                slot = (t * 32 + y) * ZW
+                left_ref[lt, slot : slot + Z0, :] = jnp.zeros((Z0, 128), F32)
+                right_ref[lt, slot + Z0 + 32 : slot + ZW, :] = jnp.zeros((Z0, 128), F32)
+        for y in range(0, 32, 8):
+            zero = jnp.zeros((32, 256), BF)
+            accs = []
+            for dx in range(3):
+                acc = jnp.zeros((256, 256), F32)
+                for dy in range(3):
+                    first = y + dy - 1
+                    if first < 0:
+                        rows = jnp.concatenate([zero, features_ref[t, :7].reshape(224, 256)], axis=0)
+                    elif first + 8 > 32:
+                        rows = jnp.concatenate([features_ref[t, first:].reshape(224, 256), zero], axis=0)
+                    else:
+                        rows = features_ref[t, first : first + 8].reshape(256, 256)
+                    acc = acc + jnp.dot(rows, conv_ref[dy * 3 + dx], preferred_element_type=F32)
+                accs.append(acc)
+            for n in range(8):
+                slot = (t * 32 + y + n) * ZW + Z0
+                row = (t * 32 + y + n) * 32
+                for lt in range(2):
+                    part = (slice(n * 32, n * 32 + 32), slice(lt * 128, lt * 128 + 128))
+                    left_ref[lt, slot : slot + 32, :] = accs[0][part]
+                    right_ref[lt, slot : slot + 32, :] = accs[2][part]
+                    out_ref[lt, row : row + 32, :] = (
+                        accs[1][part]
+                        + left_ref[lt, slot - 1 : slot + 31, :]
+                        + right_ref[lt, slot + 1 : slot + 33, :]
+                    )
+
+
+def conv_inside(features, taps):
+    vmem = pl.BlockSpec(memory_space=pltpu.VMEM)
+    return pl.pallas_call(
+        conv_kernel,
+        in_specs=[vmem, vmem],
+        out_specs=vmem,
+        out_shape=jax.ShapeDtypeStruct((2, 2048, 128), F32),
+        scratch_shapes=[pltpu.VMEM((2, 64 * ZW, 128), F32), pltpu.VMEM((2, 64 * ZW, 128), F32)],
+        compiler_params=pltpu.CompilerParams(vmem_limit_bytes=16 << 20),
+        name="conv_inside",
+    )(features, taps)
+
+
 def stem_kernel(
     halo_ref,
     conv_ref,
     cot_ref,
-    features_hbm,
+    inside_ref,
     patch_hbm,
     query_hbm,
     key_hbm,
@@ -440,11 +486,8 @@
     tokens_ref,
     packed_ref,
     rest_ref,
-    maps_ref,
     side_ref,
-    left_ref,
-    mid_ref,
-    right_ref,
+    edge_ref,
     hid_ref,
     patch_ref,
     wq_ref,
@@ -452,12 +495,10 @@
     wv_ref,
     sems,
 ):
-    loads = [pltpu.make_async_copy(features_hbm.at[t], maps_ref.at[t, 1:33], sems.at[t]) for t in range(2)]
     pairs = ((patch_hbm, patch_ref), (query_hbm, wq_ref), (key_hbm, wk_ref), (value_hbm, wv_ref))
-    loads += [pltpu.make_async_copy(src, dst, sems.at[2 + n]) for n, (src, dst) in enumerate(pairs)]
+    loads = [pltpu.make_async_copy(src, dst, sems.at[n]) for n, (src, dst) in enumerate(pairs)]
     for load in loads:
         load.start()
-    zrefs = (left_ref, mid_ref, right_ref)
 
     def halo_rows(t, first, count):
         total = halo_ref[0, t, first : first + count, :].astype(F32)
@@ -466,53 +507,49 @@
         return total
 
     for t in range(2):
-        maps_ref[t, 0] = halo_rows(t, 0, 32).astype(BF)
-        maps_ref[t, 33] = halo_rows(t, 32, 32).astype(BF)
         corner = halo_rows(t, 128, 8)
-        for side in range(2):
-            side_ref[side, t, Z0 : Z0 + 32, :] = halo_rows(t, 64 + 32 * side, 32)
-            side_ref[side, t, Z0 - 1 : Z0, :] = corner[side : side + 1]
-            side_ref[side, t, Z0 + 32 : Z0 + 33, :] = corner[2 + side : 3 + side]
-    for t in range(2):
-        for side in range(2):
-            edge = jnp.zeros((32, 256), F32)
-            for dy in range(3):
-                part = side_ref[side, t, Z0 - 1 + dy : Z0 + 31 + dy, :].astype(BF)
-                edge = edge + jnp.dot(part, conv_ref[dy * 3 + side * 2], preferred_element_type=F32)
-            dest, first = ((left_ref, Z0 - 1), (right_ref, Z0 + 32))[side]
-            for lt in range(2):
-                dest[lt, pl.ds(t * 32 * ZW + first, 32, stride=ZW), :] = edge[:, lt * 128 : lt * 128 + 128]
-    for t in range(2):
-        loads[t].wait()
-        for y in range(0, 32, 8):
-            for dx in range(3):
-                acc = jnp.zeros((256, 256), F32)
-                for dy in range(3):
-                    rows = maps_ref[t, y + dy : y + dy + 8].reshape(256, 256)
-                    acc = acc + jnp.dot(rows, conv_ref[dy * 3 + dx], preferred_element_type=F32)
-                for n in range(8):
-                    first = (t * 32 + y + n) * ZW + Z0
-                    for lt in range(2):
-                        zrefs[dx][lt, first : first + 32, :] = acc[n * 32 : n * 32 + 32, lt * 128 : lt * 128 + 128]
-
+        for side in range(4):
+            side_ref[side, t, Z0 : Z0 + 32, :] = halo_rows(t, 32 * side, 32)
+            for end, row in enumerate((Z0 - 1, Z0 + 32)):
+                if side < 2:
+                    cell = corner[side * 2 + end : side * 2 + end + 1]
+                else:
+                    cell = jnp.zeros((1, 256), F32)
+                side_ref[side, t, row : row + 1, :] = cell
+    for side in range(4):
+        edge = jnp.zeros((64, 256), F32)
+        for k in range(3):
+            part = jnp.concatenate(
+                [side_ref[side, t, Z0 - 1 + k : Z0 + 31 + k, :].astype(BF) for t in range(2)], axis=0
+            )
+            tap = (k, 6 + k, 3 * k, 3 * k + 2)[side]
+            edge = edge + jnp.dot(part, conv_ref[tap], preferred_element_type=F32)
+        for lt in range(2):
+            edge_ref[lt, side * 64 : side * 64 + 64, :] = edge[:, lt * 128 : lt * 128 + 128]
+
+    sub = lax.broadcasted_iota(jnp.int32, (8, 128), 0)
     for r in range(4):
         for c in range(4):
             for t in range(2):
                 for pr in range(8):
-                    first = (t * 32 + pr * 4 + r) * ZW + Z0 + c
+                    y = pr * 4 + r
                     row = (t * 8 + pr) * 8
                     for lt in range(2):
-                        total = (
-                            mid_ref[lt, pl.ds(first, 8, stride=4), :]
-                            + left_ref[lt, pl.ds(first - 1, 8, stride=4), :]
-                            + right_ref[lt, pl.ds(first + 1, 8, stride=4), :]
-                        )
+                        total = inside_ref[lt, pl.ds((t * 32 + y) * 32 + c, 8, stride=4), :]
+                        if y == 0:
+                            total = total + edge_ref[lt, pl.ds(t * 32 + c, 8, stride=4), :]
+                        if y == 31:
+                            total = total + edge_ref[lt, pl.ds(64 + t * 32 + c, 8, stride=4), :]
+                        if c == 0 or c == 3:
+                            at = (128 if c == 0 else 192) + t * 32 + y
+                            cell = jnp.broadcast_to(edge_ref[lt, at : at + 1, :], (8, 128))
+                            total = total + jnp.where(sub == (0 if c == 0 else 7), cell, 0.0)
                         col = (r * 4 + c) * 256 + lt * 128
                         hid_ref[row : row + 8, col : col + 128] = jax.nn.gelu(total).astype(BF)
-    loads[2].wait()
+    loads[0].wait()
     tokens = jnp.dot(hid_ref[...], patch_ref[...], preferred_element_type=F32).astype(BF)
     tokens_ref[...] = tokens
-    for load in loads[3:]:
+    for load in loads[1:]:
         load.wait()
     query = jnp.dot(tokens, wq_ref[...], preferred_element_type=F32)
     keys = jnp.dot(tokens, wk_ref[...], preferred_element_type=F32)
@@ -550,12 +587,12 @@
                     rest_ref[at, 48 + 8 * c : 56 + 8 * c, :] = cot_ref[row : row + 8, c * 128 : (c + 1) * 128]
 
 
-def stem(halo, conv_weight, cotangent, features, patch_weight, query_weight, key_weight, value_weight):
+def stem(halo, conv_weight, cotangent, inside, patch_weight, query_weight, key_weight, value_weight):
     hbm = pl.BlockSpec(memory_space=pl.ANY)
     vmem = pl.BlockSpec(memory_space=pltpu.VMEM)
     return pl.pallas_call(
         stem_kernel,
-        in_specs=[vmem, vmem, vmem, hbm, pl.BlockSpec(memory_space=pltpu.HBM)] + [hbm] * 3,
+        in_specs=[vmem] * 4 + [hbm] * 4,
         out_specs=(vmem, vmem, vmem),
         out_shape=(
             jax.ShapeDtypeStruct((128, DM), BF),
@@ -563,21 +600,18 @@
             jax.ShapeDtypeStruct((64, CHUNK, 128), BF),
         ),
         scratch_shapes=[
-            pltpu.VMEM((2, 34, 32, 256), BF),
-            pltpu.VMEM((2, 2, ZW, 256), F32),
-            pltpu.VMEM((2, 64 * ZW, 128), F32),
-            pltpu.VMEM((2, 64 * ZW, 128), F32),
-            pltpu.VMEM((2, 64 * ZW, 128), F32),
+            pltpu.VMEM((4, 2, ZW, 256), F32),
+            pltpu.VMEM((2, 256, 128), F32),
             pltpu.VMEM((128, 4096), BF),
             pltpu.VMEM((4096, DM), BF),
             pltpu.VMEM((DM, DM), BF),
             pltpu.VMEM((DM, DM), BF),
             pltpu.VMEM((DM, DM), BF),
-            pltpu.SemaphoreType.DMA((6,)),
-        ],
-        compiler_params=pltpu.CompilerParams(vmem_limit_bytes=36 << 20),
+            pltpu.SemaphoreType.DMA((4,)),
+        ],
+        compiler_params=pltpu.CompilerParams(vmem_limit_bytes=28 << 20),
         name="stem",
-    )(halo, conv_weight, cotangent, features, patch_weight, query_weight, key_weight, value_weight)
+    )(halo, conv_weight, cotangent, inside, patch_weight, query_weight, key_weight, value_weight)
 
 
 def in_hbm(x):
@@ -596,15 +630,24 @@
     cotangent,
 ):
     _, inner = split_device(lax.axis_index("tile"))
-    faces = swap(gather_faces(neighbours, in_hbm(features)), INNER).reshape(16, HALO, 256)
+    faces = gather_faces(neighbours, in_hbm(features))
+    faces, inner = lax.optimization_barrier((faces, inner))
+    faces = swap(faces, INNER).reshape(16, HALO, 256)
     tiles = faces[:, 128, :8].astype(jnp.int32)
     outer, goal = split_device(tiles >> 1)
     targets = jnp.where((tiles < 128) & (goal == inner), (outer & 7) * 2 + (tiles & 1), -1)
-    halo = swap(route(targets, faces), OUTER).reshape(8, 2, HALO, 256)
-    halo, conv_weight = lax.optimization_barrier((halo, conv_weight))
-    taps = conv_weight.reshape(9, 256, 256)
+    routed, taps = lax.optimization_barrier((route(targets, faces), conv_weight.reshape(9, 256, 256)))
+    halo = swap(routed, OUTER).reshape(8, 2, HALO, 256)
+    inside = conv_inside(features, taps)
     tokens, packed, rest = stem(
-        halo, taps, cotangent, features, in_hbm(patch_weight), query_weight, key_weight, value_weight
+        halo,
+        taps,
+        cotangent,
+        inside,
+        in_hbm(patch_weight),
+        in_hbm(query_weight),
+        in_hbm(key_weight),
+        in_hbm(value_weight),
     )
     packed = swap(packed)
     packed, rest = lax.optimization_barrier((packed, rest))

time: 178 us -> 177 us (level)
  blocking collectives: 103 us -> 97.3 us
  starting transfers between devices: 10.4 us -> 13 us
    all_to_all x5, blocking collectives: 103 us -> 97.3 us  [swap(): lax.all_to_all(x, 'tile', split_axis=0, concat_axis=0, tiled=True, axis_i...]
    all_to_all x2, starting transfers between devices: 10.4 us -> 13 us  [swap(): lax.all_to_all(x, 'tile', split_axis=0, concat_axis=0, tiled=True, axis_i...]
    pallas_call x1 -> x2, Pallas kernels: 6.67 us -> 9.24 us  [the longest x1 6.38 us: stem(): pl.pallas_call(stem_kernel, in_specs=[vmem] * 4 + [hbm] * 4, out_specs=(v...]
  transfers between devices with their start and end apart: 2 -> 2, of which waited for: 2 -> 2; matrix products, arithmetic and copies ran while one was open for 0% -> 0% of each run, Pallas kernels for 7% -> 8%
where the time goes in v7:
time: 177 us; the launch traced here: 176 us
  blocking collectives  97.3 us (55%)
  Pallas kernels  38.1 us (22%)
  waiting for transfers between devices  25.1 us (14%)
  starting transfers between devices  13 us (7%)
  local copies, waits for them, and re-layouts  1.92 us (1%)
    all_to_all x5, blocking collectives, swap(): lax.all_to_all(x, 'tile', split_axis=0, concat_axis=0, tiled=True, axis_i...  97.3 us
    all_to_all x2, waiting for transfers between devices, swap(): lax.all_to_all(x, 'tile', split_axis=0, concat_axis=0, tiled=True, axis_i...  25.1 us
    all_to_all x2, starting transfers between devices, swap(): lax.all_to_all(x, 'tile', split_axis=0, concat_axis=0, tiled=True, axis_i...  13 us
    pallas_call x1, Pallas kernels, attend_pair(): pl.pallas_call(pair_kernel, grid=(64 // srcs,), in_specs=[pl.BlockSpec((s...  11.9 us
    pallas_call x1, Pallas kernels, attend_single(): pl.pallas_call(single_kernel, grid=(64 // srcs,), in_specs=[pl.BlockSpec(...  7 us
    pallas_call x1, Pallas kernels, stem(): pl.pallas_call(stem_kernel, in_specs=[vmem] * 4 + [hbm] * 4, out_specs=(v...  6.38 us
  transfers between devices with their start and end apart: 2, of which 2 were waited for; matrix products, arithmetic and copies ran while one was open for 0% of the time, Pallas kernels for 8%

profile of v7, /device:TPU:0, one launch (start us, length us, event | category | flops | bytes accessed | tf_op | source)
XLA Modules:
  0.0 176.4 jit_solution(17646944973090311430)
XLA Ops:
  0.6 0.0 copy-start.7
  0.7 0.7 copy-done.7
  1.3 2.0 %faces.1 = bf16[8,2,136,256]{3,2,1,0:T(8,128)(2,1)S(1)} custom-call(s32[2,8]{1,0:T(2,128)S(1)} %copy-done.7, bf16[2,32,32,256]{3,2,1,0:T(8,128)(2,1)} %features_ref.1), custom_call_target="tpu_custom_call" | custom-call | tf_op jit(solution)/shard_map/faces/pallas_call | solution.py:99
  3.3 21.2 %all_to_all.35 = bf16[8,2,136,256]{3,2,1,0:T(8,128)(2,1)S(1)} all-to-all(bf16[8,2,136,256]{3,2,1,0:T(8,128)(2,1)S(1)} %faces.1), channel_id=1, replica_groups={{0,2,8,10,32,34,40,42},{6,4,14,12,38,36,46,44},{24,26,16,18,56,58,48,50..., dimensions={0} | all-to-all | bytes 2228224 | tf_op jit(solution)/shard_map/all_to_all | solution.py:62
  24.6 3.0 %route.1 = bf16[16,136,256]{2,1,0:T(8,128)(2,1)} custom-call(s32[16,8]{1,0:T(8,128)S(1)} %fusion.12.targets_ref, bf16[16,136,256]{2,1,0:T(8,128)(2,1)S(1)} %bitcast.17), custom_call_target="tpu_custom_call" | custom-call | tf_op jit(solution)/shard_map/route/pallas_call | solution.py:147
  27.6 7.8 %all-to-all-start.1 = ((bf16[16,136,256]{2,1,0:T(8,128)(2,1)}), bf16[16,136,256]{2,1,0:T(8,128)(2,1)}, u32[]{:S(2)}, u32[]{:S(2)}) async-start(bf16[16,136,256]{2,1,0:T(8,128)(2,1)} %route.1), calls=%async_computation.1 | async-start | bytes 2228224 | tf_op jit(solution)/shard_map/all_to_all | solution.py:62
  35.3 0.0 copy-done
  35.3 0.0 copy-start.1
  35.3 1.2 copy-done.1
  36.6 2.9 %conv_inside.1.inside_ref = f32[2,2048,128]{2,1,0:T(8,128)S(1)} custom-call(bf16[2,32,32,256]{3,2,1,0:T(8,128)(2,1)S(1)} %copy-done.1, bf16[9,256,256]{2,1,0:T(8,128)(2,1)S(1)} %bitcast.13), custom_call_target="tpu_custom_call" | custom-call | tf_op jit(solution)/shard_map/conv_inside/pallas_call | solution.py:466
  39.4 14.6 %all-to-all-done.1 = bf16[16,136,256]{2,1,0:T(8,128)(2,1)} async-done(((bf16[16,136,256]{2,1,0:T(8,128)(2,1)}), bf16[16,136,256]{2,1,0:T(8,128)(2,1)}, u32[]{:S(2)}, u32[]{:S(2)}) %all-to-all-start.1) | async-done | bytes 1114144 | tf_op jit(solution)/shard_map/all_to_all | solution.py:62
  54.0 0.0 copy-done.4
  54.0 6.4 %stem.1 = (bf16[128,768]{1,0:T(8,128)(2,1)S(1)}, bf16[64,96,128]{2,1,0:T(8,128)(2,1)S(1)}, bf16[64,96,128]{2,1,0:T(8,128)(2,1)S(1)}) custom-call(bf16[8,2,136,256]{3,2,1,0:T(8,128)(2,1)} %bitcast.8.halo_ref, bf16[9,256,256]{2,1,0:T(8,128)(2,1)S(1)} %bitcast.14, bf16[128,768]{1,0:T(8,128)(2,1)S(1)} %copy-done.4, f32[2,2048,128]{2,1,0:T(8,128)S(1)} %conv_inside.1.inside_ref, ...), custom_call_target="tpu_custom_call" | custom-call | tf_op jit(solution)/shard_map/stem/pallas_call | solution.py:593
  60.4 0.0 copy-start.2
  60.4 0.0 copy-start.5
  60.4 27.3 %all_to_all.36.in_ref.all_ref = bf16[64,96,128]{2,1,0:T(8,128)(2,1)S(1)} all-to-all(bf16[64,96,128]{2,1,0:T(8,128)(2,1)S(1)} %get-tuple-element.17), channel_id=1, replica_groups=mesh['tile'=64,'slide'=2] {'tile'}, dimensions={0} | all-to-all | bytes 3145728 | tf_op jit(solution)/shard_map/all_to_all | solution.py:62
  87.7 0.0 copy-done.2
  87.7 0.0 copy-done.5
  87.7 5.2 %all-to-all-start.3 = ((bf16[64,96,128]{2,1,0:T(8,128)(2,1)}), bf16[64,96,128]{2,1,0:T(8,128)(2,1)S(1)}, u32[]{:S(2)}, u32[]{:S(2)}) async-start(bf16[64,96,128]{2,1,0:T(8,128)(2,1)} %copy-done.2), calls=%async_computation.3 | async-start | bytes 3145728 | tf_op jit(solution)/shard_map/all_to_all | solution.py:62
  92.9 11.9 %attend_pair.1.part_ref = bf16[4,512,256]{2,1,0:T(8,128)(2,1)} custom-call(bf16[64,96,128]{2,1,0:T(8,128)(2,1)S(1)} %all_to_all.36.in_ref.all_ref, bf16[64,96,128]{2,1,0:T(8,128)(2,1)S(1)} %all_to_all.36.in_ref.all_ref), custom_call_target="tpu_custom_call" | custom-call | tf_op jit(solution)/shard_map/attend_pair/pallas_call | solution.py:245
  104.9 10.5 %all-to-all-done.3.in_ref.all_ref.rest_ref = bf16[64,96,128]{2,1,0:T(8,128)(2,1)S(1)} async-done(((bf16[64,96,128]{2,1,0:T(8,128)(2,1)}), bf16[64,96,128]{2,1,0:T(8,128)(2,1)S(1)}, u32[]{:S(2)}, u32[]{:S(2)}) %all-to-all-start.3) | async-done | bytes 1572896 | tf_op jit(solution)/shard_map/all_to_all | solution.py:62
  115.4 7.0 %attend_single.1 = bf16[4,512,256]{2,1,0:T(8,128)(2,1)S(1)} custom-call(bf16[64,96,128]{2,1,0:T(8,128)(2,1)S(1)} %all-to-all-done.3.in_ref.all_ref.rest_ref, bf16[64,96,128]{2,1,0:T(8,128)(2,1)S(1)} %all-to-all-done.3.in_ref.all_ref.rest_ref, bf16[4,512,256]{2,1,0:T(8,128)(2,1)} %attend_pair.1.part_ref), custom_call_target="tpu_custom_call" | custom-call | tf_op jit(solution)/shard_map/attend_single/pallas_call | solution.py:267
  122.4 13.8 %all_to_all.37.parts_ref = bf16[4,512,256]{2,1,0:T(8,128)(2,1)S(1)} all-to-all(bf16[4,512,256]{2,1,0:T(8,128)(2,1)S(1)} %attend_single.1), channel_id=1, replica_groups={{0,8,32,40},{24,16,56,48},{96,104,64,72},{120,112,88,80},{2,10,34,42},{..., dimensions={0} | all-to-all | bytes 2097152 | tf_op jit(solution)/shard_map/all_to_all | solution.py:62
  136.2 2.2 %merge.1 = (bf16[64,16,128]{2,1,0:T(8,128)(2,1)S(1)}, bf16[6,192,128]{2,1,0:T(8,128)(2,1)S(1)}) custom-call(bf16[4,512,256]{2,1,0:T(8,128)(2,1)S(1)} %all_to_all.37.parts_ref, bf16[64,96,128]{2,1,0:T(8,128)(2,1)S(1)} %all-to-all-done.3.in_ref.all_ref.rest_ref), custom_call_target="tpu_custom_call" | custom-call | tf_op jit(solution)/shard_map/merge/pallas_call | solution.py:325
  138.4 11.5 %all_to_all.38.terms_ref = bf16[16,72,128]{2,1,0:T(8,128)(2,1)S(1)} all-to-all(bf16[16,72,128]{2,1,0:T(8,128)(2,1)S(1)} %bitcast.18), channel_id=1, replica_groups={{0,8,32,40,24,16,56,48,96,104,64,72,120,112,88,80},{2,10,34,42,26,18,58..., dimensions={0} | all-to-all | bytes 589824 | tf_op jit(solution)/shard_map/all_to_all | solution.py:62
  149.8 0.3 share.1
  150.1 0.0 copy-start.3
  150.1 0.0 copy-start.6
  150.2 23.6 %all_to_all.39.all_ref = bf16[64,88,128]{2,1,0:T(8,128)(2,1)S(1)} all-to-all(bf16[64,88,128]{2,1,0:T(8,128)(2,1)S(1)} %share.1), channel_id=1, replica_groups=mesh['tile'=64,'slide'=2] {'tile'}, dimensions={0} | all-to-all | bytes 2883584 | tf_op jit(solution)/shard_map/all_to_all | solution.py:62
  173.7 0.0 copy-done.3
  173.7 0.0 copy-done.6
  173.7 2.5 %finish.1 = (bf16[128,768]{1,0:T(8,128)(2,1)}, f32[768,768]{1,0:T(8,128)}) custom-call(bf16[64,88,128]{2,1,0:T(8,128)(2,1)S(1)} %all_to_all.39.all_ref, bf16[128,768]{1,0:T(8,128)(2,1)S(1)} %copy-done.6, bf16[768,768]{1,0:T(8,128)(2,1)S(1)} %copy-done.3), custom_call_target="tpu_custom_call" | custom-call | tf_op jit(solution)/shard_map/finish/pallas_call | solution.py:406
  (5 shorter events, 0.1 us)
Async XLA Ops:
  0.6 0.7 copy-start.7
  27.6 7.8 %copy-start = (bf16[3,3,256,256]{3,2,1,0:T(8,128)(2,1)S(1)}, bf16[3,3,256,256]{3,2,1,0:T(8,128)(2,1)}, u32[]{:S(2)}) copy-start(bf16[3,3,256,256]{3,2,1,0:T(8,128)(2,1)} %param.11) | copy-start | bytes 3538948
  27.6 26.4 %all-to-all-start.1 = ((bf16[16,136,256]{2,1,0:T(8,128)(2,1)}), bf16[16,136,256]{2,1,0:T(8,128)(2,1)}, u32[]{:S(2)}, u32[]{:S(2)}) async-start(bf16[16,136,256]{2,1,0:T(8,128)(2,1)} %route.1), calls=%async_computation.1 | async-start | bytes 2228224 | tf_op jit(solution)/shard_map/all_to_all | solution.py:62
  35.3 1.2 copy-start.1
  36.6 17.5 %copy-start.4 = (bf16[128,768]{1,0:T(8,128)(2,1)S(1)}, bf16[128,768]{1,0:T(8,128)(2,1)}, u32[]{:S(2)}) copy-start(bf16[128,768]{1,0:T(8,128)(2,1)} %cot_ref.1) | copy-start | bytes 589828
  60.4 27.3 %copy-start.2 = (bf16[64,96,128]{2,1,0:T(8,128)(2,1)}, bf16[64,96,128]{2,1,0:T(8,128)(2,1)S(1)}, u32[]{:S(2)}) copy-start(bf16[64,96,128]{2,1,0:T(8,128)(2,1)S(1)} %get-tuple-element.19) | copy-start | bytes 4718596
  60.4 27.3 %copy-start.5 = (bf16[128,768]{1,0:T(8,128)(2,1)}, bf16[128,768]{1,0:T(8,128)(2,1)S(1)}, u32[]{:S(2)}) copy-start(bf16[128,768]{1,0:T(8,128)(2,1)S(1)} %get-tuple-element.23.tokens_ref) | copy-start | bytes 589828
  87.7 27.7 %all-to-all-start.3 = ((bf16[64,96,128]{2,1,0:T(8,128)(2,1)}), bf16[64,96,128]{2,1,0:T(8,128)(2,1)S(1)}, u32[]{:S(2)}, u32[]{:S(2)}) async-start(bf16[64,96,128]{2,1,0:T(8,128)(2,1)} %copy-done.2), calls=%async_computation.3 | async-start | bytes 3145728 | tf_op jit(solution)/shard_map/all_to_all | solution.py:62
  150.1 23.6 %copy-start.3 = (bf16[768,768]{1,0:T(8,128)(2,1)S(1)}, bf16[768,768]{1,0:T(8,128)(2,1)}, u32[]{:S(2)}) copy-start(bf16[768,768]{1,0:T(8,128)(2,1)} %weight_ref.1) | copy-start | bytes 3538948
  150.1 23.6 %copy-start.6 = (bf16[128,768]{1,0:T(8,128)(2,1)S(1)}, bf16[128,768]{1,0:T(8,128)(2,1)}, u32[]{:S(2)}) copy-start(bf16[128,768]{1,0:T(8,128)(2,1)} %copy-done.5) | copy-start | bytes 589828

commit v8 on v7

--- a/solution.py
+++ b/solution.py
@@ -14,7 +14,7 @@
 GW = HG * HD
 BLK = 32
 CHUNK = 96
-OW = 256
+PARTS = 512 + 256 + 64
 HALO = 136
 BF = jnp.bfloat16
 F32 = jnp.float32
@@ -56,6 +56,10 @@
 
 KEY_GROUPS = [[place(h, a, b) for b in range(SPLIT)] for h in range(SPLIT) for a in range(SPLIT)]
 HEAD_GROUPS = [[place(h, a, b) for a in range(SPLIT) for b in range(SPLIT)] for h in range(SPLIT)]
+
+
+def in_hbm(x):
+    return pltpu.with_memory_space_constraint(x, pltpu.HBM)
 
 
 def swap(x, groups=None):
@@ -172,72 +176,80 @@
     return results
 
 
-def put_rows(row_ref, out_ref, lanes):
+def put_rows(row_ref, out_ref, first):
     for n in range(row_ref.shape[0] // BLK):
         for b in range(SPLIT):
-            first = n * BLK + b * 8
-            out_ref[b, n * 8 : n * 8 + 8, :] = row_ref[first : first + 8, lanes].astype(BF)
-
-
-def pair_kernel(in_ref, all_ref, out_ref, key_ref, val_ref, row_ref):
-    @pl.when(pl.program_id(0) == 0)
+            row = n * BLK + b * 8
+            out_ref[b, first + n * 8 : first + n * 8 + 8, :] = row_ref[row : row + 8, :].astype(BF)
+
+
+UNIT = 8
+
+
+def pair_kernel(in_ref, all_ref, out_ref, lse_ref, key_ref, val_ref, row_ref, tail_ref):
+    step = pl.program_id(0)
+
+    @pl.when(step == 0)
     def _():
         ones = jnp.where(lax.broadcasted_iota(jnp.int32, (2048, HD), 1) == 0, 1.0, 0.0).astype(BF)
         for g in range(2):
             key_ref[g] = all_ref[:, 32:64, g * HD : (g + 1) * HD].reshape(2048, HD)
             val_ref[g, :, :HD] = all_ref[:, 64:96, g * HD : (g + 1) * HD].reshape(2048, HD)
             val_ref[g, :, HD:] = ones
-
-    half = 8
+        tail_ref[...] = jnp.zeros(tail_ref.shape, F32)
+
+    count = in_ref.shape[0] // UNIT
     units = []
-    for first in range(0, in_ref.shape[0], half):
+    for n in range(count):
         for g in range(2):
-            query = in_ref[first : first + half, :BLK, g * HD : (g + 1) * HD].reshape(half * BLK, HD)
+            query = in_ref[n * UNIT : (n + 1) * UNIT, :BLK, g * HD : (g + 1) * HD].reshape(UNIT * BLK, HD)
             units.append((query, key_ref[g], val_ref[g]))
     results = attend_heads(units)
-    lanes = lax.broadcasted_iota(jnp.int32, (half * BLK, 128), 1)
-    for n in range(len(units) // 2):
-        rows = slice(n * half * BLK, (n + 1) * half * BLK)
-        tail = jnp.zeros((half * BLK, 128), F32)
+    lanes = lax.broadcasted_iota(jnp.int32, tail_ref.shape, 1)
+    tail = tail_ref[...]
+    for n in range(count):
+        rows = slice(n * UNIT * BLK, (n + 1) * UNIT * BLK)
         for g in range(2):
             out, parts = results[2 * n + g]
             row_ref[rows, g * HD : (g + 1) * HD] = out
             for i, part in enumerate(parts):
-                tail = jnp.where(lanes == HD + 3 * g + i, part, tail)
-        row_ref[rows, 128:] = tail
-    put_rows(row_ref, out_ref, slice(0, OW))
-
-
-def single_kernel(in_ref, all_ref, part_ref, out_ref, key_ref, val_ref, row_ref):
-    @pl.when(pl.program_id(0) == 0)
-    def _():
-        ones = jnp.where(lax.broadcasted_iota(jnp.int32, (2048, HD), 1) == 0, 1.0, 0.0).astype(BF)
-        val_ref[:, HD:] = ones
-        for g in range(2):
-            rows = slice(g * 1024, (g + 1) * 1024)
-            key_ref[rows, :] = all_ref[:, g * 16 : g * 16 + 16, HD:].reshape(1024, HD)
-            val_ref[rows, :HD] = all_ref[:, 32:48, g * HD : (g + 1) * HD].reshape(1024, HD)
-
-    half = 8
+                tail = jnp.where(lanes == 16 * (step * count + n) + 3 * g + i, part, tail)
+    tail_ref[...] = tail
+    put_rows(row_ref, out_ref, 0)
+    put_rows(tail_ref, lse_ref, 0)
+
+
+def single_kernel(all_ref, part_ref, lse_ref, out_ref, key_ref, val_ref, row_ref, tail_ref):
+    ones = jnp.where(lax.broadcasted_iota(jnp.int32, (2048, HD), 1) == 0, 1.0, 0.0).astype(BF)
+    val_ref[:, HD:] = ones
+    for g in range(2):
+        rows = slice(g * 1024, (g + 1) * 1024)
+        key_ref[rows, :] = all_ref[:, g * 16 : g * 16 + 16, HD:].reshape(1024, HD)
+        val_ref[rows, :HD] = all_ref[:, 32:48, g * HD : (g + 1) * HD].reshape(1024, HD)
+
+    count = 64 // UNIT
     units = []
-    for first in range(0, in_ref.shape[0], half):
-        query = in_ref[first : first + half, :BLK, :HD].reshape(half * BLK, HD)
+    for n in range(count):
+        query = all_ref[n * UNIT : (n + 1) * UNIT, :BLK, :HD].reshape(UNIT * BLK, HD)
         units.append((query, key_ref[...], val_ref[...]))
     results = attend_heads(units)
-    lanes = lax.broadcasted_iota(jnp.int32, (half * BLK, 128), 1)
+    lanes = lax.broadcasted_iota(jnp.int32, tail_ref.shape, 1)
+    tail = jnp.zeros(tail_ref.shape, F32)
     for n, (out, parts) in enumerate(results):
-        rows = slice(n * half * BLK, (n + 1) * half * BLK)
-        tail = jnp.zeros((half * BLK, 128), F32)
+        first = n % (count // 2) * UNIT * BLK
+        lane = n // (count // 2) * HD
+        row_ref[first : first + UNIT * BLK, lane : lane + HD] = out
         for i, part in enumerate(parts):
-            tail = jnp.where(lanes == HD + 6 + i, part, tail)
-        row_ref[rows, :] = tail
-        row_ref[rows, :HD] = out
-    for n in range(row_ref.shape[0] // BLK):
+            tail = jnp.where(lanes == 16 * n + 6 + i, part, tail)
+    tail_ref[...] = tail
+    for b in range(SPLIT):
+        out_ref[b, :512, :] = part_ref[b]
+    put_rows(row_ref, out_ref, 512)
+    for n in range(UNIT):
         for b in range(SPLIT):
-            first = n * BLK + b * 8
-            old = part_ref[b, n * 8 : n * 8 + 8, 128:].astype(F32)
-            out_ref[b, n * 8 : n * 8 + 8, :128] = part_ref[b, n * 8 : n * 8 + 8, :128]
-            out_ref[b, n * 8 : n * 8 + 8, 128:] = (old + row_ref[first : first + 8, :]).astype(BF)
+            row = n * BLK + b * 8
+            new = lse_ref[b, n * 8 : n * 8 + 8, :].astype(F32) + tail_ref[row : row + 8, :]
+            out_ref[b, 768 + n * 8 : 776 + n * 8, :] = new.astype(BF)
 
 
 def attend_pair(packed):
@@ -249,39 +261,38 @@
             pl.BlockSpec((srcs, CHUNK, 128), lambda i: (i, 0, 0)),
             pl.BlockSpec((64, CHUNK, 128), lambda i: (0, 0, 0)),
         ],
-        out_specs=pl.BlockSpec((SPLIT, srcs * 8, OW), lambda i: (0, i, 0)),
-        out_shape=pltpu.HBM((SPLIT, 512, OW), BF),
+        out_specs=(
+            pl.BlockSpec((SPLIT, srcs * 8, 128), lambda i: (0, i, 0)),
+            pl.BlockSpec((SPLIT, 64, 128), lambda i: (0, 0, 0)),
+        ),
+        out_shape=(pltpu.HBM((SPLIT, 512, 128), BF), pltpu.HBM((SPLIT, 64, 128), BF)),
         scratch_shapes=[
             pltpu.VMEM((2, 2048, HD), BF),
             pltpu.VMEM((2, 2048, 2 * HD), BF),
-            pltpu.VMEM((srcs * BLK, OW), F32),
+            pltpu.VMEM((srcs * BLK, 128), F32),
+            pltpu.VMEM((UNIT * BLK, 128), F32),
         ],
         compiler_params=pltpu.CompilerParams(vmem_limit_bytes=38 << 20),
         name="attend_pair",
     )(packed, packed)
 
 
-def attend_single(rest, parts):
-    srcs = 64
-    block = pl.BlockSpec((SPLIT, srcs * 8, OW), lambda i: (0, i, 0))
+def attend_single(rest, parts, lses):
+    vmem = pl.BlockSpec(memory_space=pltpu.VMEM)
     return pl.pallas_call(
         single_kernel,
-        grid=(64 // srcs,),
-        in_specs=[
-            pl.BlockSpec((srcs, CHUNK, 128), lambda i: (i, 0, 0)),
-            pl.BlockSpec((64, CHUNK, 128), lambda i: (0, 0, 0)),
-            block,
-        ],
-        out_specs=block,
-        out_shape=jax.ShapeDtypeStruct((SPLIT, 512, OW), BF),
+        in_specs=[vmem] * 3,
+        out_specs=vmem,
+        out_shape=jax.ShapeDtypeStruct((SPLIT, PARTS, 128), BF),
         scratch_shapes=[
             pltpu.VMEM((2048, HD), BF),
             pltpu.VMEM((2048, 2 * HD), BF),
-            pltpu.VMEM((srcs * BLK, 128), F32),
+            pltpu.VMEM((1024, 128), F32),
+            pltpu.VMEM((UNIT * BLK, 128), F32),
         ],
         compiler_params=pltpu.CompilerParams(vmem_limit_bytes=38 << 20),
         name="attend_single",
-    )(rest, rest, parts)
+    )(rest, in_hbm(parts), in_hbm(lses))
 
 
 SHARE = 72
@@ -293,21 +304,21 @@
         cot_ref[:, c * 128 : (c + 1) * 128] = rest_ref[:, 48 + 8 * c : 56 + 8 * c, :].reshape(512, 128)
     tails = []
     for b in range(SPLIT):
-        tail = parts_ref[b, :, 128:].astype(F32)
+        tile = parts_ref[b, 768:, :].astype(F32)
+        tail = jnp.concatenate([tile] + [pltpu.roll(tile, 128 - 16 * j, 1) for j in range(1, 8)], axis=0)
         tails.append(tail + pltpu.roll(tail, 127, 1) + pltpu.roll(tail, 126, 1))
     top = jnp.maximum(jnp.maximum(tails[0], tails[1]), jnp.maximum(tails[2], tails[3]))
     ws = [jnp.exp(tail - top) for tail in tails]
-    total = ws[0] + ws[1] + ws[2] + ws[3]
+    inverse = 1.0 / (ws[0] + ws[1] + ws[2] + ws[3])
     low = lax.broadcasted_iota(jnp.int32, (512, 128), 1) < HD
     pair = jnp.zeros((512, 128), F32)
-    single = jnp.zeros((512, 128), F32)
-    inverse = 1.0 / total
+    folded = jnp.zeros((256, 128), F32)
     for b in range(SPLIT):
         share = ws[b] * inverse
-        w0, w1, w2 = (share[:, HD + 3 * g : HD + 3 * g + 1] for g in range(HG))
-        pair = pair + jnp.where(low, w0, w1) * parts_ref[b, :, :128].astype(F32)
-        single = single + w2 * parts_ref[b, :, 128:].astype(F32)
-    single = jnp.where(low, single, 0.0)
+        w0, w1, w2 = (share[:, 3 * g : 3 * g + 1] for g in range(HG))
+        pair = pair + jnp.where(low, w0, w1) * parts_ref[b, :512, :].astype(F32)
+        folded = folded + jnp.where(low[:256], w2[:256], w2[256:]) * parts_ref[b, 512:768, :].astype(F32)
+    single = jnp.where(low, jnp.concatenate([folded, pltpu.roll(folded, HD, 1)], axis=0), 0.0)
     pair_ref[...] = pair.astype(BF)
     single_ref[...] = single.astype(BF)
     for n in range(64):
@@ -614,10 +625,6 @@
     )(halo, conv_weight, cotangent, inside, patch_weight, query_weight, key_weight, value_weight)
 
 
-def in_hbm(x):
-    return pltpu.with_memory_space_constraint(x, pltpu.HBM)
-
-
 def local(
     features,
     neighbours,
@@ -630,7 +637,7 @@
     cotangent,
 ):
     _, inner = split_device(lax.axis_index("tile"))
-    faces = gather_faces(neighbours, in_hbm(features))
+    faces = gather_faces(in_hbm(neighbours), in_hbm(features))
     faces, inner = lax.optimization_barrier((faces, inner))
     faces = swap(faces, INNER).reshape(16, HALO, 256)
     tiles = faces[:, 128, :8].astype(jnp.int32)
@@ -652,7 +659,7 @@
     packed = swap(packed)
     packed, rest = lax.optimization_barrier((packed, rest))
     rest = swap(rest)
-    parts = swap(attend_single(rest, in_hbm(attend_pair(packed))), KEY_GROUPS)
+    parts = swap(attend_single(rest, *attend_pair(packed)), KEY_GROUPS)
     att, grad = merge(parts, rest)
     terms = swap(grad.reshape(16, SHARE, 128), HEAD_GROUPS)
     received = swap(share_out(terms, att))

time: 177 us -> 174 us (0.983)
  blocking collectives: 97.3 us -> 95.4 us
    all_to_all x5, blocking collectives: 97.3 us -> 95.4 us  [swap(): lax.all_to_all(x, 'tile', split_axis=0, concat_axis=0, tiled=True, axis_i...]
where the time goes in v8:
time: 174 us
  blocking collectives  95.4 us (55%)
  Pallas kernels  38.1 us (22%)
  waiting for transfers between devices  25.2 us (14%)
  starting transfers between devices  13 us (7%)
    all_to_all x5, blocking collectives, swap(): lax.all_to_all(x, 'tile', split_axis=0, concat_axis=0, tiled=True, axis_i...  95.4 us
    all_to_all x2, waiting for transfers between devices, swap(): lax.all_to_all(x, 'tile', split_axis=0, concat_axis=0, tiled=True, axis_i...  25.2 us
    all_to_all x2, starting transfers between devices, swap(): lax.all_to_all(x, 'tile', split_axis=0, concat_axis=0, tiled=True, axis_i...  13 us
    pallas_call x1, Pallas kernels, attend_pair(): pl.pallas_call(pair_kernel, grid=(64 // srcs,), in_specs=[pl.BlockSpec((s...  11.9 us
    pallas_call x1, Pallas kernels, attend_single(): pl.pallas_call(single_kernel, in_specs=[vmem] * 3, out_specs=vmem, out_sh...  6.61 us
    pallas_call x1, Pallas kernels, stem(): pl.pallas_call(stem_kernel, in_specs=[vmem] * 4 + [hbm] * 4, out_specs=(v...  6.39 us
  transfers between devices with their start and end apart: 2, of which 2 were waited for; matrix products, arithmetic and copies ran while one was open for 0% of the time, Pallas kernels for 8%

profile of v8, /device:TPU:0, one launch (start us, length us, event | category | flops | bytes accessed | tf_op | source)
XLA Modules:
  0.0 173.9 jit_solution(8036562564122382823)
XLA Ops:
  0.6 2.1 %faces.1 = bf16[8,2,136,256]{3,2,1,0:T(8,128)(2,1)S(1)} custom-call(s32[2,8]{1,0:T(2,128)} %links_ref.1, bf16[2,32,32,256]{3,2,1,0:T(8,128)(2,1)} %features_ref.1), custom_call_target="tpu_custom_call" | custom-call | tf_op jit(solution)/shard_map/faces/pallas_call | solution.py:103
  2.8 21.2 %all_to_all.35 = bf16[8,2,136,256]{3,2,1,0:T(8,128)(2,1)S(1)} all-to-all(bf16[8,2,136,256]{3,2,1,0:T(8,128)(2,1)S(1)} %faces.1), channel_id=1, replica_groups={{0,2,8,10,32,34,40,42},{6,4,14,12,38,36,46,44},{24,26,16,18,56,58,48,50..., dimensions={0} | all-to-all | bytes 2228224 | tf_op jit(solution)/shard_map/all_to_all | solution.py:66
  24.1 3.0 %route.1 = bf16[16,136,256]{2,1,0:T(8,128)(2,1)} custom-call(s32[16,8]{1,0:T(8,128)S(1)} %fusion.12.targets_ref, bf16[16,136,256]{2,1,0:T(8,128)(2,1)S(1)} %bitcast.17), custom_call_target="tpu_custom_call" | custom-call | tf_op jit(solution)/shard_map/route/pallas_call | solution.py:151
  27.0 0.0 copy-start
  27.0 7.7 %all-to-all-start.1 = ((bf16[16,136,256]{2,1,0:T(8,128)(2,1)}), bf16[16,136,256]{2,1,0:T(8,128)(2,1)}, u32[]{:S(2)}, u32[]{:S(2)}) async-start(bf16[16,136,256]{2,1,0:T(8,128)(2,1)} %route.1), calls=%async_computation.1 | async-start | bytes 2228224 | tf_op jit(solution)/shard_map/all_to_all | solution.py:66
  34.8 0.0 copy-done
  34.8 0.0 copy-start.1
  34.8 1.2 copy-done.1
  36.0 0.0 copy-start.4
  36.0 2.9 %conv_inside.1.inside_ref = f32[2,2048,128]{2,1,0:T(8,128)S(1)} custom-call(bf16[2,32,32,256]{3,2,1,0:T(8,128)(2,1)S(1)} %copy-done.1, bf16[9,256,256]{2,1,0:T(8,128)(2,1)S(1)} %bitcast.13), custom_call_target="tpu_custom_call" | custom-call | tf_op jit(solution)/shard_map/conv_inside/pallas_call | solution.py:477
  38.9 14.6 %all-to-all-done.1 = bf16[16,136,256]{2,1,0:T(8,128)(2,1)} async-done(((bf16[16,136,256]{2,1,0:T(8,128)(2,1)}), bf16[16,136,256]{2,1,0:T(8,128)(2,1)}, u32[]{:S(2)}, u32[]{:S(2)}) %all-to-all-start.1) | async-done | bytes 1114144 | tf_op jit(solution)/shard_map/all_to_all | solution.py:66
  53.5 0.0 copy-done.4
  53.5 6.4 %stem.1 = (bf16[128,768]{1,0:T(8,128)(2,1)S(1)}, bf16[64,96,128]{2,1,0:T(8,128)(2,1)S(1)}, bf16[64,96,128]{2,1,0:T(8,128)(2,1)S(1)}) custom-call(bf16[8,2,136,256]{3,2,1,0:T(8,128)(2,1)} %bitcast.8.halo_ref, bf16[9,256,256]{2,1,0:T(8,128)(2,1)S(1)} %bitcast.14, bf16[128,768]{1,0:T(8,128)(2,1)S(1)} %copy-done.4, f32[2,2048,128]{2,1,0:T(8,128)S(1)} %conv_inside.1.inside_ref, ...), custom_call_target="tpu_custom_call" | custom-call | tf_op jit(solution)/shard_map/stem/pallas_call | solution.py:604
  59.9 0.0 copy-start.2
  59.9 0.0 copy-start.5
  59.9 27.2 %all_to_all.36.in_ref.all_ref = bf16[64,96,128]{2,1,0:T(8,128)(2,1)S(1)} all-to-all(bf16[64,96,128]{2,1,0:T(8,128)(2,1)S(1)} %get-tuple-element.19), channel_id=1, replica_groups=mesh['tile'=64,'slide'=2] {'tile'}, dimensions={0} | all-to-all | bytes 3145728 | tf_op jit(solution)/shard_map/all_to_all | solution.py:66
  87.1 0.0 copy-done.2
  87.2 0.0 copy-done.5
  87.2 5.2 %all-to-all-start.3 = ((bf16[64,96,128]{2,1,0:T(8,128)(2,1)}), bf16[64,96,128]{2,1,0:T(8,128)(2,1)S(1)}, u32[]{:S(2)}, u32[]{:S(2)}) async-start(bf16[64,96,128]{2,1,0:T(8,128)(2,1)} %copy-done.2), calls=%async_computation.3 | async-start | bytes 3145728 | tf_op jit(solution)/shard_map/all_to_all | solution.py:66
  92.4 11.9 %attend_pair.1 = (bf16[4,512,128]{2,1,0:T(8,128)(2,1)}, bf16[4,64,128]{2,1,0:T(8,128)(2,1)}) custom-call(bf16[64,96,128]{2,1,0:T(8,128)(2,1)S(1)} %all_to_all.36.in_ref.all_ref, bf16[64,96,128]{2,1,0:T(8,128)(2,1)S(1)} %all_to_all.36.in_ref.all_ref), custom_call_target="tpu_custom_call" | custom-call | tf_op jit(solution)/shard_map/attend_pair/pallas_call | solution.py:257
  104.3 10.6 %all-to-all-done.3.all_ref.rest_ref = bf16[64,96,128]{2,1,0:T(8,128)(2,1)S(1)} async-done(((bf16[64,96,128]{2,1,0:T(8,128)(2,1)}), bf16[64,96,128]{2,1,0:T(8,128)(2,1)S(1)}, u32[]{:S(2)}, u32[]{:S(2)}) %all-to-all-start.3) | async-done | bytes 1572896 | tf_op jit(solution)/shard_map/all_to_all | solution.py:66
  114.9 6.6 %attend_single.1 = bf16[4,832,128]{2,1,0:T(8,128)(2,1)S(1)} custom-call(bf16[64,96,128]{2,1,0:T(8,128)(2,1)S(1)} %all-to-all-done.3.all_ref.rest_ref, bf16[4,512,128]{2,1,0:T(8,128)(2,1)} %get-tuple-element.23.part_ref, bf16[4,64,128]{2,1,0:T(8,128)(2,1)} %get-tuple-element.24.lse_ref), custom_call_target="tpu_custom_call" | custom-call | tf_op jit(solution)/shard_map/attend_single/pallas_call | solution.py:282
  121.5 11.9 %all_to_all.37.parts_ref = bf16[4,832,128]{2,1,0:T(8,128)(2,1)S(1)} all-to-all(bf16[4,832,128]{2,1,0:T(8,128)(2,1)S(1)} %attend_single.1), channel_id=1, replica_groups={{0,8,32,40},{24,16,56,48},{96,104,64,72},{120,112,88,80},{2,10,34,42},{..., dimensions={0} | all-to-all | bytes 1703936 | tf_op jit(solution)/shard_map/all_to_all | solution.py:66
  133.3 2.4 %merge.1 = (bf16[64,16,128]{2,1,0:T(8,128)(2,1)S(1)}, bf16[6,192,128]{2,1,0:T(8,128)(2,1)S(1)}) custom-call(bf16[4,832,128]{2,1,0:T(8,128)(2,1)S(1)} %all_to_all.37.parts_ref, bf16[64,96,128]{2,1,0:T(8,128)(2,1)S(1)} %all-to-all-done.3.all_ref.rest_ref), custom_call_target="tpu_custom_call" | custom-call | tf_op jit(solution)/shard_map/merge/pallas_call | solution.py:336
  135.8 11.5 %all_to_all.38.terms_ref = bf16[16,72,128]{2,1,0:T(8,128)(2,1)S(1)} all-to-all(bf16[16,72,128]{2,1,0:T(8,128)(2,1)S(1)} %bitcast.18), channel_id=1, replica_groups={{0,8,32,40,24,16,56,48,96,104,64,72,120,112,88,80},{2,10,34,42,26,18,58..., dimensions={0} | all-to-all | bytes 589824 | tf_op jit(solution)/shard_map/all_to_all | solution.py:66
  147.2 0.3 share.1
  147.5 0.0 copy-start.3
  147.5 0.0 copy-start.6
  147.5 23.6 %all_to_all.39.all_ref = bf16[64,88,128]{2,1,0:T(8,128)(2,1)S(1)} all-to-all(bf16[64,88,128]{2,1,0:T(8,128)(2,1)S(1)} %share.1), channel_id=1, replica_groups=mesh['tile'=64,'slide'=2] {'tile'}, dimensions={0} | all-to-all | bytes 2883584 | tf_op jit(solution)/shard_map/all_to_all | solution.py:66
  171.2 0.0 copy-done.3
  171.2 0.0 copy-done.6
  171.2 2.5 %finish.1 = (bf16[128,768]{1,0:T(8,128)(2,1)}, f32[768,768]{1,0:T(8,128)}) custom-call(bf16[64,88,128]{2,1,0:T(8,128)(2,1)S(1)} %all_to_all.39.all_ref, bf16[128,768]{1,0:T(8,128)(2,1)S(1)} %copy-done.6, bf16[768,768]{1,0:T(8,128)(2,1)S(1)} %copy-done.3), custom_call_target="tpu_custom_call" | custom-call | tf_op jit(solution)/shard_map/finish/pallas_call | solution.py:417
  (3 shorter events, 0.1 us)
Async XLA Ops:
  27.0 7.7 %copy-start = (bf16[3,3,256,256]{3,2,1,0:T(8,128)(2,1)S(1)}, bf16[3,3,256,256]{3,2,1,0:T(8,128)(2,1)}, u32[]{:S(2)}) copy-start(bf16[3,3,256,256]{3,2,1,0:T(8,128)(2,1)} %param.11) | copy-start | bytes 3538948
  27.0 26.4 %all-to-all-start.1 = ((bf16[16,136,256]{2,1,0:T(8,128)(2,1)}), bf16[16,136,256]{2,1,0:T(8,128)(2,1)}, u32[]{:S(2)}, u32[]{:S(2)}) async-start(bf16[16,136,256]{2,1,0:T(8,128)(2,1)} %route.1), calls=%async_computation.1 | async-start | bytes 2228224 | tf_op jit(solution)/shard_map/all_to_all | solution.py:66
  34.8 1.2 copy-start.1
  36.0 17.5 %copy-start.4 = (bf16[128,768]{1,0:T(8,128)(2,1)S(1)}, bf16[128,768]{1,0:T(8,128)(2,1)}, u32[]{:S(2)}) copy-start(bf16[128,768]{1,0:T(8,128)(2,1)} %cot_ref.1) | copy-start | bytes 589828
  59.9 27.3 %copy-start.2 = (bf16[64,96,128]{2,1,0:T(8,128)(2,1)}, bf16[64,96,128]{2,1,0:T(8,128)(2,1)S(1)}, u32[]{:S(2)}) copy-start(bf16[64,96,128]{2,1,0:T(8,128)(2,1)S(1)} %get-tuple-element.21) | copy-start | bytes 4718596
  59.9 27.3 %copy-start.5 = (bf16[128,768]{1,0:T(8,128)(2,1)}, bf16[128,768]{1,0:T(8,128)(2,1)S(1)}, u32[]{:S(2)}) copy-start(bf16[128,768]{1,0:T(8,128)(2,1)S(1)} %get-tuple-element.27.tokens_ref) | copy-start | bytes 589828
  87.2 27.7 %all-to-all-start.3 = ((bf16[64,96,128]{2,1,0:T(8,128)(2,1)}), bf16[64,96,128]{2,1,0:T(8,128)(2,1)S(1)}, u32[]{:S(2)}, u32[]{:S(2)}) async-start(bf16[64,96,128]{2,1,0:T(8,128)(2,1)} %copy-done.2), calls=%async_computation.3 | async-start | bytes 3145728 | tf_op jit(solution)/shard_map/all_to_all | solution.py:66
  147.5 23.7 %copy-start.3 = (bf16[768,768]{1,0:T(8,128)(2,1)S(1)}, bf16[768,768]{1,0:T(8,128)(2,1)}, u32[]{:S(2)}) copy-start(bf16[768,768]{1,0:T(8,128)(2,1)} %weight_ref.1) | copy-start | bytes 3538948
  147.5 23.6 %copy-start.6 = (bf16[128,768]{1,0:T(8,128)(2,1)S(1)}, bf16[128,768]{1,0:T(8,128)(2,1)}, u32[]{:S(2)}) copy-start(bf16[128,768]{1,0:T(8,128)(2,1)} %copy-done.5) | copy-start | bytes 589828

commit v9 on v8

--- a/solution.py
+++ b/solution.py
@@ -15,7 +15,8 @@
 BLK = 32
 CHUNK = 96
 PARTS = 512 + 256 + 64
-HALO = 136
+FACES = 128
+HALO = 264
 BF = jnp.bfloat16
 F32 = jnp.float32
 
@@ -78,15 +79,10 @@
     loads = [pltpu.make_async_copy(src, dst, sems.at[n]) for n, (src, dst) in enumerate(loads)]
     for load in loads:
         load.start()
-    lanes = lax.broadcasted_iota(jnp.int32, (8, 128), 1)
-    for t in range(2):
-        row = jnp.zeros((8, 128), F32)
-        for d in range(8):
-            row = jnp.where(lanes == d, links_ref[t, d].astype(F32), row)
-        faces_ref[t, 128:HALO, :128] = row.astype(BF)
-        faces_ref[t, 128:HALO, 128:] = jnp.zeros((8, 128), BF)
     for load in loads:
         load.wait()
+    lanes = lax.broadcasted_iota(jnp.int32, (8, 128), 1)
+    subs = lax.broadcasted_iota(jnp.int32, (8, 128), 0)
     for t in range(2):
         for n, x in enumerate((0, 7)):
             for lt in range(2):
@@ -94,6 +90,11 @@
                 faces_ref[t, 64 + n * 32 : 96 + n * 32, lt * 128 : lt * 128 + 128] = cols_ref[
                     pl.ds(x, 32, stride=8), :
                 ].astype(BF)
+    for t in range(2):
+        row = faces_ref[t, 64:72, :128].astype(F32)
+        for d in range(8):
+            row = jnp.where((lanes == d) & (subs == 0), links_ref[t, d].astype(F32), row)
+        faces_ref[t, 64:72, :128] = row.astype(BF)
     for n in range(8):
         out_ref[n] = faces_ref[...]
 
@@ -104,11 +105,11 @@
         faces_kernel,
         in_specs=[pl.BlockSpec(memory_space=pltpu.SMEM), hbm],
         out_specs=pl.BlockSpec(memory_space=pltpu.VMEM),
-        out_shape=jax.ShapeDtypeStruct((8, 2, HALO, 256), BF),
+        out_shape=jax.ShapeDtypeStruct((8, 2, FACES, 256), BF),
         scratch_shapes=[
             pltpu.VMEM((2, 2, 32, 8, 256), BF),
             pltpu.VMEM((256, 128), F32),
-            pltpu.VMEM((2, HALO, 256), BF),
+            pltpu.VMEM((2, FACES, 256), BF),
             pltpu.SemaphoreType.DMA((8,)),
         ],
         compiler_params=pltpu.CompilerParams(vmem_limit_bytes=6 << 20),
@@ -130,16 +131,22 @@
 
             @pl.when(target >= 0)
             def _():
+                outer, slot = target >> 1, target & 1
                 if direction in EDGES:
                     first, dest = EDGES[direction]
-                    out_ref[target, dest : dest + 32, :] = faces_ref[src, first : first + 32, :]
+                    row = pl.multiple_of(slot * FACES + dest, 32)
+                    out_ref[outer, pl.ds(row, 32), :] = faces_ref[src, first : first + 32, :]
+                    if direction == 3:
+                        tile = faces_ref[src, first : first + 8, :].astype(F32)
+                        cell = faces_ref[src, 0:8, :].astype(F32)
+                        out_ref[outer, pl.ds(row, 8), :] = jnp.where(row_ids == 0, cell, tile).astype(BF)
                 else:
                     row, dest = CORNERS[direction]
                     base = row // 8 * 8
                     cell = faces_ref[src, base : base + 8, :].astype(F32)[row - base : row - base + 1, :]
-                    old = out_ref[target, 128:HALO, :].astype(F32)
-                    new = jnp.where(row_ids == dest, jnp.broadcast_to(cell, (8, 256)), old)
-                    out_ref[target, 128:HALO, :] = new.astype(BF)
+                    old = out_ref[outer, 2 * FACES :, :].astype(F32)
+                    new = jnp.where(row_ids == slot * 4 + dest, jnp.broadcast_to(cell, (8, 256)), old)
+                    out_ref[outer, 2 * FACES :, :] = new.astype(BF)
 
         return carry
 
@@ -152,7 +159,7 @@
         route_kernel,
         in_specs=[pl.BlockSpec(memory_space=pltpu.SMEM), vmem],
         out_specs=vmem,
-        out_shape=jax.ShapeDtypeStruct((16, HALO, 256), BF),
+        out_shape=jax.ShapeDtypeStruct((8, HALO, 256), BF),
         compiler_params=pltpu.CompilerParams(vmem_limit_bytes=8 << 20),
         name="route",
     )(targets, faces)
@@ -376,6 +383,7 @@
 
 
 def finish_kernel(all_ref, tokens_ref, weight_ref, mixed_ref, grad_hbm, att_ref, grad_ref, sems):
+    copies = []
     for h in range(SPLIT):
         for m in range(16):
             at = place(h, m // SPLIT, m % SPLIT)
@@ -388,12 +396,11 @@
                     at, done : done + count, :
                 ].astype(F32)
                 done += count
-    copies = [
-        pltpu.make_async_copy(grad_ref.at[n * 384 : (n + 1) * 384], grad_hbm.at[n * 384 : (n + 1) * 384], sems.at[n])
-        for n in range(2)
-    ]
-    for copy in copies:
-        copy.start()
+        for n, (first, count) in enumerate(((h * 128, 128), (512 + h * HD, HD))):
+            rows = slice(first, first + count)
+            copy = pltpu.make_async_copy(grad_ref.at[rows], grad_hbm.at[rows], sems.at[2 * h + n])
+            copy.start()
+            copies.append(copy)
     lanes = lax.broadcasted_iota(jnp.int32, (8, 128), 1) < HD
     for a in range(SPLIT):
         for b in range(SPLIT):
@@ -425,7 +432,7 @@
         scratch_shapes=[
             pltpu.VMEM((128, DM), BF),
             pltpu.VMEM((DM, DM), F32),
-            pltpu.SemaphoreType.DMA((2,)),
+            pltpu.SemaphoreType.DMA((8,)),
         ],
         compiler_params=pltpu.CompilerParams(vmem_limit_bytes=12 << 20),
         name="finish",
@@ -506,24 +513,26 @@
     wv_ref,
     sems,
 ):
-    pairs = ((patch_hbm, patch_ref), (query_hbm, wq_ref), (key_hbm, wk_ref), (value_hbm, wv_ref))
+    pairs = [(patch_hbm.at[r * 1024 : r * 1024 + 1024], patch_ref.at[r * 1024 : r * 1024 + 1024]) for r in range(4)]
+    pairs += [(query_hbm, wq_ref), (key_hbm, wk_ref), (value_hbm, wv_ref)]
     loads = [pltpu.make_async_copy(src, dst, sems.at[n]) for n, (src, dst) in enumerate(pairs)]
     for load in loads:
         load.start()
 
     def halo_rows(t, first, count):
-        total = halo_ref[0, t, first : first + count, :].astype(F32)
+        first = t * FACES + first
+        total = halo_ref[0, first : first + count, :].astype(F32)
         for n in range(1, 8):
-            total = total + halo_ref[n, t, first : first + count, :].astype(F32)
+            total = total + halo_ref[n, first : first + count, :].astype(F32)
         return total
 
+    corner = halo_rows(2, 0, 8)
     for t in range(2):
-        corner = halo_rows(t, 128, 8)
         for side in range(4):
             side_ref[side, t, Z0 : Z0 + 32, :] = halo_rows(t, 32 * side, 32)
             for end, row in enumerate((Z0 - 1, Z0 + 32)):
                 if side < 2:
-                    cell = corner[side * 2 + end : side * 2 + end + 1]
+                    cell = corner[t * 4 + side * 2 + end : t * 4 + side * 2 + end + 1]
                 else:
                     cell = jnp.zeros((1, 256), F32)
                 side_ref[side, t, row : row + 1, :] = cell
@@ -539,6 +548,7 @@
             edge_ref[lt, side * 64 : side * 64 + 64, :] = edge[:, lt * 128 : lt * 128 + 128]
 
     sub = lax.broadcasted_iota(jnp.int32, (8, 128), 0)
+    embedded = jnp.zeros((128, DM), F32)
     for r in range(4):
         for c in range(4):
             for t in range(2):
@@ -557,10 +567,12 @@
                             total = total + jnp.where(sub == (0 if c == 0 else 7), cell, 0.0)
                         col = (r * 4 + c) * 256 + lt * 128
                         hid_ref[row : row + 8, col : col + 128] = jax.nn.gelu(total).astype(BF)
-    loads[0].wait()
-    tokens = jnp.dot(hid_ref[...], patch_ref[...], preferred_element_type=F32).astype(BF)
+        loads[r].wait()
+        part = slice(r * 1024, r * 1024 + 1024)
+        embedded = embedded + jnp.dot(hid_ref[:, part], patch_ref[part, :], preferred_element_type=F32)
+    tokens = embedded.astype(BF)
     tokens_ref[...] = tokens
-    for load in loads[1:]:
+    for load in loads[4:]:
         load.wait()
     query = jnp.dot(tokens, wq_ref[...], preferred_element_type=F32)
     keys = jnp.dot(tokens, wk_ref[...], preferred_element_type=F32)
@@ -618,7 +630,7 @@
             pltpu.VMEM((DM, DM), BF),
             pltpu.VMEM((DM, DM), BF),
             pltpu.VMEM((DM, DM), BF),
-            pltpu.SemaphoreType.DMA((4,)),
+            pltpu.SemaphoreType.DMA((7,)),
         ],
         compiler_params=pltpu.CompilerParams(vmem_limit_bytes=28 << 20),
         name="stem",
@@ -639,12 +651,12 @@
     _, inner = split_device(lax.axis_index("tile"))
     faces = gather_faces(in_hbm(neighbours), in_hbm(features))
     faces, inner = lax.optimization_barrier((faces, inner))
-    faces = swap(faces, INNER).reshape(16, HALO, 256)
-    tiles = faces[:, 128, :8].astype(jnp.int32)
+    faces = swap(faces, INNER).reshape(16, FACES, 256)
+    tiles = faces[:, 64, :8].astype(jnp.int32)
     outer, goal = split_device(tiles >> 1)
     targets = jnp.where((tiles < 128) & (goal == inner), (outer & 7) * 2 + (tiles & 1), -1)
     routed, taps = lax.optimization_barrier((route(targets, faces), conv_weight.reshape(9, 256, 256)))
-    halo = swap(routed, OUTER).reshape(8, 2, HALO, 256)
+    halo = swap(routed, OUTER)
     inside = conv_inside(features, taps)
     tokens, packed, rest = stem(
         halo,

time: 174 us -> 173 us (level)
  transfers between devices with their start and end apart: 2 -> 2, of which waited for: 2 -> 2; matrix products, arithmetic and copies ran while one was open for 0% -> 0% of each run, Pallas kernels for 8% -> 9%
where the time goes in v9:
time: 173 us
  blocking collectives  94.7 us (55%)
  Pallas kernels  38.1 us (22%)
  waiting for transfers between devices  24.8 us (14%)
  starting transfers between devices  13 us (8%)
    all_to_all x5, blocking collectives, swap(): lax.all_to_all(x, 'tile', split_axis=0, concat_axis=0, tiled=True, axis_i...  94.7 us
    all_to_all x2, waiting for transfers between devices, swap(): lax.all_to_all(x, 'tile', split_axis=0, concat_axis=0, tiled=True, axis_i...  24.8 us
    all_to_all x2, starting transfers between devices, swap(): lax.all_to_all(x, 'tile', split_axis=0, concat_axis=0, tiled=True, axis_i...  13 us
    pallas_call x1, Pallas kernels, attend_pair(): pl.pallas_call(pair_kernel, grid=(64 // srcs,), in_specs=[pl.BlockSpec((s...  11.9 us
    pallas_call x1, Pallas kernels, attend_single(): pl.pallas_call(single_kernel, in_specs=[vmem] * 3, out_specs=vmem, out_sh...  6.6 us
    pallas_call x1, Pallas kernels, stem(): pl.pallas_call(stem_kernel, in_specs=[vmem] * 4 + [hbm] * 4, out_specs=(v...  6.5 us
  transfers between devices with their start and end apart: 2, of which 2 were waited for; matrix products, arithmetic and copies ran while one was open for 0% of the time, Pallas kernels for 9%

profile of v9, /device:TPU:0, one launch (start us, length us, event | category | flops | bytes accessed | tf_op | source)
XLA Modules:
  0.0 172.9 jit_solution(14721128938036138352)
XLA Ops:
  0.6 2.1 %faces.1 = bf16[8,2,128,256]{3,2,1,0:T(8,128)(2,1)S(1)} custom-call(s32[2,8]{1,0:T(2,128)} %links_ref.1, bf16[2,32,32,256]{3,2,1,0:T(8,128)(2,1)} %features_ref.1), custom_call_target="tpu_custom_call" | custom-call | tf_op jit(solution)/shard_map/faces/pallas_call | solution.py:104
  2.8 20.5 %all_to_all.35 = bf16[8,2,128,256]{3,2,1,0:T(8,128)(2,1)S(1)} all-to-all(bf16[8,2,128,256]{3,2,1,0:T(8,128)(2,1)S(1)} %faces.1), channel_id=1, replica_groups={{0,2,8,10,32,34,40,42},{6,4,14,12,38,36,46,44},{24,26,16,18,56,58,48,50..., dimensions={0} | all-to-all | bytes 2097152 | tf_op jit(solution)/shard_map/all_to_all | solution.py:67
  23.4 3.0 %route.1 = bf16[8,264,256]{2,1,0:T(8,128)(2,1)} custom-call(s32[16,8]{1,0:T(8,128)S(1)} %fusion.12.targets_ref, bf16[16,128,256]{2,1,0:T(8,128)(2,1)S(1)} %bitcast.16), custom_call_target="tpu_custom_call" | custom-call | tf_op jit(solution)/shard_map/route/pallas_call | solution.py:158
  26.3 0.0 copy-start
  26.3 7.8 %all-to-all-start.1 = ((bf16[8,264,256]{2,1,0:T(8,128)(2,1)}), bf16[8,264,256]{2,1,0:T(8,128)(2,1)}, u32[]{:S(2)}, u32[]{:S(2)}) async-start(bf16[8,264,256]{2,1,0:T(8,128)(2,1)} %route.1), calls=%async_computation.1 | async-start | bytes 2162688 | tf_op jit(solution)/shard_map/all_to_all | solution.py:67
  34.1 0.0 copy-done
  34.1 0.0 copy-start.1
  34.1 1.2 copy-done.1
  35.3 0.0 copy-start.4
  35.3 2.9 %conv_inside.1.inside_ref = f32[2,2048,128]{2,1,0:T(8,128)S(1)} custom-call(bf16[2,32,32,256]{3,2,1,0:T(8,128)(2,1)S(1)} %copy-done.1, bf16[9,256,256]{2,1,0:T(8,128)(2,1)S(1)} %bitcast.12), custom_call_target="tpu_custom_call" | custom-call | tf_op jit(solution)/shard_map/conv_inside/pallas_call | solution.py:484
  38.2 14.2 %all-to-all-done.1.halo_ref = bf16[8,264,256]{2,1,0:T(8,128)(2,1)} async-done(((bf16[8,264,256]{2,1,0:T(8,128)(2,1)}), bf16[8,264,256]{2,1,0:T(8,128)(2,1)}, u32[]{:S(2)}, u32[]{:S(2)}) %all-to-all-start.1) | async-done | bytes 1081376 | tf_op jit(solution)/shard_map/all_to_all | solution.py:67
  52.4 0.0 copy-done.4
  52.5 6.5 %stem.1 = (bf16[128,768]{1,0:T(8,128)(2,1)S(1)}, bf16[64,96,128]{2,1,0:T(8,128)(2,1)S(1)}, bf16[64,96,128]{2,1,0:T(8,128)(2,1)S(1)}) custom-call(bf16[8,264,256]{2,1,0:T(8,128)(2,1)} %all-to-all-done.1.halo_ref, bf16[9,256,256]{2,1,0:T(8,128)(2,1)S(1)} %bitcast.13, bf16[128,768]{1,0:T(8,128)(2,1)S(1)} %copy-done.4, ...), custom_call_target="tpu_custom_call" | custom-call | tf_op jit(solution)/shard_map/stem/pallas_call | solution.py:616
  59.0 0.0 copy-start.2
  59.0 0.0 copy-start.5
  59.0 27.3 %all_to_all.36.in_ref.all_ref = bf16[64,96,128]{2,1,0:T(8,128)(2,1)S(1)} all-to-all(bf16[64,96,128]{2,1,0:T(8,128)(2,1)S(1)} %get-tuple-element.19), channel_id=1, replica_groups=mesh['tile'=64,'slide'=2] {'tile'}, dimensions={0} | all-to-all | bytes 3145728 | tf_op jit(solution)/shard_map/all_to_all | solution.py:67
  86.3 0.0 copy-done.2
  86.3 0.0 copy-done.5
  86.3 5.2 %all-to-all-start.3 = ((bf16[64,96,128]{2,1,0:T(8,128)(2,1)}), bf16[64,96,128]{2,1,0:T(8,128)(2,1)S(1)}, u32[]{:S(2)}, u32[]{:S(2)}) async-start(bf16[64,96,128]{2,1,0:T(8,128)(2,1)} %copy-done.2), calls=%async_computation.3 | async-start | bytes 3145728 | tf_op jit(solution)/shard_map/all_to_all | solution.py:67
  91.5 11.9 %attend_pair.1 = (bf16[4,512,128]{2,1,0:T(8,128)(2,1)}, bf16[4,64,128]{2,1,0:T(8,128)(2,1)}) custom-call(bf16[64,96,128]{2,1,0:T(8,128)(2,1)S(1)} %all_to_all.36.in_ref.all_ref, bf16[64,96,128]{2,1,0:T(8,128)(2,1)S(1)} %all_to_all.36.in_ref.all_ref), custom_call_target="tpu_custom_call" | custom-call | tf_op jit(solution)/shard_map/attend_pair/pallas_call | solution.py:264
  103.4 10.6 %all-to-all-done.3.all_ref.rest_ref = bf16[64,96,128]{2,1,0:T(8,128)(2,1)S(1)} async-done(((bf16[64,96,128]{2,1,0:T(8,128)(2,1)}), bf16[64,96,128]{2,1,0:T(8,128)(2,1)S(1)}, u32[]{:S(2)}, u32[]{:S(2)}) %all-to-all-start.3) | async-done | bytes 1572896 | tf_op jit(solution)/shard_map/all_to_all | solution.py:67
  114.0 6.6 %attend_single.1 = bf16[4,832,128]{2,1,0:T(8,128)(2,1)S(1)} custom-call(bf16[64,96,128]{2,1,0:T(8,128)(2,1)S(1)} %all-to-all-done.3.all_ref.rest_ref, bf16[4,512,128]{2,1,0:T(8,128)(2,1)} %get-tuple-element.23.part_ref, bf16[4,64,128]{2,1,0:T(8,128)(2,1)} %get-tuple-element.24.lse_ref), custom_call_target="tpu_custom_call" | custom-call | tf_op jit(solution)/shard_map/attend_single/pallas_call | solution.py:289
  120.6 11.9 %all_to_all.37.parts_ref = bf16[4,832,128]{2,1,0:T(8,128)(2,1)S(1)} all-to-all(bf16[4,832,128]{2,1,0:T(8,128)(2,1)S(1)} %attend_single.1), channel_id=1, replica_groups={{0,8,32,40},{24,16,56,48},{96,104,64,72},{120,112,88,80},{2,10,34,42},{..., dimensions={0} | all-to-all | bytes 1703936 | tf_op jit(solution)/shard_map/all_to_all | solution.py:67
  132.4 2.4 %merge.1 = (bf16[64,16,128]{2,1,0:T(8,128)(2,1)S(1)}, bf16[6,192,128]{2,1,0:T(8,128)(2,1)S(1)}) custom-call(bf16[4,832,128]{2,1,0:T(8,128)(2,1)S(1)} %all_to_all.37.parts_ref, bf16[64,96,128]{2,1,0:T(8,128)(2,1)S(1)} %all-to-all-done.3.all_ref.rest_ref), custom_call_target="tpu_custom_call" | custom-call | tf_op jit(solution)/shard_map/merge/pallas_call | solution.py:343
  134.9 11.5 %all_to_all.38.terms_ref = bf16[16,72,128]{2,1,0:T(8,128)(2,1)S(1)} all-to-all(bf16[16,72,128]{2,1,0:T(8,128)(2,1)S(1)} %bitcast.17), channel_id=1, replica_groups={{0,8,32,40,24,16,56,48,96,104,64,72,120,112,88,80},{2,10,34,42,26,18,58..., dimensions={0} | all-to-all | bytes 589824 | tf_op jit(solution)/shard_map/all_to_all | solution.py:67
  146.3 0.3 share.1
  146.6 0.0 copy-start.3
  146.6 0.0 copy-start.6
  146.6 23.6 %all_to_all.39.all_ref = bf16[64,88,128]{2,1,0:T(8,128)(2,1)S(1)} all-to-all(bf16[64,88,128]{2,1,0:T(8,128)(2,1)S(1)} %share.1), channel_id=1, replica_groups=mesh['tile'=64,'slide'=2] {'tile'}, dimensions={0} | all-to-all | bytes 2883584 | tf_op jit(solution)/shard_map/all_to_all | solution.py:67
  170.3 0.0 copy-done.3
  170.3 0.0 copy-done.6
  170.3 2.4 %finish.1 = (bf16[128,768]{1,0:T(8,128)(2,1)}, f32[768,768]{1,0:T(8,128)}) custom-call(bf16[64,88,128]{2,1,0:T(8,128)(2,1)S(1)} %all_to_all.39.all_ref, bf16[128,768]{1,0:T(8,128)(2,1)S(1)} %copy-done.6, bf16[768,768]{1,0:T(8,128)(2,1)S(1)} %copy-done.3), custom_call_target="tpu_custom_call" | custom-call | tf_op jit(solution)/shard_map/finish/pallas_call | solution.py:424
  (3 shorter events, 0.1 us)
Async XLA Ops:
  26.3 7.8 %copy-start = (bf16[3,3,256,256]{3,2,1,0:T(8,128)(2,1)S(1)}, bf16[3,3,256,256]{3,2,1,0:T(8,128)(2,1)}, u32[]{:S(2)}) copy-start(bf16[3,3,256,256]{3,2,1,0:T(8,128)(2,1)} %param.11) | copy-start | bytes 3538948
  26.3 26.1 %all-to-all-start.1 = ((bf16[8,264,256]{2,1,0:T(8,128)(2,1)}), bf16[8,264,256]{2,1,0:T(8,128)(2,1)}, u32[]{:S(2)}, u32[]{:S(2)}) async-start(bf16[8,264,256]{2,1,0:T(8,128)(2,1)} %route.1), calls=%async_computation.1 | async-start | bytes 2162688 | tf_op jit(solution)/shard_map/all_to_all | solution.py:67
  34.1 1.2 copy-start.1
  35.3 17.1 %copy-start.4 = (bf16[128,768]{1,0:T(8,128)(2,1)S(1)}, bf16[128,768]{1,0:T(8,128)(2,1)}, u32[]{:S(2)}) copy-start(bf16[128,768]{1,0:T(8,128)(2,1)} %cot_ref.1) | copy-start | bytes 589828
  59.0 27.3 %copy-start.2 = (bf16[64,96,128]{2,1,0:T(8,128)(2,1)}, bf16[64,96,128]{2,1,0:T(8,128)(2,1)S(1)}, u32[]{:S(2)}) copy-start(bf16[64,96,128]{2,1,0:T(8,128)(2,1)S(1)} %get-tuple-element.21) | copy-start | bytes 4718596
  59.0 27.3 %copy-start.5 = (bf16[128,768]{1,0:T(8,128)(2,1)}, bf16[128,768]{1,0:T(8,128)(2,1)S(1)}, u32[]{:S(2)}) copy-start(bf16[128,768]{1,0:T(8,128)(2,1)S(1)} %get-tuple-element.27.tokens_ref) | copy-start | bytes 589828
  86.3 27.7 %all-to-all-start.3 = ((bf16[64,96,128]{2,1,0:T(8,128)(2,1)}), bf16[64,96,128]{2,1,0:T(8,128)(2,1)S(1)}, u32[]{:S(2)}, u32[]{:S(2)}) async-start(bf16[64,96,128]{2,1,0:T(8,128)(2,1)} %copy-done.2), calls=%async_computation.3 | async-start | bytes 3145728 | tf_op jit(solution)/shard_map/all_to_all | solution.py:67
  146.6 23.6 %copy-start.3 = (bf16[768,768]{1,0:T(8,128)(2,1)S(1)}, bf16[768,768]{1,0:T(8,128)(2,1)}, u32[]{:S(2)}) copy-start(bf16[768,768]{1,0:T(8,128)(2,1)} %weight_ref.1) | copy-start | bytes 3538948
  146.6 23.6 %copy-start.6 = (bf16[128,768]{1,0:T(8,128)(2,1)S(1)}, bf16[128,768]{1,0:T(8,128)(2,1)}, u32[]{:S(2)}) copy-start(bf16[128,768]{1,0:T(8,128)(2,1)} %copy-done.5) | copy-start | bytes 589828

commit v10 on v9

--- a/solution.py
+++ b/solution.py
@@ -443,81 +443,33 @@
 Z0 = 8
 
 
-def conv_kernel(features_ref, conv_ref, out_ref, left_ref, right_ref):
-    for t in range(2):
-        for y in range(32):
-            for lt in range(2):
-                slot = (t * 32 + y) * ZW
-                left_ref[lt, slot : slot + Z0, :] = jnp.zeros((Z0, 128), F32)
-                right_ref[lt, slot + Z0 + 32 : slot + ZW, :] = jnp.zeros((Z0, 128), F32)
-        for y in range(0, 32, 8):
-            zero = jnp.zeros((32, 256), BF)
-            accs = []
-            for dx in range(3):
-                acc = jnp.zeros((256, 256), F32)
-                for dy in range(3):
-                    first = y + dy - 1
-                    if first < 0:
-                        rows = jnp.concatenate([zero, features_ref[t, :7].reshape(224, 256)], axis=0)
-                    elif first + 8 > 32:
-                        rows = jnp.concatenate([features_ref[t, first:].reshape(224, 256), zero], axis=0)
-                    else:
-                        rows = features_ref[t, first : first + 8].reshape(256, 256)
-                    acc = acc + jnp.dot(rows, conv_ref[dy * 3 + dx], preferred_element_type=F32)
-                accs.append(acc)
-            for n in range(8):
-                slot = (t * 32 + y + n) * ZW + Z0
-                row = (t * 32 + y + n) * 32
-                for lt in range(2):
-                    part = (slice(n * 32, n * 32 + 32), slice(lt * 128, lt * 128 + 128))
-                    left_ref[lt, slot : slot + 32, :] = accs[0][part]
-                    right_ref[lt, slot : slot + 32, :] = accs[2][part]
-                    out_ref[lt, row : row + 32, :] = (
-                        accs[1][part]
-                        + left_ref[lt, slot - 1 : slot + 31, :]
-                        + right_ref[lt, slot + 1 : slot + 33, :]
-                    )
-
-
-def conv_inside(features, taps):
-    vmem = pl.BlockSpec(memory_space=pltpu.VMEM)
-    return pl.pallas_call(
-        conv_kernel,
-        in_specs=[vmem, vmem],
-        out_specs=vmem,
-        out_shape=jax.ShapeDtypeStruct((2, 2048, 128), F32),
-        scratch_shapes=[pltpu.VMEM((2, 64 * ZW, 128), F32), pltpu.VMEM((2, 64 * ZW, 128), F32)],
-        compiler_params=pltpu.CompilerParams(vmem_limit_bytes=16 << 20),
-        name="conv_inside",
-    )(features, taps)
-
-
 def stem_kernel(
     halo_ref,
     conv_ref,
     cot_ref,
-    inside_ref,
+    features_hbm,
     patch_hbm,
-    query_hbm,
-    key_hbm,
-    value_hbm,
+    wq_ref,
+    wk_ref,
+    wv_ref,
     tokens_ref,
     packed_ref,
     rest_ref,
+    maps_ref,
     side_ref,
-    edge_ref,
+    left_ref,
+    mid_ref,
+    right_ref,
     hid_ref,
     patch_ref,
-    wq_ref,
-    wk_ref,
-    wv_ref,
     sems,
 ):
-    pairs = [(patch_hbm.at[r * 1024 : r * 1024 + 1024], patch_ref.at[r * 1024 : r * 1024 + 1024]) for r in range(4)]
-    pairs += [(query_hbm, wq_ref), (key_hbm, wk_ref), (value_hbm, wv_ref)]
-    loads = [pltpu.make_async_copy(src, dst, sems.at[n]) for n, (src, dst) in enumerate(pairs)]
+    loads = [pltpu.make_async_copy(features_hbm.at[t], maps_ref.at[t, 1:33], sems.at[t]) for t in range(2)]
+    parts = [slice(r * 1024, r * 1024 + 1024) for r in range(4)]
+    loads += [pltpu.make_async_copy(patch_hbm.at[p], patch_ref.at[p], sems.at[2 + r]) for r, p in enumerate(parts)]
     for load in loads:
         load.start()
+    zrefs = (left_ref, mid_ref, right_ref)
 
     def halo_rows(t, first, count):
         first = t * FACES + first
@@ -528,52 +480,54 @@
 
     corner = halo_rows(2, 0, 8)
     for t in range(2):
-        for side in range(4):
-            side_ref[side, t, Z0 : Z0 + 32, :] = halo_rows(t, 32 * side, 32)
+        maps_ref[t, 0] = halo_rows(t, 0, 32).astype(BF)
+        maps_ref[t, 33] = halo_rows(t, 32, 32).astype(BF)
+        for side in range(2):
+            side_ref[side, t, Z0 : Z0 + 32, :] = halo_rows(t, 64 + 32 * side, 32)
             for end, row in enumerate((Z0 - 1, Z0 + 32)):
-                if side < 2:
-                    cell = corner[t * 4 + side * 2 + end : t * 4 + side * 2 + end + 1]
-                else:
-                    cell = jnp.zeros((1, 256), F32)
-                side_ref[side, t, row : row + 1, :] = cell
-    for side in range(4):
-        edge = jnp.zeros((64, 256), F32)
-        for k in range(3):
-            part = jnp.concatenate(
-                [side_ref[side, t, Z0 - 1 + k : Z0 + 31 + k, :].astype(BF) for t in range(2)], axis=0
-            )
-            tap = (k, 6 + k, 3 * k, 3 * k + 2)[side]
-            edge = edge + jnp.dot(part, conv_ref[tap], preferred_element_type=F32)
-        for lt in range(2):
-            edge_ref[lt, side * 64 : side * 64 + 64, :] = edge[:, lt * 128 : lt * 128 + 128]
-
-    sub = lax.broadcasted_iota(jnp.int32, (8, 128), 0)
+                cell = t * 4 + 2 * end + side
+                side_ref[side, t, row : row + 1, :] = corner[cell : cell + 1]
+    for t in range(2):
+        for side in range(2):
+            edge = jnp.zeros((32, 256), F32)
+            for dy in range(3):
+                part = side_ref[side, t, Z0 - 1 + dy : Z0 + 31 + dy, :].astype(BF)
+                edge = edge + jnp.dot(part, conv_ref[dy * 3 + side * 2], preferred_element_type=F32)
+            dest, first = ((left_ref, Z0 - 1), (right_ref, Z0 + 32))[side]
+            for lt in range(2):
+                dest[lt, pl.ds(t * 32 * ZW + first, 32, stride=ZW), :] = edge[:, lt * 128 : lt * 128 + 128]
+    for t in range(2):
+        loads[t].wait()
+        for y in range(0, 32, 8):
+            for dx in range(3):
+                acc = jnp.zeros((256, 256), F32)
+                for dy in range(3):
+                    rows = maps_ref[t, y + dy : y + dy + 8].reshape(256, 256)
+                    acc = acc + jnp.dot(rows, conv_ref[dy * 3 + dx], preferred_element_type=F32)
+                for n in range(8):
+                    first = (t * 32 + y + n) * ZW + Z0
+                    for lt in range(2):
+                        zrefs[dx][lt, first : first + 32, :] = acc[n * 32 : n * 32 + 32, lt * 128 : lt * 128 + 128]
+
     embedded = jnp.zeros((128, DM), F32)
     for r in range(4):
         for c in range(4):
             for t in range(2):
                 for pr in range(8):
-                    y = pr * 4 + r
+                    first = (t * 32 + pr * 4 + r) * ZW + Z0 + c
                     row = (t * 8 + pr) * 8
                     for lt in range(2):
-                        total = inside_ref[lt, pl.ds((t * 32 + y) * 32 + c, 8, stride=4), :]
-                        if y == 0:
-                            total = total + edge_ref[lt, pl.ds(t * 32 + c, 8, stride=4), :]
-                        if y == 31:
-                            total = total + edge_ref[lt, pl.ds(64 + t * 32 + c, 8, stride=4), :]
-                        if c == 0 or c == 3:
-                            at = (128 if c == 0 else 192) + t * 32 + y
-                            cell = jnp.broadcast_to(edge_ref[lt, at : at + 1, :], (8, 128))
-                            total = total + jnp.where(sub == (0 if c == 0 else 7), cell, 0.0)
+                        total = (
+                            mid_ref[lt, pl.ds(first, 8, stride=4), :]
+                            + left_ref[lt, pl.ds(first - 1, 8, stride=4), :]
+                            + right_ref[lt, pl.ds(first + 1, 8, stride=4), :]
+                        )
                         col = (r * 4 + c) * 256 + lt * 128
                         hid_ref[row : row + 8, col : col + 128] = jax.nn.gelu(total).astype(BF)
-        loads[r].wait()
-        part = slice(r * 1024, r * 1024 + 1024)
-        embedded = embedded + jnp.dot(hid_ref[:, part], patch_ref[part, :], preferred_element_type=F32)
+        loads[2 + r].wait()
+        embedded = embedded + jnp.dot(hid_ref[:, parts[r]], patch_ref[parts[r], :], preferred_element_type=F32)
     tokens = embedded.astype(BF)
     tokens_ref[...] = tokens
-    for load in loads[4:]:
-        load.wait()
     query = jnp.dot(tokens, wq_ref[...], preferred_element_type=F32)
     keys = jnp.dot(tokens, wk_ref[...], preferred_element_type=F32)
     values = jnp.dot(tokens, wv_ref[...], preferred_element_type=F32)
@@ -610,12 +564,12 @@
                     rest_ref[at, 48 + 8 * c : 56 + 8 * c, :] = cot_ref[row : row + 8, c * 128 : (c + 1) * 128]
 
 
-def stem(halo, conv_weight, cotangent, inside, patch_weight, query_weight, key_weight, value_weight):
+def stem(halo, conv_weight, cotangent, features, patch_weight, query_weight, key_weight, value_weight):
     hbm = pl.BlockSpec(memory_space=pl.ANY)
     vmem = pl.BlockSpec(memory_space=pltpu.VMEM)
     return pl.pallas_call(
         stem_kernel,
-        in_specs=[vmem] * 4 + [hbm] * 4,
+        in_specs=[vmem] * 3 + [hbm] * 2 + [vmem] * 3,
         out_specs=(vmem, vmem, vmem),
         out_shape=(
             jax.ShapeDtypeStruct((128, DM), BF),
@@ -623,18 +577,18 @@
             jax.ShapeDtypeStruct((64, CHUNK, 128), BF),
         ),
         scratch_shapes=[
-            pltpu.VMEM((4, 2, ZW, 256), F32),
-            pltpu.VMEM((2, 256, 128), F32),
+            pltpu.VMEM((2, 34, 32, 256), BF),
+            pltpu.VMEM((2, 2, ZW, 256), F32),
+            pltpu.VMEM((2, 64 * ZW, 128), F32),
+            pltpu.VMEM((2, 64 * ZW, 128), F32),
+            pltpu.VMEM((2, 64 * ZW, 128), F32),
             pltpu.VMEM((128, 4096), BF),
             pltpu.VMEM((4096, DM), BF),
-            pltpu.VMEM((DM, DM), BF),
-            pltpu.VMEM((DM, DM), BF),
-            pltpu.VMEM((DM, DM), BF),
-            pltpu.SemaphoreType.DMA((7,)),
+            pltpu.SemaphoreType.DMA((6,)),
         ],
-        compiler_params=pltpu.CompilerParams(vmem_limit_bytes=28 << 20),
+        compiler_params=pltpu.CompilerParams(vmem_limit_bytes=26 << 20),
         name="stem",
-    )(halo, conv_weight, cotangent, inside, patch_weight, query_weight, key_weight, value_weight)
+    )(halo, conv_weight, cotangent, features, patch_weight, query_weight, key_weight, value_weight)
 
 
 def local(
@@ -655,18 +609,16 @@
     tiles = faces[:, 64, :8].astype(jnp.int32)
     outer, goal = split_device(tiles >> 1)
     targets = jnp.where((tiles < 128) & (goal == inner), (outer & 7) * 2 + (tiles & 1), -1)
-    routed, taps = lax.optimization_barrier((route(targets, faces), conv_weight.reshape(9, 256, 256)))
-    halo = swap(routed, OUTER)
-    inside = conv_inside(features, taps)
+    halo = swap(route(targets, faces), OUTER)
     tokens, packed, rest = stem(
         halo,
-        taps,
+        conv_weight.reshape(9, 256, 256),
         cotangent,
-        inside,
+        features,
         in_hbm(patch_weight),
-        in_hbm(query_weight),
-        in_hbm(key_weight),
-        in_hbm(value_weight),
+        query_weight,
+        key_weight,
+        value_weight,
     )
     packed = swap(packed)
     packed, rest = lax.optimization_barrier((packed, rest))

time: 173 us -> 170 us (0.983)
  blocking collectives: 94.7 us -> 120 us
  waiting for transfers between devices: 24.8 us -> 9.47 us
  starting transfers between devices: 13 us -> 5 us
  Pallas kernels: 38.1 us -> 34.1 us
    all_to_all x5 -> x6, blocking collectives: 94.7 us -> 120 us  [swap(): lax.all_to_all(x, 'tile', split_axis=0, concat_axis=0, tiled=True, axis_i...]
    all_to_all x2 -> x1, waiting for transfers between devices: 24.8 us -> 9.47 us  [swap(): lax.all_to_all(x, 'tile', split_axis=0, concat_axis=0, tiled=True, axis_i...]
    all_to_all x2 -> x1, starting transfers between devices: 13 us -> 5 us  [swap(): lax.all_to_all(x, 'tile', split_axis=0, concat_axis=0, tiled=True, axis_i...]
    pallas_call x2 -> x1, Pallas kernels: 9.35 us -> 6.36 us  [stem(): pl.pallas_call(stem_kernel, in_specs=[vmem] * 3 + [hbm] * 2 + [vmem] * 3,...]
  transfers between devices with their start and end apart: 2 -> 1, of which waited for: 2 -> 1; matrix products, arithmetic and copies ran while one was open for 0% -> 0% of each run, Pallas kernels for 9% -> 7%
where the time goes in v10:
time: 170 us
  blocking collectives  120 us (71%)
  Pallas kernels  34.1 us (20%)
  waiting for transfers between devices  9.47 us (6%)
  starting transfers between devices  5 us (3%)
    all_to_all x6, blocking collectives, swap(): lax.all_to_all(x, 'tile', split_axis=0, concat_axis=0, tiled=True, axis_i...  120 us
    pallas_call x1, Pallas kernels, attend_pair(): pl.pallas_call(pair_kernel, grid=(64 // srcs,), in_specs=[pl.BlockSpec((s...  11.9 us
    all_to_all x1, waiting for transfers between devices, swap(): lax.all_to_all(x, 'tile', split_axis=0, concat_axis=0, tiled=True, axis_i...  9.47 us
    pallas_call x1, Pallas kernels, attend_single(): pl.pallas_call(single_kernel, in_specs=[vmem] * 3, out_specs=vmem, out_sh...  6.61 us
    pallas_call x1, Pallas kernels, stem(): pl.pallas_call(stem_kernel, in_specs=[vmem] * 3 + [hbm] * 2 + [vmem] * 3,...  6.36 us
    all_to_all x1, starting transfers between devices, swap(): lax.all_to_all(x, 'tile', split_axis=0, concat_axis=0, tiled=True, axis_i...  5 us
  transfers between devices with their start and end apart: 1, of which 1 were waited for; matrix products, arithmetic and copies ran while one was open for 0% of the time, Pallas kernels for 7%

profile of v10, /device:TPU:0, one launch (start us, length us, event | category | flops | bytes accessed | tf_op | source)
XLA Modules:
  0.0 169.6 jit_solution(11298491550550727749)
XLA Ops:
  0.6 2.1 %faces.1 = bf16[8,2,128,256]{3,2,1,0:T(8,128)(2,1)S(1)} custom-call(s32[2,8]{1,0:T(2,128)} %links_ref.1, bf16[2,32,32,256]{3,2,1,0:T(8,128)(2,1)} %features_hbm.3), custom_call_target="tpu_custom_call" | custom-call | tf_op jit(solution)/shard_map/faces/pallas_call | solution.py:104
  2.8 0.0 copy-start.4
  2.8 0.0 copy-start.5
  2.8 20.6 %all_to_all.35 = bf16[8,2,128,256]{3,2,1,0:T(8,128)(2,1)S(1)} all-to-all(bf16[8,2,128,256]{3,2,1,0:T(8,128)(2,1)S(1)} %faces.1), channel_id=1, replica_groups={{0,2,8,10,32,34,40,42},{6,4,14,12,38,36,46,44},{24,26,16,18,56,58,48,50..., dimensions={0} | all-to-all | bytes 2097152 | tf_op jit(solution)/shard_map/all_to_all | solution.py:67
  23.5 0.0 copy-start.2
  23.5 0.0 copy-start.3
  23.5 2.0 %route.1 = bf16[8,264,256]{2,1,0:T(8,128)(2,1)S(1)} custom-call(s32[16,8]{1,0:T(8,128)S(1)} %fusion.12.targets_ref, bf16[16,128,256]{2,1,0:T(8,128)(2,1)S(1)} %bitcast.14), custom_call_target="tpu_custom_call" | custom-call | tf_op jit(solution)/shard_map/route/pallas_call | solution.py:158
  25.5 0.0 copy-start
  25.5 0.0 copy-start.7
  25.6 25.8 %all_to_all.36.halo_ref = bf16[8,264,256]{2,1,0:T(8,128)(2,1)S(1)} all-to-all(bf16[8,264,256]{2,1,0:T(8,128)(2,1)S(1)} %route.1), channel_id=1, replica_groups={{0,6,24,30,96,102,120,126},{2,4,26,28,98,100,122,124},{8,14,16,22,104,1..., dimensions={0} | all-to-all | bytes 2162688 | tf_op jit(solution)/shard_map/all_to_all | solution.py:67
  51.4 0.0 copy-done.4
  51.4 0.0 copy-done.5
  51.4 0.0 copy-done.2
  51.4 0.0 copy-done.3
  51.4 0.0 copy-done
  51.4 0.0 copy-done.7
  51.4 6.4 %stem.1 = (bf16[128,768]{1,0:T(8,128)(2,1)S(1)}, bf16[64,96,128]{2,1,0:T(8,128)(2,1)S(1)}, bf16[64,96,128]{2,1,0:T(8,128)(2,1)S(1)}) custom-call(bf16[8,264,256]{2,1,0:T(8,128)(2,1)S(1)} %all_to_all.36.halo_ref, bf16[9,256,256]{2,1,0:T(8,128)(2,1)S(1)} %bitcast.15, bf16[128,768]{1,0:T(8,128)(2,1)S(1)} %copy-done.7, bf16[2,32,32,256]{3,2,1,0:T(8,128)(2,1)S(1)} %copy-done, ...), custom_call_target="tpu_custom_call" | custom-call | tf_op jit(solution)/shard_map/stem/pallas_call | solution.py:570
  57.8 0.0 copy-start.1
  57.8 26.0 %all_to_all.37.in_ref.all_ref = bf16[64,96,128]{2,1,0:T(8,128)(2,1)S(1)} all-to-all(bf16[64,96,128]{2,1,0:T(8,128)(2,1)S(1)} %get-tuple-element.15), channel_id=1, replica_groups=mesh['tile'=64,'slide'=2] {'tile'}, dimensions={0} | all-to-all | bytes 3145728 | tf_op jit(solution)/shard_map/all_to_all | solution.py:67
  83.8 0.0 copy-done.1
  83.8 5.0 %all-to-all-start.3 = ((bf16[64,96,128]{2,1,0:T(8,128)(2,1)}), bf16[64,96,128]{2,1,0:T(8,128)(2,1)S(1)}, u32[]{:S(2)}, u32[]{:S(2)}) async-start(bf16[64,96,128]{2,1,0:T(8,128)(2,1)} %copy-done.1), calls=%async_computation.3 | async-start | bytes 3145728 | tf_op jit(solution)/shard_map/all_to_all | solution.py:67
  88.9 11.9 %attend_pair.1 = (bf16[4,512,128]{2,1,0:T(8,128)(2,1)}, bf16[4,64,128]{2,1,0:T(8,128)(2,1)}) custom-call(bf16[64,96,128]{2,1,0:T(8,128)(2,1)S(1)} %all_to_all.37.in_ref.all_ref, bf16[64,96,128]{2,1,0:T(8,128)(2,1)S(1)} %all_to_all.37.in_ref.all_ref), custom_call_target="tpu_custom_call" | custom-call | tf_op jit(solution)/shard_map/attend_pair/pallas_call | solution.py:264
  100.7 9.5 %all-to-all-done.3.all_ref.rest_ref = bf16[64,96,128]{2,1,0:T(8,128)(2,1)S(1)} async-done(((bf16[64,96,128]{2,1,0:T(8,128)(2,1)}), bf16[64,96,128]{2,1,0:T(8,128)(2,1)S(1)}, u32[]{:S(2)}, u32[]{:S(2)}) %all-to-all-start.3) | async-done | bytes 1572896 | tf_op jit(solution)/shard_map/all_to_all | solution.py:67
  110.2 6.6 %attend_single.1 = bf16[4,832,128]{2,1,0:T(8,128)(2,1)S(1)} custom-call(bf16[64,96,128]{2,1,0:T(8,128)(2,1)S(1)} %all-to-all-done.3.all_ref.rest_ref, bf16[4,512,128]{2,1,0:T(8,128)(2,1)} %get-tuple-element.19.part_ref, bf16[4,64,128]{2,1,0:T(8,128)(2,1)} %get-tuple-element.20.lse_ref), custom_call_target="tpu_custom_call" | custom-call | tf_op jit(solution)/shard_map/attend_single/pallas_call | solution.py:289
  116.8 11.5 %all_to_all.38.parts_ref = bf16[4,832,128]{2,1,0:T(8,128)(2,1)S(1)} all-to-all(bf16[4,832,128]{2,1,0:T(8,128)(2,1)S(1)} %attend_single.1), channel_id=1, replica_groups={{0,8,32,40},{24,16,56,48},{96,104,64,72},{120,112,88,80},{2,10,34,42},{..., dimensions={0} | all-to-all | bytes 1703936 | tf_op jit(solution)/shard_map/all_to_all | solution.py:67
  128.3 2.4 %merge.1 = (bf16[64,16,128]{2,1,0:T(8,128)(2,1)S(1)}, bf16[6,192,128]{2,1,0:T(8,128)(2,1)S(1)}) custom-call(bf16[4,832,128]{2,1,0:T(8,128)(2,1)S(1)} %all_to_all.38.parts_ref, bf16[64,96,128]{2,1,0:T(8,128)(2,1)S(1)} %all-to-all-done.3.all_ref.rest_ref), custom_call_target="tpu_custom_call" | custom-call | tf_op jit(solution)/shard_map/merge/pallas_call | solution.py:343
  130.7 11.5 %all_to_all.39.terms_ref = bf16[16,72,128]{2,1,0:T(8,128)(2,1)S(1)} all-to-all(bf16[16,72,128]{2,1,0:T(8,128)(2,1)S(1)} %bitcast.16), channel_id=1, replica_groups={{0,8,32,40,24,16,56,48,96,104,64,72,120,112,88,80},{2,10,34,42,26,18,58..., dimensions={0} | all-to-all | bytes 589824 | tf_op jit(solution)/shard_map/all_to_all | solution.py:67
  142.2 0.3 share.1
  142.5 0.0 copy-start.6
  142.5 24.5 %all_to_all.40.all_ref = bf16[64,88,128]{2,1,0:T(8,128)(2,1)S(1)} all-to-all(bf16[64,88,128]{2,1,0:T(8,128)(2,1)S(1)} %share.1), channel_id=1, replica_groups=mesh['tile'=64,'slide'=2] {'tile'}, dimensions={0} | all-to-all | bytes 2883584 | tf_op jit(solution)/shard_map/all_to_all | solution.py:67
  167.0 0.0 copy-done.6
  167.0 2.4 %finish.1 = (bf16[128,768]{1,0:T(8,128)(2,1)}, f32[768,768]{1,0:T(8,128)}) custom-call(bf16[64,88,128]{2,1,0:T(8,128)(2,1)S(1)} %all_to_all.40.all_ref, bf16[128,768]{1,0:T(8,128)(2,1)S(1)} %get-tuple-element.23.tokens_ref, bf16[768,768]{1,0:T(8,128)(2,1)S(1)} %copy-done.6), custom_call_target="tpu_custom_call" | custom-call | tf_op jit(solution)/shard_map/finish/pallas_call | solution.py:424
  (3 shorter events, 0.1 us)
Async XLA Ops:
  2.8 48.6 %copy-start.4 = (bf16[768,768]{1,0:T(8,128)(2,1)S(1)}, bf16[768,768]{1,0:T(8,128)(2,1)}, u32[]{:S(2)}) copy-start(bf16[768,768]{1,0:T(8,128)(2,1)} %wk_ref.1) | copy-start | bytes 3538948
  2.8 48.6 %copy-start.5 = (bf16[768,768]{1,0:T(8,128)(2,1)S(1)}, bf16[768,768]{1,0:T(8,128)(2,1)}, u32[]{:S(2)}) copy-start(bf16[768,768]{1,0:T(8,128)(2,1)} %wv_ref.1) | copy-start | bytes 3538948
  23.5 27.9 %copy-start.2 = (bf16[3,3,256,256]{3,2,1,0:T(8,128)(2,1)S(1)}, bf16[3,3,256,256]{3,2,1,0:T(8,128)(2,1)}, u32[]{:S(2)}) copy-start(bf16[3,3,256,256]{3,2,1,0:T(8,128)(2,1)} %param.11) | copy-start | bytes 3538948
  23.5 27.9 %copy-start.3 = (bf16[768,768]{1,0:T(8,128)(2,1)S(1)}, bf16[768,768]{1,0:T(8,128)(2,1)}, u32[]{:S(2)}) copy-start(bf16[768,768]{1,0:T(8,128)(2,1)} %wq_ref.1) | copy-start | bytes 3538948
  25.5 25.9 %copy-start = (bf16[2,32,32,256]{3,2,1,0:T(8,128)(2,1)S(1)}, bf16[2,32,32,256]{3,2,1,0:T(8,128)(2,1)}, u32[]{:S(2)}) copy-start(bf16[2,32,32,256]{3,2,1,0:T(8,128)(2,1)} %features_hbm.3) | copy-start | bytes 3145732
  25.5 25.9 %copy-start.7 = (bf16[128,768]{1,0:T(8,128)(2,1)S(1)}, bf16[128,768]{1,0:T(8,128)(2,1)}, u32[]{:S(2)}) copy-start(bf16[128,768]{1,0:T(8,128)(2,1)} %cot_ref.1) | copy-start | bytes 589828
  57.8 26.1 %copy-start.1 = (bf16[64,96,128]{2,1,0:T(8,128)(2,1)}, bf16[64,96,128]{2,1,0:T(8,128)(2,1)S(1)}, u32[]{:S(2)}) copy-start(bf16[64,96,128]{2,1,0:T(8,128)(2,1)S(1)} %get-tuple-element.17) | copy-start | bytes 4718596
  83.8 26.4 %all-to-all-start.3 = ((bf16[64,96,128]{2,1,0:T(8,128)(2,1)}), bf16[64,96,128]{2,1,0:T(8,128)(2,1)S(1)}, u32[]{:S(2)}, u32[]{:S(2)}) async-start(bf16[64,96,128]{2,1,0:T(8,128)(2,1)} %copy-done.1), calls=%async_computation.3 | async-start | bytes 3145728 | tf_op jit(solution)/shard_map/all_to_all | solution.py:67
  142.5 24.5 %copy-start.6 = (bf16[768,768]{1,0:T(8,128)(2,1)S(1)}, bf16[768,768]{1,0:T(8,128)(2,1)}, u32[]{:S(2)}) copy-start(bf16[768,768]{1,0:T(8,128)(2,1)} %weight_ref.1) | copy-start | bytes 3538948

commit v11 on v10

--- a/solution.py
+++ b/solution.py
@@ -86,7 +86,7 @@
     for t in range(2):
         for n, x in enumerate((0, 7)):
             for lt in range(2):
-                cols_ref[...] = sides_ref[t, n, :, :, lt * 128 : lt * 128 + 128].astype(F32).reshape(256, 128)
+                cols_ref[:256] = sides_ref[t, n, :, :, lt * 128 : lt * 128 + 128].astype(F32).reshape(256, 128)
                 faces_ref[t, 64 + n * 32 : 96 + n * 32, lt * 128 : lt * 128 + 128] = cols_ref[
                     pl.ds(x, 32, stride=8), :
                 ].astype(BF)
@@ -108,7 +108,7 @@
         out_shape=jax.ShapeDtypeStruct((8, 2, FACES, 256), BF),
         scratch_shapes=[
             pltpu.VMEM((2, 2, 32, 8, 256), BF),
-            pltpu.VMEM((256, 128), F32),
+            pltpu.VMEM((264, 128), F32),
             pltpu.VMEM((2, FACES, 256), BF),
             pltpu.SemaphoreType.DMA((8,)),
         ],
@@ -226,7 +226,12 @@
     put_rows(tail_ref, lse_ref, 0)
 
 
-def single_kernel(all_ref, part_ref, lse_ref, out_ref, key_ref, val_ref, row_ref, tail_ref):
+def single_kernel(all_ref, part_hbm, lse_ref, out_ref, key_ref, val_ref, row_ref, tail_ref, sems):
+    copies = [
+        pltpu.make_async_copy(part_hbm.at[b], out_ref.at[b, :512], sems.at[b]) for b in range(SPLIT)
+    ]
+    for copy in copies:
+        copy.start()
     ones = jnp.where(lax.broadcasted_iota(jnp.int32, (2048, HD), 1) == 0, 1.0, 0.0).astype(BF)
     val_ref[:, HD:] = ones
     for g in range(2):
@@ -249,14 +254,14 @@
         for i, part in enumerate(parts):
             tail = jnp.where(lanes == 16 * n + 6 + i, part, tail)
     tail_ref[...] = tail
-    for b in range(SPLIT):
-        out_ref[b, :512, :] = part_ref[b]
     put_rows(row_ref, out_ref, 512)
     for n in range(UNIT):
         for b in range(SPLIT):
             row = n * BLK + b * 8
             new = lse_ref[b, n * 8 : n * 8 + 8, :].astype(F32) + tail_ref[row : row + 8, :]
             out_ref[b, 768 + n * 8 : 776 + n * 8, :] = new.astype(BF)
+    for copy in copies:
+        copy.wait()
 
 
 def attend_pair(packed):
@@ -288,7 +293,7 @@
     vmem = pl.BlockSpec(memory_space=pltpu.VMEM)
     return pl.pallas_call(
         single_kernel,
-        in_specs=[vmem] * 3,
+        in_specs=[vmem, pl.BlockSpec(memory_space=pltpu.HBM), vmem],
         out_specs=vmem,
         out_shape=jax.ShapeDtypeStruct((SPLIT, PARTS, 128), BF),
         scratch_shapes=[
@@ -296,6 +301,7 @@
             pltpu.VMEM((2048, 2 * HD), BF),
             pltpu.VMEM((1024, 128), F32),
             pltpu.VMEM((UNIT * BLK, 128), F32),
+            pltpu.SemaphoreType.DMA((SPLIT,)),
         ],
         compiler_params=pltpu.CompilerParams(vmem_limit_bytes=38 << 20),
         name="attend_single",
@@ -579,9 +585,9 @@
         scratch_shapes=[
             pltpu.VMEM((2, 34, 32, 256), BF),
             pltpu.VMEM((2, 2, ZW, 256), F32),
-            pltpu.VMEM((2, 64 * ZW, 128), F32),
-            pltpu.VMEM((2, 64 * ZW, 128), F32),
-            pltpu.VMEM((2, 64 * ZW, 128), F32),
+            pltpu.VMEM((2, 65 * ZW, 128), F32),
+            pltpu.VMEM((2, 65 * ZW, 128), F32),
+            pltpu.VMEM((2, 65 * ZW, 128), F32),
             pltpu.VMEM((128, 4096), BF),
             pltpu.VMEM((4096, DM), BF),
             pltpu.SemaphoreType.DMA((6,)),

time: 170 us -> 170 us (level)
  no operation moved by 1% of the time
where the time goes in v11:
time: 170 us; the launch traced here: 169 us
  blocking collectives  120 us (71%)
  Pallas kernels  33.9 us (20%)
  waiting for transfers between devices  9.47 us (6%)
  starting transfers between devices  5.01 us (3%)
    all_to_all x6, blocking collectives, swap(): lax.all_to_all(x, 'tile', split_axis=0, concat_axis=0, tiled=True, axis_i...  120 us
    pallas_call x1, Pallas kernels, attend_pair(): pl.pallas_call(pair_kernel, grid=(64 // srcs,), in_specs=[pl.BlockSpec((s...  11.9 us
    all_to_all x1, waiting for transfers between devices, swap(): lax.all_to_all(x, 'tile', split_axis=0, concat_axis=0, tiled=True, axis_i...  9.47 us
    pallas_call x1, Pallas kernels, attend_single(): pl.pallas_call(single_kernel, in_specs=[vmem, pl.BlockSpec(memory_space=p...  6.44 us
    pallas_call x1, Pallas kernels, stem(): pl.pallas_call(stem_kernel, in_specs=[vmem] * 3 + [hbm] * 2 + [vmem] * 3,...  6.35 us
    all_to_all x1, starting transfers between devices, swap(): lax.all_to_all(x, 'tile', split_axis=0, concat_axis=0, tiled=True, axis_i...  5.01 us
  transfers between devices with their start and end apart: 1, of which 1 were waited for; matrix products, arithmetic and copies ran while one was open for 0% of the time, Pallas kernels for 7%

profile of v11, /device:TPU:0, one launch (start us, length us, event | category | flops | bytes accessed | tf_op | source)
XLA Modules:
  0.0 169.4 jit_solution(16070720662127036822)
XLA Ops:
  0.6 2.1 %faces.1 = bf16[8,2,128,256]{3,2,1,0:T(8,128)(2,1)S(1)} custom-call(s32[2,8]{1,0:T(2,128)} %links_ref.1, bf16[2,32,32,256]{3,2,1,0:T(8,128)(2,1)} %features_hbm.3), custom_call_target="tpu_custom_call" | custom-call | tf_op jit(solution)/shard_map/faces/pallas_call | solution.py:104
  2.8 0.0 copy-start.4
  2.8 0.0 copy-start.5
  2.8 20.6 %all_to_all.35 = bf16[8,2,128,256]{3,2,1,0:T(8,128)(2,1)S(1)} all-to-all(bf16[8,2,128,256]{3,2,1,0:T(8,128)(2,1)S(1)} %faces.1), channel_id=1, replica_groups={{0,2,8,10,32,34,40,42},{6,4,14,12,38,36,46,44},{24,26,16,18,56,58,48,50..., dimensions={0} | all-to-all | bytes 2097152 | tf_op jit(solution)/shard_map/all_to_all | solution.py:67
  23.5 0.0 copy-start.2
  23.5 0.0 copy-start.3
  23.5 2.0 %route.1 = bf16[8,264,256]{2,1,0:T(8,128)(2,1)S(1)} custom-call(s32[16,8]{1,0:T(8,128)S(1)} %fusion.12.targets_ref, bf16[16,128,256]{2,1,0:T(8,128)(2,1)S(1)} %bitcast.14), custom_call_target="tpu_custom_call" | custom-call | tf_op jit(solution)/shard_map/route/pallas_call | solution.py:158
  25.5 0.0 copy-start
  25.5 0.0 copy-start.7
  25.5 25.8 %all_to_all.36.halo_ref = bf16[8,264,256]{2,1,0:T(8,128)(2,1)S(1)} all-to-all(bf16[8,264,256]{2,1,0:T(8,128)(2,1)S(1)} %route.1), channel_id=1, replica_groups={{0,6,24,30,96,102,120,126},{2,4,26,28,98,100,122,124},{8,14,16,22,104,1..., dimensions={0} | all-to-all | bytes 2162688 | tf_op jit(solution)/shard_map/all_to_all | solution.py:67
  51.4 0.0 copy-done.4
  51.4 0.0 copy-done.5
  51.4 0.0 copy-done.2
  51.4 0.0 copy-done.3
  51.4 0.0 copy-done
  51.4 0.0 copy-done.7
  51.4 6.3 %stem.1 = (bf16[128,768]{1,0:T(8,128)(2,1)S(1)}, bf16[64,96,128]{2,1,0:T(8,128)(2,1)S(1)}, bf16[64,96,128]{2,1,0:T(8,128)(2,1)S(1)}) custom-call(bf16[8,264,256]{2,1,0:T(8,128)(2,1)S(1)} %all_to_all.36.halo_ref, bf16[9,256,256]{2,1,0:T(8,128)(2,1)S(1)} %bitcast.15, bf16[128,768]{1,0:T(8,128)(2,1)S(1)} %copy-done.7, bf16[2,32,32,256]{3,2,1,0:T(8,128)(2,1)S(1)} %copy-done, ...), custom_call_target="tpu_custom_call" | custom-call | tf_op jit(solution)/shard_map/stem/pallas_call | solution.py:576
  57.8 0.0 copy-start.1
  57.8 26.1 %all_to_all.37.in_ref.all_ref = bf16[64,96,128]{2,1,0:T(8,128)(2,1)S(1)} all-to-all(bf16[64,96,128]{2,1,0:T(8,128)(2,1)S(1)} %get-tuple-element.15), channel_id=1, replica_groups=mesh['tile'=64,'slide'=2] {'tile'}, dimensions={0} | all-to-all | bytes 3145728 | tf_op jit(solution)/shard_map/all_to_all | solution.py:67
  83.8 0.0 copy-done.1
  83.8 5.0 %all-to-all-start.3 = ((bf16[64,96,128]{2,1,0:T(8,128)(2,1)}), bf16[64,96,128]{2,1,0:T(8,128)(2,1)S(1)}, u32[]{:S(2)}, u32[]{:S(2)}) async-start(bf16[64,96,128]{2,1,0:T(8,128)(2,1)} %copy-done.1), calls=%async_computation.3 | async-start | bytes 3145728 | tf_op jit(solution)/shard_map/all_to_all | solution.py:67
  88.8 11.9 %attend_pair.1 = (bf16[4,512,128]{2,1,0:T(8,128)(2,1)}, bf16[4,64,128]{2,1,0:T(8,128)(2,1)}) custom-call(bf16[64,96,128]{2,1,0:T(8,128)(2,1)S(1)} %all_to_all.37.in_ref.all_ref, bf16[64,96,128]{2,1,0:T(8,128)(2,1)S(1)} %all_to_all.37.in_ref.all_ref), custom_call_target="tpu_custom_call" | custom-call | tf_op jit(solution)/shard_map/attend_pair/pallas_call | solution.py:269
  100.7 9.5 %all-to-all-done.3.all_ref.rest_ref = bf16[64,96,128]{2,1,0:T(8,128)(2,1)S(1)} async-done(((bf16[64,96,128]{2,1,0:T(8,128)(2,1)}), bf16[64,96,128]{2,1,0:T(8,128)(2,1)S(1)}, u32[]{:S(2)}, u32[]{:S(2)}) %all-to-all-start.3) | async-done | bytes 1572896 | tf_op jit(solution)/shard_map/all_to_all | solution.py:67
  110.2 6.4 %attend_single.1 = bf16[4,832,128]{2,1,0:T(8,128)(2,1)S(1)} custom-call(bf16[64,96,128]{2,1,0:T(8,128)(2,1)S(1)} %all-to-all-done.3.all_ref.rest_ref, bf16[4,512,128]{2,1,0:T(8,128)(2,1)} %get-tuple-element.19.part_hbm, bf16[4,64,128]{2,1,0:T(8,128)(2,1)} %get-tuple-element.20.lse_ref), custom_call_target="tpu_custom_call" | custom-call | tf_op jit(solution)/shard_map/attend_single/pallas_call | solution.py:294
  116.6 11.5 %all_to_all.38.parts_ref = bf16[4,832,128]{2,1,0:T(8,128)(2,1)S(1)} all-to-all(bf16[4,832,128]{2,1,0:T(8,128)(2,1)S(1)} %attend_single.1), channel_id=1, replica_groups={{0,8,32,40},{24,16,56,48},{96,104,64,72},{120,112,88,80},{2,10,34,42},{..., dimensions={0} | all-to-all | bytes 1703936 | tf_op jit(solution)/shard_map/all_to_all | solution.py:67
  128.1 2.4 %merge.1 = (bf16[64,16,128]{2,1,0:T(8,128)(2,1)S(1)}, bf16[6,192,128]{2,1,0:T(8,128)(2,1)S(1)}) custom-call(bf16[4,832,128]{2,1,0:T(8,128)(2,1)S(1)} %all_to_all.38.parts_ref, bf16[64,96,128]{2,1,0:T(8,128)(2,1)S(1)} %all-to-all-done.3.all_ref.rest_ref), custom_call_target="tpu_custom_call" | custom-call | tf_op jit(solution)/shard_map/merge/pallas_call | solution.py:349
  130.5 11.5 %all_to_all.39.terms_ref = bf16[16,72,128]{2,1,0:T(8,128)(2,1)S(1)} all-to-all(bf16[16,72,128]{2,1,0:T(8,128)(2,1)S(1)} %bitcast.16), channel_id=1, replica_groups={{0,8,32,40,24,16,56,48,96,104,64,72,120,112,88,80},{2,10,34,42,26,18,58..., dimensions={0} | all-to-all | bytes 589824 | tf_op jit(solution)/shard_map/all_to_all | solution.py:67
  142.0 0.3 share.1
  142.3 0.0 copy-start.6
  142.3 24.5 %all_to_all.40.all_ref = bf16[64,88,128]{2,1,0:T(8,128)(2,1)S(1)} all-to-all(bf16[64,88,128]{2,1,0:T(8,128)(2,1)S(1)} %share.1), channel_id=1, replica_groups=mesh['tile'=64,'slide'=2] {'tile'}, dimensions={0} | all-to-all | bytes 2883584 | tf_op jit(solution)/shard_map/all_to_all | solution.py:67
  166.8 0.0 copy-done.6
  166.8 2.4 %finish.1 = (bf16[128,768]{1,0:T(8,128)(2,1)}, f32[768,768]{1,0:T(8,128)}) custom-call(bf16[64,88,128]{2,1,0:T(8,128)(2,1)S(1)} %all_to_all.40.all_ref, bf16[128,768]{1,0:T(8,128)(2,1)S(1)} %get-tuple-element.23.tokens_ref, bf16[768,768]{1,0:T(8,128)(2,1)S(1)} %copy-done.6), custom_call_target="tpu_custom_call" | custom-call | tf_op jit(solution)/shard_map/finish/pallas_call | solution.py:430
  (3 shorter events, 0.1 us)
Async XLA Ops:
  2.8 48.6 %copy-start.4 = (bf16[768,768]{1,0:T(8,128)(2,1)S(1)}, bf16[768,768]{1,0:T(8,128)(2,1)}, u32[]{:S(2)}) copy-start(bf16[768,768]{1,0:T(8,128)(2,1)} %wk_ref.1) | copy-start | bytes 3538948
  2.8 48.6 %copy-start.5 = (bf16[768,768]{1,0:T(8,128)(2,1)S(1)}, bf16[768,768]{1,0:T(8,128)(2,1)}, u32[]{:S(2)}) copy-start(bf16[768,768]{1,0:T(8,128)(2,1)} %wv_ref.1) | copy-start | bytes 3538948
  23.5 27.9 %copy-start.2 = (bf16[3,3,256,256]{3,2,1,0:T(8,128)(2,1)S(1)}, bf16[3,3,256,256]{3,2,1,0:T(8,128)(2,1)}, u32[]{:S(2)}) copy-start(bf16[3,3,256,256]{3,2,1,0:T(8,128)(2,1)} %param.11) | copy-start | bytes 3538948
  23.5 27.8 %copy-start.3 = (bf16[768,768]{1,0:T(8,128)(2,1)S(1)}, bf16[768,768]{1,0:T(8,128)(2,1)}, u32[]{:S(2)}) copy-start(bf16[768,768]{1,0:T(8,128)(2,1)} %wq_ref.1) | copy-start | bytes 3538948
  25.5 25.9 %copy-start = (bf16[2,32,32,256]{3,2,1,0:T(8,128)(2,1)S(1)}, bf16[2,32,32,256]{3,2,1,0:T(8,128)(2,1)}, u32[]{:S(2)}) copy-start(bf16[2,32,32,256]{3,2,1,0:T(8,128)(2,1)} %features_hbm.3) | copy-start | bytes 3145732
  25.5 25.9 %copy-start.7 = (bf16[128,768]{1,0:T(8,128)(2,1)S(1)}, bf16[128,768]{1,0:T(8,128)(2,1)}, u32[]{:S(2)}) copy-start(bf16[128,768]{1,0:T(8,128)(2,1)} %cot_ref.1) | copy-start | bytes 589828
  57.8 26.1 %copy-start.1 = (bf16[64,96,128]{2,1,0:T(8,128)(2,1)}, bf16[64,96,128]{2,1,0:T(8,128)(2,1)S(1)}, u32[]{:S(2)}) copy-start(bf16[64,96,128]{2,1,0:T(8,128)(2,1)S(1)} %get-tuple-element.17) | copy-start | bytes 4718596
  83.8 26.4 %all-to-all-start.3 = ((bf16[64,96,128]{2,1,0:T(8,128)(2,1)}), bf16[64,96,128]{2,1,0:T(8,128)(2,1)S(1)}, u32[]{:S(2)}, u32[]{:S(2)}) async-start(bf16[64,96,128]{2,1,0:T(8,128)(2,1)} %copy-done.1), calls=%async_computation.3 | async-start | bytes 3145728 | tf_op jit(solution)/shard_map/all_to_all | solution.py:67
  142.3 24.5 %copy-start.6 = (bf16[768,768]{1,0:T(8,128)(2,1)S(1)}, bf16[768,768]{1,0:T(8,128)(2,1)}, u32[]{:S(2)}) copy-start(bf16[768,768]{1,0:T(8,128)(2,1)} %weight_ref.1) | copy-start | bytes 3538948
